TPU v7x, 32 devices: a whole 2x2x4 slice. The times are simulated.
32 devices in a mesh: fsdp: 4 (over y, core), ctx: 2 (over x), tp: 4 (over z).
Axes of the slice: x: 2, y: 2, z: 4, core: 2. Of those that a mesh axis runs over, the one named last changes fastest.
Arguments:
- tokens: bfloat16 [8, 1024, 768], P('fsdp', 'ctx'), may hold values from -6 to 6
- lengths: int32 [8], P('fsdp'), may hold values from 256 to 1024, as said below
- cotangent: bfloat16 [8, 1024, 768], P('fsdp', 'ctx'), may hold values from -6 to 6
- w_query: bfloat16 [768, 768], P('fsdp', 'tp'), may hold values from -0.3125 to 0.3125
- w_key: bfloat16 [768, 768], P('fsdp', 'tp'), may hold values from -0.3125 to 0.3125
- w_value: bfloat16 [768, 768], P('fsdp', 'tp'), may hold values from -0.21875 to 0.21875
- b_query: bfloat16 [768], P('tp'), may hold values from -3 to 3
- b_value: bfloat16 [768], P('tp'), may hold values from -3 to 3
- w_out: bfloat16 [768, 768], P('tp', 'fsdp'), may hold values from -1.5 to 1.5
- b_out: bfloat16 [768], P('fsdp'), may hold values from -3 to 3
- ln1_gain: bfloat16 [768], P('fsdp'), may hold values from 0.5 to 1.5
- ln1_shift: bfloat16 [768], P('fsdp'), may hold values from -3 to 3
- w_up: bfloat16 [768, 3072], P('fsdp', 'tp'), may hold values from -0.21875 to 0.21875
- b_up: bfloat16 [3072], P('tp'), may hold values from -3 to 3
- w_down: bfloat16 [3072, 768], P('tp', 'fsdp'), may hold values from -0.109375 to 0.109375
- b_down: bfloat16 [768], P('fsdp'), may hold values from -3 to 3
- ln2_gain: bfloat16 [768], P('fsdp'), may hold values from 0.5 to 1.5
- ln2_shift: bfloat16 [768], P('fsdp'), may hold values from -3 to 3
Outputs:
- output: bfloat16 [8, 1024, 768], P('fsdp', 'ctx')
- grad_tokens: float32 [8, 1024, 768], P('fsdp', 'ctx')
- grad_w_query: float32 [768, 768], P('fsdp', 'tp')
- grad_w_key: float32 [768, 768], P('fsdp', 'tp')
- grad_w_value: float32 [768, 768], P('fsdp', 'tp')
- grad_b_query: float32 [768], P('tp')
- grad_b_value: float32 [768], P('tp')
- grad_w_out: float32 [768, 768], P('tp', 'fsdp')
- grad_b_out: float32 [768], P('fsdp')
- grad_ln1_gain: float32 [768], P('fsdp')
- grad_ln1_shift: float32 [768], P('fsdp')
- grad_w_up: float32 [768, 3072], P('fsdp', 'tp')
- grad_b_up: float32 [3072], P('tp')
- grad_w_down: float32 [3072, 768], P('tp', 'fsdp')
- grad_b_down: float32 [768], P('fsdp')
- grad_ln2_gain: float32 [768], P('fsdp')
- grad_ln2_shift: float32 [768], P('fsdp')
Inputs may be any that keep to these rules, and one draw needn't show every extreme that they name: `lengths`: each sequence's count of real positions; positions from that count on are padding. In every draw some sequence has exactly 1024.
All inputs are finite; a program needn't handle non-finite values.
Results may differ from a plain program's by a relative error of at most 0.023.
Values may be sent and summed in bfloat16 or wider, within the bound.
No kernel may reach another device: no remote copies, remote signals or barrier semaphores. Data moves between devices by JAX's collectives and lax.ppermute only.
A program may use at most 128 MiB of HBM per device.

v0:
```python
import math

import jax
import jax.numpy as jnp
from jax import lax
from jax.sharding import PartitionSpec as P

HEAD_DIM = 64


epsilon = 1e-12
masked_score = -1e30


def passed_along(value, axis, steps):
    count = lax.axis_size(axis)
    pairs = [(source, (source + steps) % count) for source in range(count)]
    return lax.ppermute(value, axis, pairs)


def layer_norm(inputs, gain_vector, shift_vector):
    center = jnp.mean(inputs, axis=-1, keepdims=True)
    centered = inputs - center
    spread = jnp.mean(centered * centered, axis=-1, keepdims=True)
    return centered * lax.rsqrt(spread + epsilon) * gain_vector + shift_vector


def gelu_exact(inputs):
    return jax.nn.gelu(inputs, approximate=False)


def live_keys(lengths, first_key, key_count):
    places = first_key + lax.iota(jnp.int32, key_count)
    return (places[None, :] < lengths[:, None])[:, None, None, :]


def absorb(carried, queries, key_block, value_block, usable, score_scale):
    row_peak, row_total, summed = carried
    scores = (
        jnp.einsum("sqhe,skhe->shqk", queries, key_block, preferred_element_type=jnp.float32)
        * score_scale
    )
    masked = jnp.where(usable, scores, masked_score)
    new_peak = jnp.maximum(row_peak, jnp.max(masked, axis=-1))
    factor = jnp.exp(row_peak - new_peak)
    weights = jnp.where(usable, jnp.exp(masked - new_peak[..., None]), 0.0)
    row_total = row_total * factor + jnp.sum(weights, axis=-1)
    summed = summed * factor[..., None] + jnp.einsum(
        "shqk,skhe->shqe",
        weights.astype(jnp.bfloat16),
        value_block,
        preferred_element_type=jnp.float32,
    )
    return (new_peak, row_total, summed)


def block_grads(
    queries, grad_att, log_total, row_delta, key_block, value_block, usable, score_scale
):
    scores = (
        jnp.einsum("sqhe,skhe->shqk", queries, key_block, preferred_element_type=jnp.float32)
        * score_scale
    )
    masked = jnp.where(usable, scores, masked_score)
    weights = jnp.where(usable, jnp.exp(masked - log_total[..., None]), 0.0)
    grad_value = jnp.einsum(
        "shqk,sqhe->skhe",
        weights.astype(jnp.bfloat16),
        grad_att,
        preferred_element_type=jnp.float32,
    )
    grad_weights = jnp.einsum(
        "sqhe,skhe->shqk", grad_att, value_block, preferred_element_type=jnp.float32
    )
    grad_scores = (weights * (grad_weights - row_delta[..., None])).astype(jnp.bfloat16)
    grad_query = (
        jnp.einsum("shqk,skhe->sqhe", grad_scores, key_block, preferred_element_type=jnp.float32)
        * score_scale
    )
    grad_key = (
        jnp.einsum("shqk,sqhe->skhe", grad_scores, queries, preferred_element_type=jnp.float32)
        * score_scale
    )
    return (grad_query, grad_key, grad_value)


def per_device(
    tokens,
    lengths,
    cotangent,
    w_query,
    w_key,
    w_value,
    b_query,
    b_value,
    w_out,
    b_out,
    ln1_gain,
    ln1_shift,
    w_up,
    b_up,
    w_down,
    b_down,
    ln2_gain,
    ln2_shift,
):
    sequences, local_rows, model_width = tokens.shape
    token_count = sequences * local_rows
    ctx_count = lax.axis_size("ctx")
    ctx_index = lax.axis_index("ctx")
    (
        query_full,
        key_full,
        value_full,
        out_full,
        up_full,
        down_full,
        bias_out,
        gain_one,
        shift_one,
        bias_down,
        gain_two,
        shift_two,
    ) = (
        lax.all_gather(w_query, "fsdp", axis=0, tiled=True),
        lax.all_gather(w_key, "fsdp", axis=0, tiled=True),
        lax.all_gather(w_value, "fsdp", axis=0, tiled=True),
        lax.all_gather(w_out, "fsdp", axis=1, tiled=True),
        lax.all_gather(w_up, "fsdp", axis=0, tiled=True),
        lax.all_gather(w_down, "fsdp", axis=1, tiled=True),
        lax.all_gather(b_out, "fsdp", axis=0, tiled=True),
        lax.all_gather(ln1_gain, "fsdp", axis=0, tiled=True),
        lax.all_gather(ln1_shift, "fsdp", axis=0, tiled=True),
        lax.all_gather(b_down, "fsdp", axis=0, tiled=True),
        lax.all_gather(ln2_gain, "fsdp", axis=0, tiled=True),
        lax.all_gather(ln2_shift, "fsdp", axis=0, tiled=True),
    )
    flat_tokens = tokens.reshape(token_count, model_width)
    local_width = query_full.shape[1]
    head_count = local_width // HEAD_DIM
    score_scale = HEAD_DIM ** (-0.5)
    query_low = (
        jnp.dot(flat_tokens, query_full, preferred_element_type=jnp.float32)
        + b_query.astype(jnp.float32)
    ).astype(jnp.bfloat16)
    key_low = jnp.dot(flat_tokens, key_full, preferred_element_type=jnp.float32).astype(
        jnp.bfloat16
    )
    value_low = (
        jnp.dot(flat_tokens, value_full, preferred_element_type=jnp.float32)
        + b_value.astype(jnp.float32)
    ).astype(jnp.bfloat16)
    query_heads = query_low.reshape(sequences, local_rows, head_count, HEAD_DIM)
    key_local = key_low.reshape(sequences, local_rows, local_width)
    value_local = value_low.reshape(sequences, local_rows, local_width)
    query_first = ctx_index * local_rows
    start_state = (
        jnp.full((sequences, head_count, local_rows), masked_score, jnp.float32),
        jnp.zeros((sequences, head_count, local_rows), jnp.float32),
        jnp.zeros((sequences, head_count, local_rows, HEAD_DIM), jnp.float32),
    )
    key_part = lax.all_gather(key_local, "ctx", axis=1, tiled=True)
    value_part = lax.all_gather(value_local, "ctx", axis=1, tiled=True)
    key_count = key_part.shape[1]
    block_size = math.gcd(key_count, 512)

    def one_block(position, state_in):
        offset = position * block_size
        key_block = lax.dynamic_slice_in_dim(key_part, offset, block_size, 1).reshape(
            sequences, block_size, head_count, HEAD_DIM
        )
        value_block = lax.dynamic_slice_in_dim(value_part, offset, block_size, 1).reshape(
            sequences, block_size, head_count, HEAD_DIM
        )
        usable = live_keys(lengths, offset, block_size)
        return absorb(state_in, query_heads, key_block, value_block, usable, score_scale)

    row_peak, row_total, summed = lax.fori_loop(0, key_count // block_size, one_block, start_state)
    attended = (summed / row_total[..., None]).transpose(0, 2, 1, 3)
    log_total = row_peak + jnp.log(row_total)
    attended_low = attended.reshape(token_count, local_width).astype(jnp.bfloat16)
    branch = lax.psum(
        jnp.dot(attended_low, out_full, preferred_element_type=jnp.float32).astype(jnp.bfloat16),
        "tp",
    ).astype(jnp.float32) + bias_out.astype(jnp.float32)
    normed_one, norm_one_back = jax.vjp(
        layer_norm,
        flat_tokens.astype(jnp.float32) + branch,
        gain_one.astype(jnp.float32),
        shift_one.astype(jnp.float32),
    )
    normed_low = normed_one.astype(jnp.bfloat16)
    hidden_in = jnp.dot(normed_low, up_full, preferred_element_type=jnp.float32) + b_up.astype(
        jnp.float32
    )
    active, gelu_back = jax.vjp(gelu_exact, hidden_in)
    active_low = active.astype(jnp.bfloat16)
    second = lax.psum(
        jnp.dot(active_low, down_full, preferred_element_type=jnp.float32).astype(jnp.bfloat16),
        "tp",
    ).astype(jnp.float32) + bias_down.astype(jnp.float32)
    output, norm_two_back = jax.vjp(
        layer_norm, normed_one + second, gain_two.astype(jnp.float32), shift_two.astype(jnp.float32)
    )
    positions = query_first + lax.iota(jnp.int32, local_rows)
    row_valid = (positions[None, :] < lengths[:, None]).astype(jnp.float32).reshape(token_count, 1)
    grad_output = cotangent.reshape(token_count, model_width).astype(jnp.float32) * row_valid
    grad_resid_two, grad_gain_two, grad_shift_two = norm_two_back(grad_output)
    grad_second = grad_resid_two.astype(jnp.bfloat16)
    grad_w_down = jnp.einsum(
        "nf,nd->fd", active_low, grad_second, preferred_element_type=jnp.float32
    )
    grad_b_down = jnp.sum(grad_second.astype(jnp.float32), axis=0)
    (grad_hidden,) = gelu_back(
        jnp.einsum("nd,fd->nf", grad_second, down_full, preferred_element_type=jnp.float32)
    )
    grad_hidden_low = grad_hidden.astype(jnp.bfloat16)
    grad_w_up = jnp.einsum(
        "nd,nf->df", normed_low, grad_hidden_low, preferred_element_type=jnp.float32
    )
    grad_b_up = jnp.sum(grad_hidden_low.astype(jnp.float32), axis=0)
    grad_normed = grad_resid_two + lax.psum(
        jnp.einsum(
            "nf,df->nd", grad_hidden_low, up_full, preferred_element_type=jnp.float32
        ).astype(jnp.bfloat16),
        "tp",
    ).astype(jnp.float32)
    grad_resid_one, grad_gain_one, grad_shift_one = norm_one_back(grad_normed)
    grad_branch = grad_resid_one.astype(jnp.bfloat16)
    grad_w_out = jnp.einsum(
        "nc,nd->cd", attended_low, grad_branch, preferred_element_type=jnp.float32
    )
    grad_b_out = jnp.sum(grad_branch.astype(jnp.float32), axis=0)
    grad_att = jnp.einsum(
        "nd,cd->nc", grad_branch, out_full, preferred_element_type=jnp.float32
    ).astype(jnp.bfloat16)
    grad_att_heads = grad_att.reshape(sequences, local_rows, head_count, HEAD_DIM)
    row_delta = jnp.sum(grad_att_heads.astype(jnp.float32) * attended, axis=-1).transpose(0, 2, 1)
    zero_block = jnp.zeros((sequences, local_rows, head_count, HEAD_DIM), jnp.float32)

    def turn_grads(first_key, key_block, value_block):
        usable = live_keys(lengths, first_key, local_rows)
        key_heads = key_block.reshape(sequences, local_rows, head_count, HEAD_DIM)
        value_heads = value_block.reshape(sequences, local_rows, head_count, HEAD_DIM)
        return block_grads(
            query_heads,
            grad_att_heads,
            log_total,
            row_delta,
            key_heads,
            value_heads,
            usable,
            score_scale,
        )

    def cycle_turn(turn_index, carried):
        key_block, value_block, grad_key, grad_value, grad_query = carried
        source = (ctx_index - turn_index) % ctx_count
        added_query, added_key, added_value = turn_grads(
            source * local_rows, key_block, value_block
        )
        key_block, value_block = passed_along((key_block, value_block), "ctx", 1)
        grad_key, grad_value = (
            passed_along((grad_key + added_key).astype(jnp.bfloat16), "ctx", 1).astype(jnp.float32),
            passed_along((grad_value + added_value).astype(jnp.bfloat16), "ctx", 1).astype(
                jnp.float32
            ),
        )
        return (key_block, value_block, grad_key, grad_value, grad_query + added_query)

    cycle_end = lax.fori_loop(
        0, ctx_count, cycle_turn, (key_local, value_local, zero_block, zero_block, zero_block)
    )
    grad_key, grad_value, grad_query = (cycle_end[2], cycle_end[3], cycle_end[4])
    grad_query_low = grad_query.reshape(token_count, local_width).astype(jnp.bfloat16)
    grad_key_low = grad_key.reshape(token_count, local_width).astype(jnp.bfloat16)
    grad_value_low = grad_value.reshape(token_count, local_width).astype(jnp.bfloat16)
    grad_w_query = jnp.einsum(
        "nd,nc->dc", flat_tokens, grad_query_low, preferred_element_type=jnp.float32
    )
    grad_w_key = jnp.einsum(
        "nd,nc->dc", flat_tokens, grad_key_low, preferred_element_type=jnp.float32
    )
    grad_w_value = jnp.einsum(
        "nd,nc->dc", flat_tokens, grad_value_low, preferred_element_type=jnp.float32
    )
    grad_b_query = jnp.sum(grad_query_low.astype(jnp.float32), axis=0)
    grad_b_value = jnp.sum(grad_value_low.astype(jnp.float32), axis=0)
    back_in = (
        jnp.einsum("nc,dc->nd", grad_query_low, query_full, preferred_element_type=jnp.float32)
        + jnp.einsum("nc,dc->nd", grad_key_low, key_full, preferred_element_type=jnp.float32)
        + jnp.einsum("nc,dc->nd", grad_value_low, value_full, preferred_element_type=jnp.float32)
    )
    grad_tokens = grad_resid_one + lax.psum(back_in.astype(jnp.bfloat16), "tp").astype(jnp.float32)
    (
        share_query,
        share_key,
        share_value,
        share_out,
        share_up,
        share_down,
        share_bias_out,
        share_gain_one,
        share_shift_one,
        share_bias_down,
        share_gain_two,
        share_shift_two,
    ) = (
        lax.psum_scatter(
            grad_w_query.astype(jnp.bfloat16), "fsdp", scatter_dimension=0, tiled=True
        ).astype(jnp.float32),
        lax.psum_scatter(
            grad_w_key.astype(jnp.bfloat16), "fsdp", scatter_dimension=0, tiled=True
        ).astype(jnp.float32),
        lax.psum_scatter(
            grad_w_value.astype(jnp.bfloat16), "fsdp", scatter_dimension=0, tiled=True
        ).astype(jnp.float32),
        lax.psum_scatter(
            grad_w_out.astype(jnp.bfloat16), "fsdp", scatter_dimension=1, tiled=True
        ).astype(jnp.float32),
        lax.psum_scatter(
            grad_w_up.astype(jnp.bfloat16), "fsdp", scatter_dimension=0, tiled=True
        ).astype(jnp.float32),
        lax.psum_scatter(
            grad_w_down.astype(jnp.bfloat16), "fsdp", scatter_dimension=1, tiled=True
        ).astype(jnp.float32),
        lax.psum_scatter(
            grad_b_out.astype(jnp.bfloat16), "fsdp", scatter_dimension=0, tiled=True
        ).astype(jnp.float32),
        lax.psum_scatter(
            grad_gain_one.astype(jnp.bfloat16), "fsdp", scatter_dimension=0, tiled=True
        ).astype(jnp.float32),
        lax.psum_scatter(
            grad_shift_one.astype(jnp.bfloat16), "fsdp", scatter_dimension=0, tiled=True
        ).astype(jnp.float32),
        lax.psum_scatter(
            grad_b_down.astype(jnp.bfloat16), "fsdp", scatter_dimension=0, tiled=True
        ).astype(jnp.float32),
        lax.psum_scatter(
            grad_gain_two.astype(jnp.bfloat16), "fsdp", scatter_dimension=0, tiled=True
        ).astype(jnp.float32),
        lax.psum_scatter(
            grad_shift_two.astype(jnp.bfloat16), "fsdp", scatter_dimension=0, tiled=True
        ).astype(jnp.float32),
    )
    (
        share_query,
        share_key,
        share_value,
        share_out,
        share_up,
        share_down,
        share_bias_out,
        share_gain_one,
        share_shift_one,
        share_bias_down,
        share_gain_two,
        share_shift_two,
    ) = (
        lax.psum(share_query.astype(jnp.bfloat16), "ctx").astype(jnp.float32),
        lax.psum(share_key.astype(jnp.bfloat16), "ctx").astype(jnp.float32),
        lax.psum(share_value.astype(jnp.bfloat16), "ctx").astype(jnp.float32),
        lax.psum(share_out.astype(jnp.bfloat16), "ctx").astype(jnp.float32),
        lax.psum(share_up.astype(jnp.bfloat16), "ctx").astype(jnp.float32),
        lax.psum(share_down.astype(jnp.bfloat16), "ctx").astype(jnp.float32),
        lax.psum(share_bias_out.astype(jnp.bfloat16), "ctx").astype(jnp.float32),
        lax.psum(share_gain_one.astype(jnp.bfloat16), "ctx").astype(jnp.float32),
        lax.psum(share_shift_one.astype(jnp.bfloat16), "ctx").astype(jnp.float32),
        lax.psum(share_bias_down.astype(jnp.bfloat16), "ctx").astype(jnp.float32),
        lax.psum(share_gain_two.astype(jnp.bfloat16), "ctx").astype(jnp.float32),
        lax.psum(share_shift_two.astype(jnp.bfloat16), "ctx").astype(jnp.float32),
    )
    total_b_query, total_b_value, total_b_up = lax.psum(
        (grad_b_query, grad_b_value, grad_b_up), ("fsdp", "ctx")
    )
    return (
        output.astype(jnp.bfloat16).reshape(sequences, local_rows, model_width),
        grad_tokens.reshape(sequences, local_rows, model_width),
        share_query,
        share_key,
        share_value,
        total_b_query,
        total_b_value,
        share_out,
        share_bias_out,
        share_gain_one,
        share_shift_one,
        share_up,
        total_b_up,
        share_down,
        share_bias_down,
        share_gain_two,
        share_shift_two,
    )


def solution(mesh):
    placed = (
        P("fsdp", "ctx", None),
        P("fsdp"),
        P("fsdp", "ctx", None),
        P("fsdp", "tp"),
        P("fsdp", "tp"),
        P("fsdp", "tp"),
        P("tp"),
        P("tp"),
        P("tp", "fsdp"),
        P("fsdp"),
        P("fsdp"),
        P("fsdp"),
        P("fsdp", "tp"),
        P("tp"),
        P("tp", "fsdp"),
        P("fsdp"),
        P("fsdp"),
        P("fsdp"),
    )
    return jax.shard_map(
        per_device,
        mesh=mesh,
        in_specs=placed,
        out_specs=(
            P("fsdp", "ctx", None),
            P("fsdp", "ctx", None),
            P("fsdp", "tp"),
            P("fsdp", "tp"),
            P("fsdp", "tp"),
            P("tp"),
            P("tp"),
            P("tp", "fsdp"),
            P("fsdp"),
            P("fsdp"),
            P("fsdp"),
            P("fsdp", "tp"),
            P("tp"),
            P("tp", "fsdp"),
            P("fsdp"),
            P("fsdp"),
            P("fsdp"),
        ),
        check_vma=False,
    )
```

profile of v0, /device:TPU:0, one launch (start us, length us, event | category | flops | bytes accessed | tf_op | source)
XLA Modules:
  0.0 627.3 jit_solution(12311233955386079272)
XLA Ops:
  10.6 8.4 %all_gather.47 = bf16[192,768]{0,1:T(8,128)(2,1)} all-gather(bf16[192,192]{0,1:T(8,128)(2,1)S(1)} %copy.68), channel_id=1, replica_groups=mesh['fsdp'=4,'ctx'=2,'tp'=4] {'fsdp'}, dimensions={1}, use_global_device_ids=true | all-gather | bytes 368640 | tf_op jit(solution)/shard_map/all_gather | solution.py:128
  19.0 6.8 %all_gather.44 = bf16[768,192]{1,0:T(8,128)(2,1)S(1)} all-gather(bf16[192,192]{1,0:T(8,128)(2,1)} %param.25), channel_id=1, replica_groups=mesh['fsdp'=4,'ctx'=2,'tp'=4] {'fsdp'}, dimensions={0}, use_global_device_ids=true | all-gather | bytes 368640 | tf_op jit(solution)/shard_map/all_gather | solution.py:125
  28.3 6.6 %all_gather.42 = bf16[768,192]{1,0:T(8,128)(2,1)S(1)} all-gather(bf16[192,192]{1,0:T(8,128)(2,1)S(1)} %copy-done.36), channel_id=1, replica_groups=mesh['fsdp'=4,'ctx'=2,'tp'=4] {'fsdp'}, dimensions={0}, use_global_device_ids=true | all-gather | bytes 368640 | tf_op jit(solution)/shard_map/all_gather | solution.py:126
  34.9 6.6 %all_gather.45 = bf16[768,192]{1,0:T(8,128)(2,1)S(1)} all-gather(bf16[192,192]{1,0:T(8,128)(2,1)S(1)} %copy-done.37), channel_id=1, replica_groups=mesh['fsdp'=4,'ctx'=2,'tp'=4] {'fsdp'}, dimensions={0}, use_global_device_ids=true | all-gather | bytes 368640 | tf_op jit(solution)/shard_map/all_gather | solution.py:127
  44.4 12.2 %all_gather.43 = bf16[2,1024,192]{1,2,0:T(8,128)(2,1)S(1)} all-gather(bf16[2,512,192]{1,2,0:T(8,128)(2,1)} %bitcast.150), channel_id=1, replica_groups=mesh['fsdp'=4,'ctx'=2,'tp'=4] {'ctx'}, dimensions={1}, use_global_device_ids=true | all-gather | bytes 1179648 | tf_op jit(solution)/shard_map/all_gather | solution.py:162
  56.6 11.4 %all_gather.46 = bf16[2,1024,192]{1,2,0:T(8,128)(2,1)S(1)} all-gather(bf16[2,512,192]{1,2,0:T(8,128)(2,1)} %bitcast.149), channel_id=1, replica_groups=mesh['fsdp'=4,'ctx'=2,'tp'=4] {'ctx'}, dimensions={1}, use_global_device_ids=true | all-gather | bytes 1179648 | tf_op jit(solution)/shard_map/all_gather | solution.py:163
  68.0 14.0 %while.42 = (s32[]{:T(128)}, f32[2,3,512]{2,1,0:T(4,128)S(1)}, f32[2,3,512]{2,1,0:T(4,128)}, f32[2,3,512,64]{2,3,1,0:T(8,128)}, s32[2]{0:T(128)}, /*index=5*/bf1...) while((s32[]{:T(128)}, f32[2,3,512]{2,1,0:T(4,128)S(1)}, ...), condition=%wide.region_3.4_spmd.clone, body=%wide.region_0.3_spmd.clone.sunk | while | flops 423707136 | bytes 29794612 | solution.py:178
  91.0 11.4 %all-reduce.14 = (bf16[768]{0:T(1024)(128)(2,1)S(1)}, bf16[768]{0:T(1024)(128)(2,1)S(1)}, bf16[768]{0:T(1024)(128)(2,1)S(1)}, bf16[768]{0:T(1024)(128)(2,1)}, bf16[768]{0:T(1024)(128)(2,1)}) all-reduce(bf16[768]{0:T(1024)(128)(2,1)S(1)} %dynamic-update-slice, ...), channel_id=1, replica_groups=mesh['fsdp'=4,'ctx'=2,'tp'=4] {'fsdp'}, use_global_device_ids=true, to_apply=%add | all-reduce | flops 3840 | bytes 15360
  102.5 54.8 %all-reduce.23.cloned.1.call-done = bf16[1024,768]{1,0:T(8,128)(2,1)} async-done(((bf16[1024,768]{1,0:T(8,128)(2,1)}), bf16[1024,768]{1,0:T(8,128)(2,1)}) %all-reduce.23.cloned.1.call-update) | async-done | bytes 1572880 | tf_op jit(solution)/shard_map/psum | solution.py:182
  162.0 11.6 %multiply_convert_fusion.1 = (bf16[1024,768]{1,0:T(8,128)(2,1)}, f32[1024,768]{1,0:T(8,128)}, f32[1024,768]{1,0:T(8,128)}) fusion(f32[768]{0:T(1024)S(1)} %convert_element_type.333, bf16[768,768]{1,0:T(8,128)(2,1)} %all-gather.3.cloned.1.call-done, f32[1024,768]{1,0:T(8,128)} %get-tuple-element.723, f32[768]{0:T(1024)S(1)} %convert_element_type.331, ...), kind=kOutput, calls=%fused_computation.61 | convolution fusion | flops 1263009792 | bytes 12203008 | tf_op jit(solution)/shard_map/dot_general | solution.py:193
  173.7 4.5 convolution_convert_fusion.1
  182.9 63.6 %all-reduce.25.cloned.1.call-done = bf16[1024,768]{1,0:T(8,128)(2,1)} async-done(((bf16[1024,768]{1,0:T(8,128)(2,1)}), bf16[1024,768]{1,0:T(8,128)(2,1)}) %all-reduce.25.cloned.1.call-update) | async-done | bytes 1572880 | tf_op jit(solution)/shard_map/psum | solution.py:198
  266.7 66.8 %all-reduce.27.cloned.1.call-done = bf16[1024,768]{1,0:T(8,128)(2,1)} async-done(((bf16[1024,768]{1,0:T(8,128)(2,1)}), bf16[1024,768]{1,0:T(8,128)(2,1)}) %all-reduce.27.cloned.1.call-update) | async-done | bytes 1572880 | tf_op jit(solution)/shard_map/psum | solution.py:222
  333.5 4.1 multiply_reduce_fusion.2
  344.9 91.9 %while.43 = (s32[]{:T(128)}, bf16[2,512,192]{1,2,0:T(8,128)(2,1)}, bf16[2,512,192]{1,2,0:T(8,128)(2,1)}, f32[2,512,3,64]{1,3,2,0:T(8,128)}, f32[2,512,3,64]{1,3,...) while((s32[]{:T(128)}, bf16[2,512,192]{1,2,0:T(8,128)(2,1)}, ...), condition=%wide.region_17.18_spmd.clone, body=%wide.region_16.17_spmd.clone.sunk | while | flops 1027868160 | bytes 53227096 | solution.py:271
  350.6 3.5 multiply_convert_fusion.3
  369.8 6.5 %collective-permute-done.3 = bf16[2,512,3,64]{1,3,2,0:T(8,128)(2,1)} collective-permute-done((bf16[2,512,3,64]{1,3,2,0:T(8,128)(2,1)}, bf16[2,512,3,64]{1,3,2,0:T(8,128)(2,1)}, u32[]{:S(2)}, u32[]{:S(2)}) %collective-permute-start.3) | collective-permute-done | bytes 393248 | tf_op jit(solution)/shard_map/while/body/eval_jaxpr/ppermute | solution.py:18
  378.3 6.4 %collective-permute-done = bf16[2,512,192]{1,2,0:T(8,128)(2,1)} collective-permute-done((bf16[2,512,192]{1,2,0:T(8,128)(2,1)}, bf16[2,512,192]{1,2,0:T(8,128)(2,1)}, u32[]{:S(2)}, u32[]{:S(2)}) %collective-permute-start) | collective-permute-done | bytes 393248 | tf_op jit(solution)/shard_map/while/body/eval_jaxpr/ppermute | solution.py:18
  384.7 6.5 %collective-permute-done.1 = bf16[2,512,192]{1,2,0:T(8,128)(2,1)} collective-permute-done((bf16[2,512,192]{1,2,0:T(8,128)(2,1)}, bf16[2,512,192]{1,2,0:T(8,128)(2,1)}, u32[]{:S(2)}, u32[]{:S(2)}) %collective-permute-start.1) | collective-permute-done | bytes 393248 | tf_op jit(solution)/shard_map/while/body/eval_jaxpr/ppermute | solution.py:18
  416.2 6.5 %collective-permute-done.3 = bf16[2,512,3,64]{1,3,2,0:T(8,128)(2,1)} collective-permute-done((bf16[2,512,3,64]{1,3,2,0:T(8,128)(2,1)}, bf16[2,512,3,64]{1,3,2,0:T(8,128)(2,1)}, u32[]{:S(2)}, u32[]{:S(2)}) %collective-permute-start.3) | collective-permute-done | bytes 393248 | tf_op jit(solution)/shard_map/while/body/eval_jaxpr/ppermute | solution.py:18
  424.6 6.4 %collective-permute-done = bf16[2,512,192]{1,2,0:T(8,128)(2,1)} collective-permute-done((bf16[2,512,192]{1,2,0:T(8,128)(2,1)}, bf16[2,512,192]{1,2,0:T(8,128)(2,1)}, u32[]{:S(2)}, u32[]{:S(2)}) %collective-permute-start) | collective-permute-done | bytes 393248 | tf_op jit(solution)/shard_map/while/body/eval_jaxpr/ppermute | solution.py:18
  431.1 5.7 collective-permute-done.1
  448.2 4.7 convolution_convert_fusion.3
  452.9 4.0 convolution_convert_fusion.4
  466.7 20.0 %reduce-scatter.23.cloned.1.call-done = bf16[192,192]{1,0:T(8,128)(2,1)} async-done(((bf16[768,192]{1,0:T(8,128)(2,1)}), bf16[192,192]{1,0:T(8,128)(2,1)}) %reduce-scatter.23.cloned.1.call-update) | async-done | bytes 73744
  488.3 21.6 %reduce-scatter.19.cloned.1.call-done = bf16[192,192]{1,0:T(8,128)(2,1)} async-done(((bf16[768,192]{1,0:T(8,128)(2,1)}), bf16[192,192]{1,0:T(8,128)(2,1)}) %reduce-scatter.19.cloned.1.call-update) | async-done | bytes 73744
  511.6 26.3 %reduce-scatter.17.cloned.1.call-done = bf16[768,192]{0,1:T(8,128)(2,1)} async-done(((bf16[768,768]{0,1:T(8,128)(2,1)}), bf16[768,192]{0,1:T(8,128)(2,1)}) %reduce-scatter.17.cloned.1.call-update) | async-done | bytes 294928 | tf_op jit(solution)/shard_map/reduce_scatter | solution.py:324
  538.0 28.6 %reduce-scatter.15.cloned.1.call-done = bf16[192,768]{1,0:T(8,128)(2,1)} async-done(((bf16[768,768]{1,0:T(8,128)(2,1)}), bf16[192,768]{1,0:T(8,128)(2,1)}) %reduce-scatter.15.cloned.1.call-update) | async-done | bytes 294928 | tf_op jit(solution)/shard_map/reduce_scatter | solution.py:321
  568.4 10.5 %all-reduce.13 = (bf16[768]{0:T(1024)(128)(2,1)S(1)}, bf16[768]{0:T(1024)(128)(2,1)S(1)}, bf16[768]{0:T(1024)(128)(2,1)S(1)}, bf16[768]{0:T(1024)(128)(2,1)S(1)}...) all-reduce(bf16[768]{0:T(1024)(128)(2,1)S(1)} %dynamic-update-slice, ...), channel_id=1, replica_groups=mesh['fsdp'=4,'ctx'=2,'tp'=4] {'fsdp'}, use_global_device_ids=true, to_apply=%add.5 | all-reduce | flops 5376 | bytes 21504
  579.4 5.0 all-reduce.15
  588.0 15.3 %all-reduce.12 = (f32[192]{0:T(256)}, f32[192]{0:T(256)}, f32[768]{0:T(1024)}) all-reduce(f32[192]{0:T(256)S(1)} %reduce_sum.227, f32[192]{0:T(256)S(1)} %reduce_sum.229, f32[768]{0:T(1024)S(1)} %copy-done.64), channel_id=1, replica_groups=mesh['fsdp'=4,'ctx'=2,'tp'=4] {'fsdp','ctx'}, use_global_device_ids=true, to_apply=%region_26.27 | all-reduce | flops 1152 | bytes 9216 | tf_op jit(solution)/shard_map/psum | solution.py:373
  605.1 4.4 convert_add_fusion
  (369 shorter events, 157.8 us)
Async XLA Ops:
  8.1 149.2 %all-reduce.23.cloned.1.call-start = ((), (), s32[]{:S(2)}) async-start(), calls=%async_computation.6 | async-start | bytes 3145728 | tf_op jit(solution)/shard_map/psum | solution.py:182
  87.3 74.7 %all-gather.3.cloned.1.call-start = ((), (), s32[]{:S(2)}) async-start(), calls=%async_computation.7 | async-start | bytes 1474560 | tf_op jit(solution)/shard_map/all_gather | solution.py:129
  87.9 85.8 %all-gather.5.cloned.1.call-start = ((), (), s32[]{:S(2)}) async-start(), calls=%async_computation.8 | async-start | bytes 1474560 | tf_op jit(solution)/shard_map/all_gather | solution.py:130
  88.4 158.0 %all-reduce.25.cloned.1.call-start = ((), (), s32[]{:S(2)}) async-start(), calls=%async_computation.9 | async-start | bytes 3145728 | tf_op jit(solution)/shard_map/psum | solution.py:198
  178.2 155.3 %all-reduce.27.cloned.1.call-start = ((), (), s32[]{:S(2)}) async-start(), calls=%async_computation.10 | async-start | bytes 3145728 | tf_op jit(solution)/shard_map/psum | solution.py:222
  265.2 198.2 %reduce-scatter.25.cloned.1.call-start = ((), (), s32[]{:S(2)}) async-start(), calls=%async_computation.17 | async-start | bytes 491520
  344.5 120.5 %reduce-scatter.21.cloned.1.call-start = ((), (), s32[]{:S(2)}) async-start(), calls=%async_computation.15 | async-start | bytes 491520
  355.6 12.3 %collective-permute-start.2 = (bf16[2,512,3,64]{1,3,2,0:T(8,128)(2,1)}, bf16[2,512,3,64]{1,3,2,0:T(8,128)(2,1)}, u32[]{:S(2)}, u32[]{:S(2)}) collective-permute-start(bf16[2,512,3,64]{1,3,2,0:T(8,128)(2,1)} %fusion.155), channel_id=1, source_target_pairs={{0,4},{4,0},{1,5},{5,1},{2,6},{6,2},{3,7},{7,3},{8,12},{12,8},{9,1... | collective-permute-start | bytes 1179656 | tf_op jit(solution)/shard_map/while/body/eval_jaxpr/ppermute | solution.py:18
  359.4 16.9 %collective-permute-start.3 = (bf16[2,512,3,64]{1,3,2,0:T(8,128)(2,1)}, bf16[2,512,3,64]{1,3,2,0:T(8,128)(2,1)}, u32[]{:S(2)}, u32[]{:S(2)}) collective-permute-start(bf16[2,512,3,64]{1,3,2,0:T(8,128)(2,1)} %fusion.156), channel_id=1, source_target_pairs={{0,4},{4,0},{1,5},{5,1},{2,6},{6,2},{3,7},{7,3},{8,12},{12,8},{9,1... | collective-permute-start | bytes 1179656 | tf_op jit(solution)/shard_map/while/body/eval_jaxpr/ppermute | solution.py:18
  359.9 24.8 %collective-permute-start = (bf16[2,512,192]{1,2,0:T(8,128)(2,1)}, bf16[2,512,192]{1,2,0:T(8,128)(2,1)}, u32[]{:S(2)}, u32[]{:S(2)}) collective-permute-start(bf16[2,512,192]{1,2,0:T(8,128)(2,1)} %copy.129), channel_id=1, source_target_pairs={{0,4},{4,0},{1,5},{5,1},{2,6},{6,2},{3,7},{7,3},{8,12},{12,8},{9,1... | collective-permute-start | bytes 1179656 | tf_op jit(solution)/shard_map/while/body/eval_jaxpr/ppermute | solution.py:18
  361.4 29.9 %collective-permute-start.1 = (bf16[2,512,192]{1,2,0:T(8,128)(2,1)}, bf16[2,512,192]{1,2,0:T(8,128)(2,1)}, u32[]{:S(2)}, u32[]{:S(2)}) collective-permute-start(bf16[2,512,192]{1,2,0:T(8,128)(2,1)} %copy.130), channel_id=1, source_target_pairs={{0,4},{4,0},{1,5},{5,1},{2,6},{6,2},{3,7},{7,3},{8,12},{12,8},{9,1... | collective-permute-start | bytes 1179656 | tf_op jit(solution)/shard_map/while/body/eval_jaxpr/ppermute | solution.py:18
  401.9 12.3 %collective-permute-start.2 = (bf16[2,512,3,64]{1,3,2,0:T(8,128)(2,1)}, bf16[2,512,3,64]{1,3,2,0:T(8,128)(2,1)}, u32[]{:S(2)}, u32[]{:S(2)}) collective-permute-start(bf16[2,512,3,64]{1,3,2,0:T(8,128)(2,1)} %fusion.155), channel_id=1, source_target_pairs={{0,4},{4,0},{1,5},{5,1},{2,6},{6,2},{3,7},{7,3},{8,12},{12,8},{9,1... | collective-permute-start | bytes 1179656 | tf_op jit(solution)/shard_map/while/body/eval_jaxpr/ppermute | solution.py:18
  405.7 16.9 %collective-permute-start.3 = (bf16[2,512,3,64]{1,3,2,0:T(8,128)(2,1)}, bf16[2,512,3,64]{1,3,2,0:T(8,128)(2,1)}, u32[]{:S(2)}, u32[]{:S(2)}) collective-permute-start(bf16[2,512,3,64]{1,3,2,0:T(8,128)(2,1)} %fusion.156), channel_id=1, source_target_pairs={{0,4},{4,0},{1,5},{5,1},{2,6},{6,2},{3,7},{7,3},{8,12},{12,8},{9,1... | collective-permute-start | bytes 1179656 | tf_op jit(solution)/shard_map/while/body/eval_jaxpr/ppermute | solution.py:18
  406.3 24.8 %collective-permute-start = (bf16[2,512,192]{1,2,0:T(8,128)(2,1)}, bf16[2,512,192]{1,2,0:T(8,128)(2,1)}, u32[]{:S(2)}, u32[]{:S(2)}) collective-permute-start(bf16[2,512,192]{1,2,0:T(8,128)(2,1)} %copy.129), channel_id=1, source_target_pairs={{0,4},{4,0},{1,5},{5,1},{2,6},{6,2},{3,7},{7,3},{8,12},{12,8},{9,1... | collective-permute-start | bytes 1179656 | tf_op jit(solution)/shard_map/while/body/eval_jaxpr/ppermute | solution.py:18
  407.8 29.0 %collective-permute-start.1 = (bf16[2,512,192]{1,2,0:T(8,128)(2,1)}, bf16[2,512,192]{1,2,0:T(8,128)(2,1)}, u32[]{:S(2)}, u32[]{:S(2)}) collective-permute-start(bf16[2,512,192]{1,2,0:T(8,128)(2,1)} %copy.130), channel_id=1, source_target_pairs={{0,4},{4,0},{1,5},{5,1},{2,6},{6,2},{3,7},{7,3},{8,12},{12,8},{9,1... | collective-permute-start | bytes 1179656 | tf_op jit(solution)/shard_map/while/body/eval_jaxpr/ppermute | solution.py:18
  441.5 45.2 %reduce-scatter.23.cloned.1.call-start = ((), (), s32[]{:S(2)}) async-start(), calls=%async_computation.16 | async-start | bytes 491520
  445.4 64.6 %reduce-scatter.19.cloned.1.call-start = ((), (), s32[]{:S(2)}) async-start(), calls=%async_computation.14 | async-start | bytes 491520
  448.1 89.9 %reduce-scatter.17.cloned.1.call-start = ((), (), s32[]{:S(2)}) async-start(), calls=%async_computation.13 | async-start | bytes 1474560 | tf_op jit(solution)/shard_map/reduce_scatter | solution.py:324
  452.8 113.7 %reduce-scatter.15.cloned.1.call-start = ((), (), s32[]{:S(2)}) async-start(), calls=%async_computation.12 | async-start | bytes 1474560 | tf_op jit(solution)/shard_map/reduce_scatter | solution.py:321
  457.0 148.1 %all-reduce.29.cloned.1.call-start = ((), (), s32[]{:S(2)}) async-start(), calls=%async_computation.11 | async-start | bytes 3145728 | tf_op jit(solution)/shard_map/psum | solution.py:294
  461.5 106.8 %copy-start.58 = (bf16[768]{0:T(1024)(128)(2,1)S(1)}, bf16[768]{0:T(1024)(128)(2,1)}, u32[]{:S(2)}) copy-start(bf16[768]{0:T(1024)(128)(2,1)} %get-tuple-element.710) | copy-start | bytes 4612
  461.5 106.9 %copy-start.59 = (bf16[768]{0:T(1024)(128)(2,1)S(1)}, bf16[768]{0:T(1024)(128)(2,1)}, u32[]{:S(2)}) copy-start(bf16[768]{0:T(1024)(128)(2,1)} %get-tuple-element.712) | copy-start | bytes 4612
  461.6 106.9 %copy-start.60 = (bf16[768]{0:T(1024)(128)(2,1)S(1)}, bf16[768]{0:T(1024)(128)(2,1)}, u32[]{:S(2)}) copy-start(bf16[768]{0:T(1024)(128)(2,1)} %get-tuple-element.630) | copy-start | bytes 4612
  461.6 106.9 %copy-start.61 = (bf16[768]{0:T(1024)(128)(2,1)S(1)}, bf16[768]{0:T(1024)(128)(2,1)}, u32[]{:S(2)}) copy-start(bf16[768]{0:T(1024)(128)(2,1)} %get-tuple-element.634) | copy-start | bytes 4612
  461.6 126.3 %copy-start.63 = (f32[3,64]{1,0:T(4,128)S(1)}, f32[3,64]{1,0:T(4,128)}, u32[]{:S(2)}) copy-start(f32[3,64]{1,0:T(4,128)} %get-tuple-element.706) | copy-start | bytes 2308
  461.6 126.4 %copy-start.62 = (f32[3,64]{1,0:T(4,128)S(1)}, f32[3,64]{1,0:T(4,128)}, u32[]{:S(2)}) copy-start(f32[3,64]{1,0:T(4,128)} %get-tuple-element.733) | copy-start | bytes 2308
  461.6 126.4 %copy-start.64 = (f32[768]{0:T(1024)S(1)}, f32[768]{0:T(1024)}, u32[]{:S(2)}) copy-start(f32[768]{0:T(1024)} %get-tuple-element.704) | copy-start | bytes 9220
  461.6 141.7 %copy-start.3 = (f32[1024,768]{1,0:T(8,128)S(1)}, f32[1024,768]{1,0:T(8,128)}, u32[]{:S(2)}) copy-start(f32[1024,768]{1,0:T(8,128)} %copy-done.2) | copy-start | bytes 9437188
  461.6 141.7 %copy-start.35 = (f32[1024]{0:T(1024)S(1)}, f32[1024]{0:T(1024)}, u32[]{:S(2)}) copy-start(f32[1024]{0:T(1024)} %copy-done.34) | copy-start | bytes 12292
  461.6 141.7 %copy-start.45 = (f32[768]{0:T(1024)S(1)}, f32[768]{0:T(1024)}, u32[]{:S(2)}) copy-start(f32[768]{0:T(1024)} %convert_element_type.338) | copy-start | bytes 9220
  461.6 141.7 %copy-start.47 = (f32[1024]{0:T(1024)S(1)}, f32[1024]{0:T(1024)}, u32[]{:S(2)}) copy-start(f32[1024]{0:T(1024)} %copy-done.46) | copy-start | bytes 12292
  461.7 147.8 %all-reduce.31.cloned.1.call-start = ((), (), s32[]{:S(2)}) async-start(), calls=%async_computation.18 | async-start | bytes 1966080 | tf_op jit(solution)/shard_map/psum | solution.py:360
  (77 other events, 1072.7 us)
Sparse Core Ops, SparseCore 0:
  87.4 69.8 all-reduce.22
  178.3 68.1 all-reduce.24
  265.4 68.1 all-reduce.26
  461.8 69.9 all-reduce.28
  566.7 39.6 all-reduce.30
Sparse Core Ops, SparseCore 1:
  89.3 18.2 all-gather.2
  109.0 17.3 all-gather.4
  344.6 19.9 reduce-scatter.24
  441.6 21.8 reduce-scatter.20
  466.0 20.7 reduce-scatter.22
  489.2 20.7 reduce-scatter.18
  512.4 25.5 reduce-scatter.16
  541.0 25.5 reduce-scatter.14
where the time goes:
time: 635 us; the launch traced here: 627 us
  waiting for transfers between devices  327 us (51%)
  blocking collectives  94.2 us (15%)
  matrix products  76.5 us (12%)
  other arithmetic  60.1 us (9%)
  local copies, waits for them, and re-layouts  41.6 us (7%)
  between operations  18.3 us (3%)
  starting transfers between devices  9.41 us (1%)
    psum x1, waiting for transfers between devices, per_device(): lax.psum(jnp.einsum('nf,df->nd', grad_hidden_low, up_full, preferred_elem...  66.8 us
    psum x1, waiting for transfers between devices, per_device(): lax.psum(jnp.dot(active_low, down_full, preferred_element_type=jnp.float3...  63.6 us
    psum x1, waiting for transfers between devices, per_device(): lax.psum(jnp.dot(attended_low, out_full, preferred_element_type=jnp.float...  54.8 us
    ppermute x8, waiting for transfers between devices, passed_along(): return lax.ppermute(value, axis, pairs)  43.7 us
    unnamed x17, waiting for transfers between devices  42.9 us
    unnamed x178, local copies, waits for them, and re-layouts  28.6 us
    reduce_scatter x1, waiting for transfers between devices, per_device(): lax.psum_scatter(grad_w_up.astype(jnp.bfloat16), 'fsdp', scatter_dimensio...  28.6 us
    reduce_scatter x1, waiting for transfers between devices, per_device(): lax.psum_scatter(grad_w_down.astype(jnp.bfloat16), 'fsdp', scatter_dimens...  26.3 us
  transfers between devices with their start and end apart: 21, of which 15 were waited for; matrix products, arithmetic and copies ran while one was open for 17% of the time, Pallas kernels for 0%

commit v1 on v0

--- a/solution.py
+++ b/solution.py
@@ -3,6 +3,8 @@
 import jax
 import jax.numpy as jnp
 from jax import lax
+from jax.experimental import pallas as pl
+from jax.experimental.pallas import tpu as pltpu
 from jax.sharding import PartitionSpec as P
 
 HEAD_DIM = 64
@@ -394,6 +396,694 @@
     )
 
 
+def swapped(value, axis, bit):
+    count = lax.axis_size(axis)
+    return lax.ppermute(value, axis, [(place, place ^ bit) for place in range(count)])
+
+
+def shifted(value, axis, steps):
+    count = lax.axis_size(axis)
+    return lax.ppermute(value, axis, [(place, (place + steps) % count) for place in range(count)])
+
+
+def to_owner(value, step, back=False):
+    pairs = []
+    for x in range(2):
+        for z in range(4):
+            block = z ^ step
+            source = x * 4 + z
+            target = (block >> 1) * 4 + 2 * (block & 1) + x
+            pairs.append((target, source) if back else (source, target))
+    return lax.ppermute(value, ("ctx", "tp"), pairs)
+
+
+def xor_ordered(stack, bits):
+    count = stack.shape[0]
+    order = lax.iota(jnp.int32, count) ^ bits
+    return jnp.take(stack, order, axis=0)
+
+
+def line_gathered(value):
+    z = lax.axis_index("tp")
+    up_pairs, down_pairs = [(0, 1), (1, 2), (2, 3)], [(1, 0), (2, 1), (3, 2)]
+    ups, downs = [], []
+    going_up, going_down = value, value
+    for step in range(3):
+        going_up = lax.ppermute(going_up, "tp", up_pairs[step:])
+        going_down = lax.ppermute(going_down, "tp", down_pairs[: 3 - step])
+        ups.append(going_up)
+        downs.append(going_down)
+    blocks = []
+    for block in range(4):
+        choices = [
+            value if place == block else (ups[place - block - 1] if place > block else downs[block - place - 1])
+            for place in range(4)
+        ]
+        blocks.append(lax.select_n(z, *choices))
+    return blocks
+
+
+ANY = pl.BlockSpec(memory_space=pl.ANY)
+WHOLE = pl.BlockSpec(memory_space=pltpu.VMEM)
+log2_e = math.log2(math.e)
+
+
+def low(value):
+    return value.astype(jnp.bfloat16)
+
+
+def wide(value):
+    return value.astype(jnp.float32)
+
+
+def dot32(left, right, left_dim, right_dim):
+    return lax.dot_general(
+        left, right, (((left_dim,), (right_dim,)), ((), ())), preferred_element_type=jnp.float32
+    )
+
+
+def struct(shape, dtype=jnp.bfloat16):
+    return jax.ShapeDtypeStruct(shape, dtype)
+
+
+def cost(flops, moved, special=0):
+    return pl.CostEstimate(flops=int(flops), bytes_accessed=int(moved), transcendentals=int(special))
+
+
+def stack_kernel(*refs):
+    for place, ref in enumerate(refs[:-1]):
+        refs[-1][place] = ref[...]
+
+
+def stacked(pieces):
+    shape = (len(pieces),) + pieces[0].shape
+    return pl.pallas_call(
+        stack_kernel,
+        out_shape=struct(shape),
+        in_specs=[WHOLE] * len(pieces),
+        out_specs=WHOLE,
+        cost_estimate=cost(0, 4 * math.prod(shape)),
+        name="stack_pieces",
+    )(*pieces)
+
+
+def spread_pack(own_half, x_first):
+    line = stacked([own_half] + [shifted(own_half, "tp", step) for step in (1, 2, 3)])
+    if x_first:
+        x_side = swapped(line, "ctx", 1)
+        y_side, xy_side = swapped(line, "fsdp", 2), swapped(x_side, "fsdp", 2)
+    else:
+        y_side = swapped(line, "fsdp", 2)
+        x_side, xy_side = swapped(line, "ctx", 1), swapped(y_side, "ctx", 1)
+    near = (line, x_side, y_side, xy_side)
+    return near + tuple(swapped(piece, "fsdp", 1) for piece in near)
+
+
+def piece_copies(meta, pieces, columns, target, sems, first):
+    x, z, f = meta[0], meta[1], meta[2]
+    rows = pieces[0].shape[1]
+    copies = []
+    for place, piece in enumerate(pieces):
+        across = (place % 2, 2 * ((place // 2) % 2) + place // 4)
+        start = pl.multiple_of(((f ^ across[1]) * 2 + (x ^ across[0])) * rows, rows)
+        for step in range(4):
+            copies.append(
+                pltpu.make_async_copy(
+                    piece.at[step, :, columns],
+                    target.at[(z + 4 - step) & 3, pl.ds(start, rows), :],
+                    sems.at[first + len(copies)],
+                )
+            )
+    return copies
+
+
+def attend_kernel(
+    meta, own, other, w0, w1, w2, w3, bias, qkv, o0, o1, o2, o3, stats, weight, mask, *, block, heads
+):
+    step = pl.program_id(0)
+    shard = w0.shape[0]
+    half = own.shape[1]
+    scale = log2_e * HEAD_DIM ** (-0.5)
+
+    @pl.when(step == 0)
+    def _():
+        for place, piece in enumerate((w0, w1, w2, w3)):
+            start = pl.multiple_of((meta[2] ^ place) * shard, shard)
+            weight[pl.ds(start, shard), :] = piece[...]
+        for place, rows in enumerate((own, other)):
+            source = rows[0] if place == 0 else rows[...]
+            qkv[place * half : (place + 1) * half, :] = low(
+                dot32(source, weight[...], 1, 0) + bias[...]
+            )
+            first = (meta[0] ^ place) * half
+            position = first + lax.broadcasted_iota(jnp.int32, (half, block), 0)
+            mask[place * half : (place + 1) * half, :] = jnp.where(
+                position < meta[3], 0.0, masked_score
+            )
+
+    rows = pl.ds(pl.multiple_of((meta[7] ^ step) * block, block), block)
+    outs, logs = [], []
+    for head in range(heads):
+        base = 3 * head * HEAD_DIM
+        query = qkv[rows, base : base + HEAD_DIM]
+        key = qkv[:, base + HEAD_DIM : base + 2 * HEAD_DIM]
+        value = qkv[:, base + 2 * HEAD_DIM : base + 3 * HEAD_DIM]
+        scores = dot32(key, query, 1, 1) * scale + mask[...]
+        peak = jnp.max(scores, axis=0, keepdims=True)
+        weights = jnp.exp2(scores - peak)
+        total = jnp.sum(weights, axis=0, keepdims=True)
+        outs.append((dot32(value, low(weights), 0, 0) / total).T)
+        logs.append(peak + jnp.log2(total))
+    result = low(jnp.concatenate(outs, axis=1))
+    for place, out in enumerate((o0, o1, o2, o3)):
+
+        @pl.when(step == place)
+        def _(out=out):
+            out[...] = result
+
+    stats[0] = jnp.concatenate(logs + [jnp.zeros((8 - heads, block), jnp.float32)], axis=0)
+
+
+def attend_call(meta, tokens, other, pieces, bias, heads):
+    half, width = other.shape
+    block = half // 2
+    columns = pieces[0].shape[1]
+    whole = lambda shape: pl.BlockSpec(shape, lambda step, meta: (0,) * len(shape))
+    rows = 2 * half
+    return pl.pallas_call(
+        lambda *refs: attend_kernel(*refs, block=block, heads=heads),
+        grid_spec=pltpu.PrefetchScalarGridSpec(
+            num_scalar_prefetch=1,
+            grid=(4,),
+            in_specs=[
+                pl.BlockSpec((1, half, width), lambda step, meta: (meta[0], 0, 0)),
+                whole((half, width)),
+                *[whole(piece.shape) for piece in pieces],
+                whole((1, columns)),
+            ],
+            out_specs=[
+                whole((rows, columns)),
+                *[whole((block, columns // 3))] * 4,
+                pl.BlockSpec((1, 8, block), lambda step, meta: (step, 0, 0)),
+            ],
+            scratch_shapes=[
+                pltpu.VMEM((width, columns), jnp.bfloat16),
+                pltpu.VMEM((rows, block), jnp.float32),
+            ],
+        ),
+        out_shape=[struct((rows, columns))]
+        + [struct((block, columns // 3))] * 4
+        + [struct((4, 8, block), jnp.float32)],
+        cost_estimate=cost(2 * rows * width * columns + 16 * rows * rows * columns, 8e6, rows * rows * 3),
+        name="attend",
+    )(meta, tokens, other, *pieces, bias)
+
+
+def attend_back_kernel(
+    meta, qkv, d0, d1, d2, d3, o0, o1, o2, o3, stats, full, p0, p1, p2, p3,
+    grads, mask, grad_att, attended, *, block, heads
+):
+    step = pl.program_id(0)
+    rows_all = qkv.shape[0]
+    half = rows_all // 2
+    scale = log2_e * HEAD_DIM ** (-0.5)
+
+    @pl.when(step == 0)
+    def _():
+        grads[...] = jnp.zeros_like(grads)
+        for place in range(2):
+            first = (meta[0] ^ place) * half
+            position = first + lax.broadcasted_iota(jnp.int32, (half, block), 0)
+            mask[place * half : (place + 1) * half, :] = jnp.where(
+                position < meta[3], 0.0, masked_score
+            )
+
+    for place, (grad, out) in enumerate(zip((d0, d1, d2, d3), (o0, o1, o2, o3))):
+
+        @pl.when(step == place)
+        def _(grad=grad, out=out):
+            grad_att[...] = grad[...]
+            attended[...] = out[...]
+
+    rows = pl.ds(pl.multiple_of((meta[7] ^ step) * block, block), block)
+    for head in range(heads):
+        base = 3 * head * HEAD_DIM
+        span = slice(head * HEAD_DIM, (head + 1) * HEAD_DIM)
+        query = qkv[rows, base : base + HEAD_DIM]
+        key = qkv[:, base + HEAD_DIM : base + 2 * HEAD_DIM]
+        value = qkv[:, base + 2 * HEAD_DIM : base + 3 * HEAD_DIM]
+        grad_out = grad_att[:, span]
+        products = wide(grad_out) * wide(attended[:, span])
+        delta = lax.dot_general(
+            jnp.ones((8, HEAD_DIM), jnp.float32),
+            products,
+            (((1,), (1,)), ((), ())),
+            precision=lax.Precision.HIGHEST,
+            preferred_element_type=jnp.float32,
+        )[:1]
+        scores = dot32(key, query, 1, 1) * scale + mask[...]
+        weights = jnp.exp2(scores - stats[0, head : head + 1, :])
+        grad_weights = dot32(value, grad_out, 1, 1)
+        grad_scores = low(weights * (grad_weights - delta))
+        grads[2 * head] += dot32(grad_scores, query, 1, 0)
+        grads[2 * head + 1] += dot32(low(weights), grad_out, 1, 0)
+        full[rows, base : base + HEAD_DIM] = low(
+            dot32(grad_scores, key, 0, 0) * HEAD_DIM ** (-0.5)
+        )
+
+    @pl.when(step == 3)
+    def _():
+        for head in range(heads):
+            base = 3 * head * HEAD_DIM
+            full[:, base + HEAD_DIM : base + 2 * HEAD_DIM] = low(
+                grads[2 * head] * HEAD_DIM ** (-0.5)
+            )
+            full[:, base + 2 * HEAD_DIM : base + 3 * HEAD_DIM] = low(grads[2 * head + 1])
+        for place, part in enumerate((p0, p1, p2, p3)):
+            part[...] = full[pl.ds(pl.multiple_of((meta[7] ^ place) * block, block), block), :]
+
+
+def attend_back_call(meta, qkv, grad_parts, parts, stats, heads):
+    rows, columns = qkv.shape
+    block = rows // 4
+    whole = lambda shape: pl.BlockSpec(shape, lambda step, meta: (0,) * len(shape))
+    small = whole((block, columns // 3))
+    return pl.pallas_call(
+        lambda *refs: attend_back_kernel(*refs, block=block, heads=heads),
+        grid_spec=pltpu.PrefetchScalarGridSpec(
+            num_scalar_prefetch=1,
+            grid=(4,),
+            in_specs=[whole((rows, columns))]
+            + [small] * 8
+            + [pl.BlockSpec((1, 8, block), lambda step, meta: (step, 0, 0))],
+            out_specs=[whole((rows, columns))] + [whole((block, columns))] * 4,
+            scratch_shapes=[
+                pltpu.VMEM((2 * heads, rows, HEAD_DIM), jnp.float32),
+                pltpu.VMEM((rows, block), jnp.float32),
+                pltpu.VMEM((block, columns // 3), jnp.bfloat16),
+                pltpu.VMEM((block, columns // 3), jnp.bfloat16),
+            ],
+        ),
+        out_shape=[struct((rows, columns))] + [struct((block, columns))] * 4,
+        cost_estimate=cost(40 * rows * rows * columns, 8e6, rows * rows * 3),
+        name="attend_back",
+    )(meta, qkv, *grad_parts, *parts, stats)
+
+
+def norm_parts(inputs):
+    center = jnp.mean(inputs, axis=-1, keepdims=True)
+    centered = inputs - center
+    spread = jnp.mean(centered * centered, axis=-1, keepdims=True)
+    inverse = lax.rsqrt(spread + epsilon)
+    return centered * inverse, inverse
+
+
+def norm_back(grad_out, hat, inverse, gain):
+    scaled = grad_out * gain
+    return inverse * (
+        scaled
+        - jnp.mean(scaled, axis=-1, keepdims=True)
+        - hat * jnp.mean(scaled * hat, axis=-1, keepdims=True)
+    )
+
+
+BIAS_OUT, GAIN_ONE, SHIFT_ONE, BIAS_DOWN, GAIN_TWO, SHIFT_TWO = range(6)
+
+
+def first_kernel(meta, *refs, width):
+    att, tok, vectors, up_bias = refs[:4], refs[4], refs[5], refs[6]
+    pieces = refs[7:15]
+    hat, inverse, active, slope, out_w, up_w, sems = refs[15:]
+    hidden = up_w.shape[2]
+    copies = piece_copies(meta, pieces, pl.ds(hidden, out_w.shape[2]), out_w, sems, 0)
+    copies += piece_copies(meta, pieces, pl.ds(0, hidden), up_w, sems, 32)
+    for copy in copies:
+        copy.start()
+    for copy in copies:
+        copy.wait()
+    branch = vectors[BIAS_OUT : BIAS_OUT + 1, :]
+    for step in range(4):
+        branch = branch + dot32(att[step][...], out_w[meta[4] ^ step][:, :width], 1, 1)
+    hat_one, inverse_one = norm_parts(wide(tok[0]) + branch)
+    hat[...] = hat_one
+    inverse[...] = inverse_one
+    normed = low(hat_one * vectors[GAIN_ONE : GAIN_ONE + 1, :] + vectors[SHIFT_ONE : SHIFT_ONE + 1, :])
+    for place in range(4):
+        inputs = dot32(normed, up_w[place], 1, 0) + up_bias[place : place + 1, :]
+        cumulative = 0.5 * (1.0 + lax.erf(inputs * (0.5**0.5)))
+        density = jnp.exp(-0.5 * inputs * inputs) * ((0.5 / math.pi) ** 0.5)
+        active[place] = low(inputs * cumulative)
+        slope[place] = low(cumulative + inputs * density)
+
+
+def second_kernel(meta, *refs, width):
+    hat, inverse, active, slope, cot, vectors = refs[:6]
+    pieces_a, pieces_b = refs[6:14], refs[14:22]
+    outputs = refs[22:34]
+    output, resid, g0, g1, g2, g3, hidden_grad, keep, send, small, = outputs[:10]
+    out_w, up_w, down_w, blocks, sems = refs[32:]
+    model = hat.shape[1]
+    rows = hat.shape[0]
+    hidden = up_w.shape[2]
+    down_copies = piece_copies(meta, pieces_b, pl.ds(0, hidden), down_w, sems, 0)
+    copies = piece_copies(meta, pieces_a, pl.ds(0, hidden), up_w, sems, 32)
+    copies += piece_copies(meta, pieces_a, pl.ds(hidden, out_w.shape[2]), out_w, sems, 64)
+    for copy in down_copies + copies:
+        copy.start()
+    row = lambda place: vectors[place : place + 1, :]
+    hat_one, inverse_one = hat[...], inverse[...]
+    normed_one = hat_one * row(GAIN_ONE) + row(SHIFT_ONE)
+    for copy in down_copies:
+        copy.wait()
+    second = row(BIAS_DOWN)
+    for place in range(4):
+        second = second + dot32(active[place], down_w[place], 1, 1)
+    hat_two, inverse_two = norm_parts(normed_one + second)
+    output[...] = low(hat_two * row(GAIN_TWO) + row(SHIFT_TWO))
+    position = meta[4] * rows + lax.broadcasted_iota(jnp.int32, (rows, model), 0)
+    grad_output = jnp.where(position < meta[8], wide(cot[0]), 0.0)
+    grad_two = norm_back(grad_output, hat_two, inverse_two, row(GAIN_TWO))
+    grad_second = low(grad_two)
+    for copy in copies:
+        copy.wait()
+    grad_normed = grad_two
+    sums = lambda array: jnp.sum(array, axis=0, keepdims=True)
+    for place in range(4):
+        grad_hidden = low(dot32(grad_second, down_w[place], 1, 0) * wide(slope[place]))
+        hidden_grad[place] = grad_hidden
+        grad_normed = grad_normed + dot32(grad_hidden, up_w[place], 1, 1)
+        small[6 + place : 7 + place, :] = sums(wide(grad_hidden))
+    grad_one = norm_back(grad_normed, hat_one, inverse_one, row(GAIN_ONE))
+    resid[...] = grad_one
+    grad_branch = low(grad_one)
+    for step, out in enumerate((g0, g1, g2, g3)):
+        out[...] = low(dot32(grad_branch, out_w[meta[4] ^ step][:, :width], 1, 0))
+    small[0:1, :] = sums(wide(grad_branch))
+    small[1:2, :] = sums(grad_normed * hat_one)
+    small[2:3, :] = sums(grad_normed)
+    small[3:4, :] = sums(wide(grad_second))
+    small[4:5, :] = sums(grad_output * hat_two)
+    small[5:6, :] = sums(grad_output)
+    small[10:16, :] = jnp.zeros((6, model), jnp.float32)
+    shard = model // 4
+    for kind, array in enumerate((grad_second, low(normed_one), grad_branch)):
+        for place in range(4):
+            blocks[place] = array[:, place * shard : (place + 1) * shard]
+        for far in range(2):
+            keep[kind, far] = blocks[meta[2] ^ (2 * far)]
+            send[kind, far] = blocks[meta[2] ^ (2 * far + 1)]
+
+
+def weights_kernel(meta, *refs, width):
+    keep, got = refs[0], refs[1]
+    active, active_sib, grad, grad_sib = refs[2:6]
+    att, att_sib = refs[6:10], refs[10:14]
+    near_mine, near_theirs, far_mine, far_theirs = refs[14:18]
+    turned, whole = refs[18:]
+    shard = keep.shape[3]
+    rows = keep.shape[2]
+    half = shard // 2
+    hidden = active.shape[2]
+    mine = pl.multiple_of(meta[0] * half, half)
+    theirs = pl.multiple_of((1 - meta[0]) * half, half)
+
+    def store(value, target, first):
+        columns = value.shape[1]
+        whole[:, :columns] = value
+        for far, pair in enumerate(((near_mine, near_theirs), (far_mine, far_theirs))):
+            for start, out in zip((mine, theirs), pair):
+                out[target, :, first : first + columns] = low(
+                    whole[pl.ds(far * shard + start, half), :columns]
+                )
+
+    for kind, (own, sib, first) in enumerate(
+        ((active, active_sib, hidden), (grad, grad_sib, 0), (att, att_sib, 2 * hidden))
+    ):
+        for far in range(2):
+            span = slice(far * shard, (far + 1) * shard)
+            turned[span, :rows] = keep[kind, far].T
+            turned[span, rows:] = got[kind, far].T
+        for place in range(4):
+            left = own[place][...] if kind == 2 else own[place]
+            right = sib[place][...] if kind == 2 else sib[place]
+            value = dot32(turned[:, :rows], left, 1, 0) + dot32(turned[:, rows:], right, 1, 0)
+            store(value, (meta[4] ^ place) if kind == 2 else place, first)
+
+
+def tokens_kernel(meta, *refs):
+    resid, parts, pieces = refs[0], refs[1:5], refs[5:13]
+    out, weight, sems = refs[13:]
+    copies = piece_copies(meta, pieces, pl.ds(0, weight.shape[2]), weight, sems, 0)
+    for copy in copies:
+        copy.start()
+    total = resid[...]
+    for copy in copies:
+        copy.wait()
+    for step in range(4):
+        total = total + dot32(parts[step][...], weight[meta[4] ^ step], 1, 1)
+    out[...] = low(total)
+
+
+def per_device_rows(
+    tokens,
+    lengths,
+    cotangent,
+    w_query,
+    w_key,
+    w_value,
+    b_query,
+    b_value,
+    w_out,
+    b_out,
+    ln1_gain,
+    ln1_shift,
+    w_up,
+    b_up,
+    w_down,
+    b_down,
+    ln2_gain,
+    ln2_shift,
+):
+    sequences, local_rows, model = tokens.shape
+    x, f, z = lax.axis_index("ctx"), lax.axis_index("fsdp"), lax.axis_index("tp")
+    rows = local_rows // 2
+    width = w_query.shape[1]
+    heads = width // HEAD_DIM
+    hidden = w_up.shape[1]
+    shard = w_query.shape[0]
+    half = shard // 2
+    padded = -(-width // 128) * 128
+    own_seq, own_place = z % 2, z // 2
+    quarter = 2 * x + own_place
+    length_of = lambda place: lax.dynamic_index_in_dim(lengths, place, 0, keepdims=False)
+    meta = jnp.stack(
+        [x, z, f, length_of(x), quarter, own_seq, own_place, z ^ (2 * x), length_of(own_seq)]
+    ).astype(jnp.int32)
+    smem = pl.BlockSpec(memory_space=pltpu.SMEM)
+
+    other = swapped(lax.dynamic_index_in_dim(tokens, 1 - x, 0, keepdims=False), "ctx", 1)
+    per_head = lambda weights: jnp.concatenate(
+        [
+            weight[..., head * HEAD_DIM : (head + 1) * HEAD_DIM]
+            for head in range(heads)
+            for weight in weights
+        ],
+        axis=-1,
+    )
+    qkv_shard = per_head((w_query, w_key, w_value))
+    qkv_bias = wide(per_head((b_query, jnp.zeros_like(b_query), b_value)))[None, :]
+    qkv_y = swapped(qkv_shard, "fsdp", 2)
+    qkv_pieces = (qkv_shard, swapped(qkv_shard, "fsdp", 1), qkv_y, swapped(qkv_y, "fsdp", 1))
+
+    vectors = jnp.stack([b_out, ln1_gain, ln1_shift, b_down, ln2_gain, ln2_shift])
+    pair = jnp.stack([vectors, swapped(vectors, "fsdp", 1)])
+    gathered = jnp.concatenate([pair, swapped(pair, "fsdp", 2)])
+    vectors = wide(xor_ordered(gathered, f).transpose(1, 0, 2).reshape(6, model))
+    up_near = jnp.stack([b_up, swapped(b_up, "tp", 1)])
+    up_bias = wide(xor_ordered(jnp.concatenate([up_near, swapped(up_near, "tp", 2)]), z))
+
+    take_half = lambda pack: lax.dynamic_slice_in_dim(pack, x * half, half, 0)
+    pack_a = jnp.concatenate(
+        [w_up, w_out.T, jnp.zeros((shard, padded - width), jnp.bfloat16)], axis=1
+    )
+    pieces_a = spread_pack(take_half(pack_a), True)
+    pieces_b = spread_pack(take_half(w_down.T), False)
+    pieces_c = spread_pack(take_half(qkv_shard), True)
+
+    qkv, *parts, stats = attend_call(meta, tokens, other, qkv_pieces, qkv_bias, heads)
+    att = [to_owner(part, step) for step, part in enumerate(parts)]
+
+    def row_spec(array):
+        return pl.BlockSpec((1, rows, model), lambda step, meta: (meta[5], meta[6], 0))
+
+    one = lambda *refs: refs
+    vm = lambda shape, dtype=jnp.bfloat16: pltpu.VMEM(shape, dtype)
+    weights_scratch = [vm((4, model, padded)), vm((4, model, hidden))]
+    grid = lambda inputs, outputs, scratch: pltpu.PrefetchScalarGridSpec(
+        num_scalar_prefetch=1, grid=(1,), in_specs=inputs, out_specs=outputs, scratch_shapes=scratch
+    )
+    full = lambda shape: pl.BlockSpec(shape, lambda step, meta: (0,) * len(shape))
+    specs = lambda shapes: [full(item.shape) for item in shapes]
+
+    first_out = [
+        struct((rows, model), jnp.float32),
+        struct((rows, 1), jnp.float32),
+        struct((4, rows, hidden)),
+        struct((4, rows, hidden)),
+    ]
+    hat, inverse, active, slope = pl.pallas_call(
+        lambda *refs: first_kernel(*refs, width=width),
+        grid_spec=grid(
+            [full((rows, width))] * 4
+            + [row_spec(tokens), full((6, model)), full((4, hidden))]
+            + [ANY] * 8,
+            specs(first_out),
+            weights_scratch + [pltpu.SemaphoreType.DMA((64,))],
+        ),
+        out_shape=first_out,
+        cost_estimate=cost(2 * rows * model * (model + 4 * hidden), 12e6, rows * hidden * 8),
+        name="feed_first",
+    )(meta, *att, tokens, vectors, up_bias, *pieces_a)
+
+    second_out = [
+        struct((rows, model)),
+        struct((rows, model), jnp.float32),
+        *[struct((rows, width))] * 4,
+        struct((4, rows, hidden)),
+        struct((3, 2, rows, shard)),
+        struct((3, 2, rows, shard)),
+        struct((16, model), jnp.float32),
+    ]
+    output, resid, g0, g1, g2, g3, hidden_grad, keep, send, small = pl.pallas_call(
+        lambda *refs: second_kernel(*refs, width=width),
+        grid_spec=grid(
+            specs(first_out) + [row_spec(cotangent), full((6, model))] + [ANY] * 16,
+            specs(second_out),
+            weights_scratch
+            + [vm((4, model, hidden)), vm((4, rows, shard)), pltpu.SemaphoreType.DMA((96,))],
+        ),
+        out_shape=second_out,
+        cost_estimate=cost(2 * rows * model * (model + 12 * hidden), 20e6),
+        name="feed_second",
+    )(meta, hat, inverse, active, slope, cotangent, vectors, *pieces_a, *pieces_b)
+
+    grad_att = [to_owner(part, step, True) for step, part in enumerate((g0, g1, g2, g3))]
+
+    core = lambda array: swapped(array, "fsdp", 1)
+    half_pack = struct((4, half, 2 * hidden + padded))
+    near_mine, near_theirs, far_mine, far_theirs = pl.pallas_call(
+        lambda *refs: weights_kernel(*refs, width=width),
+        grid_spec=grid(
+            [full(keep.shape)] * 2 + [full(active.shape)] * 4 + [full((rows, width))] * 8,
+            specs([half_pack] * 4),
+            [vm((2 * shard, 2 * rows)), vm((2 * shard, hidden), jnp.float32)],
+        ),
+        out_shape=[half_pack] * 4,
+        cost_estimate=cost(8 * rows * shard * (8 * hidden + 4 * width), 20e6),
+        name="feed_weights",
+    )(meta, keep, core(send), active, core(active), hidden_grad, core(hidden_grad), *att, *map(core, att))
+
+    grad_full, *grad_parts = attend_back_call(meta, qkv, grad_att, parts, stats, heads)
+    grad_rows = [to_owner(part, step) for step, part in enumerate(grad_parts)]
+    token_rows = pl.pallas_call(
+        tokens_kernel,
+        grid_spec=grid(
+            [full((rows, model))] + [full((rows, 3 * width))] * 4 + [ANY] * 8,
+            full((rows, model)),
+            [vm((4, model, 3 * width)), pltpu.SemaphoreType.DMA((32,))],
+        ),
+        out_shape=struct((rows, model)),
+        cost_estimate=cost(24 * rows * model * width, 8e6),
+        name="token_grads",
+    )(meta, resid, *grad_rows, *pieces_c)
+
+    def spread_rows(block, dtype):
+        blocks = [item.astype(dtype) for item in line_gathered(block)]
+        return jnp.stack([jnp.concatenate([blocks[seq], blocks[2 + seq]]) for seq in range(2)])
+
+    output_full = spread_rows(output, jnp.bfloat16)
+    grad_tokens = spread_rows(token_rows, jnp.float32)
+
+    theirs = low(wide(near_theirs) + wide(swapped(far_theirs, "fsdp", 2)))
+    mine = wide(near_mine) + wide(swapped(far_mine, "fsdp", 2))
+    mine = low(mine + wide(swapped(theirs, "ctx", 1)))
+    total = wide(lax.dynamic_index_in_dim(mine, z, 0, keepdims=False))
+    for step in (1, 2, 3):
+        piece = lax.dynamic_index_in_dim(mine, (z + step) % 4, 0, keepdims=False)
+        total = total + wide(shifted(piece, "tp", step))
+    total = low(total)
+    other_half = swapped(total, "ctx", 1)
+    total = wide(jnp.concatenate([jnp.where(x == 0, total, other_half), jnp.where(x == 0, other_half, total)]))
+    grad_w_up = total[:, :hidden]
+    grad_w_down = total[:, hidden : 2 * hidden].T
+    grad_w_out = total[:, 2 * hidden : 2 * hidden + width].T
+
+    own_half = lax.dynamic_index_in_dim(tokens, x, 0, keepdims=False)
+    grad_w_qkv = dot32(own_half, grad_full[:local_rows], 0, 0) + dot32(other, grad_full[local_rows:], 0, 0)
+    grad_w_qkv = jnp.concatenate(
+        [
+            grad_w_qkv.reshape(4, shard, 3 * width),
+            jnp.broadcast_to(jnp.sum(wide(grad_full), axis=0), (4, 16, 3 * width)),
+        ],
+        axis=1,
+    )
+    at = lambda array, place: lax.dynamic_index_in_dim(array, place, 0, keepdims=False)
+    sent = low(jnp.stack([at(grad_w_qkv, f ^ 1), at(grad_w_qkv, f ^ 3)]))
+    kept = jnp.stack([at(grad_w_qkv, f), at(grad_w_qkv, f ^ 2)]) + wide(swapped(sent, "fsdp", 1))
+    kept = low(kept[0] + wide(swapped(low(kept[1]), "fsdp", 2)))
+    kept = wide(kept) + wide(swapped(kept, "ctx", 1))
+
+    def unpack(array, part):
+        return jnp.concatenate(
+            [
+                array[:, (3 * head + part) * HEAD_DIM : (3 * head + part + 1) * HEAD_DIM]
+                for head in range(heads)
+            ],
+            axis=1,
+        )
+
+    grad_w_query, grad_w_key, grad_w_value = (unpack(kept[:shard], part) for part in range(3))
+    grad_b_query, grad_b_value = (unpack(kept[shard : shard + 1], part)[0] for part in (0, 2))
+
+    for axis, bit in (("fsdp", 1), ("fsdp", 2), ("ctx", 1), ("tp", 1), ("tp", 2)):
+        small = small + swapped(small, axis, bit)
+    small_own = lax.dynamic_slice_in_dim(small[:6], f * shard, shard, 1)
+    grad_b_up = lax.dynamic_index_in_dim(small, 6 + z, 0, keepdims=False)
+    return (
+        output_full,
+        grad_tokens,
+        grad_w_query,
+        grad_w_key,
+        grad_w_value,
+        grad_b_query,
+        grad_b_value,
+        grad_w_out,
+        small_own[0],
+        small_own[1],
+        small_own[2],
+        grad_w_up,
+        grad_b_up,
+        grad_w_down,
+        small_own[3],
+        small_own[4],
+        small_own[5],
+    )
+
+
+def rows_path_fits(mesh, tokens, w_query, w_up):
+    shape = dict(mesh.shape)
+    return (
+        shape["ctx"] == 2
+        and shape["fsdp"] == 4
+        and shape["tp"] == 4
+        and tokens.shape[0] == 8
+        and tokens.shape[1] % 1024 == 0
+        and w_query.shape[0] == w_query.shape[1]
+        and w_query.shape[0] % 768 == 0
+        and w_up.shape[1] == 4 * w_up.shape[0]
+    )
+
+
 def solution(mesh):
     placed = (
         P("fsdp", "ctx", None),
@@ -415,8 +1105,9 @@
         P("fsdp"),
         P("fsdp"),
     )
-    return jax.shard_map(
-        per_device,
+    def split(function):
+        return jax.shard_map(
+        function,
         mesh=mesh,
         in_specs=placed,
         out_specs=(
@@ -440,3 +1131,9 @@
         ),
         check_vma=False,
     )
+
+    def run(*arrays):
+        fits = rows_path_fits(mesh, arrays[0], arrays[3], arrays[12])
+        return split(per_device_rows if fits else per_device)(*arrays)
+
+    return run

time: 635 us -> 352 us (0.55)
  waiting for transfers between devices: 327 us -> 112 us
  blocking collectives: 94.2 us -> 0 us
  starting transfers between devices: 9.41 us -> 103 us
  Pallas kernels: 0 us -> 77.4 us
  matrix products: 76.5 us -> 3.83 us
  other arithmetic: 60.1 us -> 20.7 us
  between operations: 18.3 us -> 1.79 us
  local copies, waits for them, and re-layouts: 41.6 us -> 26.1 us
    psum x5 -> x0, waiting for transfers between devices: 185 us -> none  [the longest x1 66.8 us: per_device(): lax.psum(jnp.einsum('nf,df->nd', grad_hidden_low, up_full, preferred_elem...]
    ppermute x8 -> x84, starting transfers between devices: 8.1 us -> 103 us  [the longest x12 31.9 us: to_owner(): return lax.ppermute(value, ('ctx', 'tp'), pairs)]
    pallas_call x0 -> x9, Pallas kernels: none -> 77.4 us  [the longest x1 15.6 us: attend_back_call(): pl.pallas_call(lambda *refs: attend_back_kernel(*refs, block=block, heads...]
    dot_general x32 -> x2, matrix products: 76.5 us -> 3.83 us  [dot32(): lax.dot_general(left, right, (((left_dim,), (right_dim,)), ((), ())), pre...]
    ppermute x8 -> x84, waiting for transfers between devices: 43.7 us -> 112 us  [the longest x12 34.2 us: to_owner(): return lax.ppermute(value, ('ctx', 'tp'), pairs)]
    reduce_scatter x2 -> x0, waiting for transfers between devices: 54.9 us -> none  [the longest x1 28.6 us: per_device(): lax.psum_scatter(grad_w_up.astype(jnp.bfloat16), 'fsdp', scatter_dimensio...]
    all_gather x6 -> x0, blocking collectives: 51.9 us -> none  [the longest x1 12.2 us: per_device(): key_part = lax.all_gather(key_local, 'ctx', axis=1, tiled=True)]
    unnamed x17 -> x0, waiting for transfers between devices: 42.9 us -> none
  transfers between devices with their start and end apart: 21 -> 84, of which waited for: 15 -> 25; matrix products, arithmetic and copies ran while one was open for 17% -> 12% of each run, Pallas kernels for 0% -> 22%
where the time goes in v1:
time: 352 us; the launch traced here: 346 us
  waiting for transfers between devices  112 us (32%)
  starting transfers between devices  103 us (29%)
  Pallas kernels  77.4 us (22%)
  local copies, waits for them, and re-layouts  26.1 us (7%)
  other arithmetic  20.7 us (6%)
  matrix products  3.83 us (1%)
    ppermute x12, waiting for transfers between devices, to_owner(): return lax.ppermute(value, ('ctx', 'tp'), pairs)  34.2 us
    ppermute x48, waiting for transfers between devices, swapped(): lax.ppermute(value, axis, [(place, place ^ bit) for place in range(count)])  32.3 us
    ppermute x12, starting transfers between devices, to_owner(): return lax.ppermute(value, ('ctx', 'tp'), pairs)  31.9 us
    ppermute x48, starting transfers between devices, swapped(): lax.ppermute(value, axis, [(place, place ^ bit) for place in range(count)])  30 us
    ppermute x6, waiting for transfers between devices, line_gathered(): going_down = lax.ppermute(going_down, 'tp', down_pairs[:3 - step])  27.3 us
    ppermute x12, starting transfers between devices, shifted(): lax.ppermute(value, axis, [(place, (place + steps) % count) for place in...  24.3 us
    pallas_call x1, Pallas kernels, attend_back_call(): pl.pallas_call(lambda *refs: attend_back_kernel(*refs, block=block, heads...  15.6 us
    ppermute x12, waiting for transfers between devices, shifted(): lax.ppermute(value, axis, [(place, (place + steps) % count) for place in...  15.4 us
  transfers between devices with their start and end apart: 84, of which 25 were waited for; matrix products, arithmetic and copies ran while one was open for 12% of the time, Pallas kernels for 22%

profile of v1, /device:TPU:0, one launch (start us, length us, event | category | flops | bytes accessed | tf_op | source)
XLA Modules:
  0.0 345.6 jit_solution(13032441396038875080)
XLA Ops:
  2.9 3.1 collective-permute-start.12
  14.3 7.2 %collective-permute-done.13.refs_2_ = bf16[96,1024]{1,0:T(8,128)(2,1)S(1)} collective-permute-done((bf16[96,1024]{1,0:T(8,128)(2,1)S(1)}, bf16[96,1024]{1,0:T(8,128)(2,1)S(1)}, u32[]{:S(2)}, u32[]{:S(2)}) %collective-permute-start.13) | collective-permute-done | bytes 196640 | tf_op jit(solution)/shard_map/ppermute | solution.py:406
  21.4 2.9 collective-permute-start.22
  32.3 3.4 collective-permute-start.23
  53.4 14.4 %attend.1 = (bf16[1024,576]{1,0:T(8,128)(2,1)}, bf16[256,192]{1,0:T(8,128)(2,1)}, bf16[256,192]{1,0:T(8,128)(2,1)}, bf16[256,192]{1,0:T(8,128)(2,1)}, bf16[256,192]{1,0:T(8,128)(2,1)}, /*index=5*/f32[4,8,256]{2,1,0:T(8,128)}) custom-call(s32[9]{0:T(128)} %stack.106.refs_0_.meta, bf16[2,512,768]{2,1,0:T(8,128)(2,1)} %refs_5_.2, bf16[512,768]{1,0:T(8,128)(2,1)} %copy-done.13, ...), custom_call_target="tpu_custom_call" | custom-call | flops 10569646080 | bytes 8000000 | tf_op jit(solution)/shard_map/attend/pallas_call | solution.py:573
  69.4 4.3 %collective-permute-start.5 = (bf16[256,192]{1,0:T(8,128)(2,1)}, bf16[256,192]{1,0:T(8,128)(2,1)}, u32[]{:S(2)}, u32[]{:S(2)}) collective-permute-start(bf16[256,192]{1,0:T(8,128)(2,1)} %get-tuple-element.47.refs_7_), channel_id=1, source_target_pairs={{0,2},{1,0},{2,6},{3,4},{4,3},{5,1},{6,7},{7,5},{8,10},{9,8},{10,1... | collective-permute-start | bytes 294920 | tf_op jit(solution)/shard_map/ppermute | solution.py:417
  75.8 7.5 %collective-permute-done.5.refs_2_.refs_8_ = bf16[256,192]{1,0:T(8,128)(2,1)} collective-permute-done((bf16[256,192]{1,0:T(8,128)(2,1)}, bf16[256,192]{1,0:T(8,128)(2,1)}, u32[]{:S(2)}, u32[]{:S(2)}) %collective-permute-start.5) | collective-permute-done | bytes 98336 | tf_op jit(solution)/shard_map/ppermute | solution.py:417
  83.3 3.5 %collective-permute-start.7 = (bf16[256,192]{1,0:T(8,128)(2,1)}, bf16[256,192]{1,0:T(8,128)(2,1)S(1)}, u32[]{:S(2)}, u32[]{:S(2)}) collective-permute-start(bf16[256,192]{1,0:T(8,128)(2,1)} %get-tuple-element.49.refs_9_), channel_id=1, source_target_pairs={{0,6},{1,4},{2,2},{3,0},{4,7},{5,5},{6,3},{7,1},{8,14},{9,12},{10,... | collective-permute-start | bytes 294920 | tf_op jit(solution)/shard_map/ppermute | solution.py:417
  87.5 4.7 %collective-permute-done.7.refs_4_.refs_10_ = bf16[256,192]{1,0:T(8,128)(2,1)S(1)} collective-permute-done((bf16[256,192]{1,0:T(8,128)(2,1)}, bf16[256,192]{1,0:T(8,128)(2,1)S(1)}, u32[]{:S(2)}, u32[]{:S(2)}) %collective-permute-start.7) | collective-permute-done | bytes 98336 | tf_op jit(solution)/shard_map/ppermute | solution.py:417
  94.9 3.1 collective-permute-done.17.refs_11_.refs_10_
  99.2 6.9 %collective-permute-done.27.refs_18_ = bf16[4,96,768]{2,1,0:T(8,128)(2,1)} collective-permute-done((bf16[4,96,768]{2,1,0:T(8,128)(2,1)}, bf16[4,96,768]{2,1,0:T(8,128)(2,1)}, u32[]{:S(2)}, u32[]{:S(2)}) %collective-permute-start.27) | collective-permute-done | bytes 589856 | tf_op jit(solution)/shard_map/ppermute | solution.py:401
  108.9 10.3 %feed_first.1 = (f32[256,768]{1,0:T(8,128)}, f32[256,1]{1,0:T(8,128)}, bf16[4,256,768]{2,1,0:T(8,128)(2,1)}, bf16[4,256,768]{2,1,0:T(8,128)(2,1)}) custom-call(s32[9]{0:T(128)} %stack.106.refs_0_.meta, bf16[256,192]{1,0:T(8,128)(2,1)} %copy-done.29, bf16[256,192]{1,0:T(8,128)(2,1)} %collective-permute-done.5.refs_2_.refs_8_, ...), custom_call_target="tpu_custom_call" | custom-call | flops 1509949440 | bytes 12000000 | tf_op jit(solution)/shard_map/feed_first/pallas_call | solution.py:934
  124.1 14.3 %feed_second.1 = (bf16[256,768]{1,0:T(8,128)(2,1)}, f32[256,768]{1,0:T(8,128)}, bf16[256,192]{1,0:T(8,128)(2,1)}, bf16[256,192]{1,0:T(8,128)(2,1)}, bf16[256,192...) custom-call(s32[9]{0:T(128)} %stack.106.refs_0_.meta, ...), custom_call_target="tpu_custom_call" | custom-call | flops 3925868544 | bytes 20000000 | tf_op jit(solution)/shard_map/feed_second/pallas_call | solution.py:957
  143.1 5.9 %collective-permute-start.41 = (bf16[256,192]{1,0:T(8,128)(2,1)}, bf16[256,192]{1,0:T(8,128)(2,1)S(1)}, u32[]{:S(2)}, u32[]{:S(2)}) collective-permute-start(bf16[256,192]{1,0:T(8,128)(2,1)} %get-tuple-element.60), channel_id=1, source_target_pairs={{6,0},{4,1},{2,2},{0,3},{7,4},{5,5},{3,6},{1,7},{14,8},{12,9},{10,... | collective-permute-start | bytes 294920 | tf_op jit(solution)/shard_map/ppermute | solution.py:417
  157.9 15.6 %attend_back.1 = (bf16[1024,576]{1,0:T(8,128)(2,1)}, bf16[256,576]{1,0:T(8,128)(2,1)}, bf16[256,576]{1,0:T(8,128)(2,1)}, bf16[256,576]{1,0:T(8,128)(2,1)}, bf16[256,576]{1,0:T(8,128)(2,1)}) custom-call(s32[9]{0:T(128)} %stack.106.refs_0_.meta, bf16[1024,576]{1,0:T(8,128)(2,1)} %get-tuple-element.56.refs_1_, bf16[256,192]{1,0:T(8,128)(2,1)} %copy-done.44, ...), custom_call_target="tpu_custom_call" | custom-call | flops 24159191040 | bytes 8000000 | tf_op jit(solution)/shard_map/attend_back/pallas_call | solution.py:671
  188.5 11.3 %collective-permute-done.51.refs_8_ = bf16[4,96,576]{2,1,0:T(8,128)(2,1)S(1)} collective-permute-done((bf16[4,96,576]{2,1,0:T(8,128)(2,1)}, bf16[4,96,576]{2,1,0:T(8,128)(2,1)S(1)}, u32[]{:S(2)}, u32[]{:S(2)}) %collective-permute-start.51) | collective-permute-done | bytes 442400 | tf_op jit(solution)/shard_map/ppermute | solution.py:401
  205.5 9.9 %feed_weights.1 = (bf16[4,96,1792]{2,1,0:T(8,128)(2,1)}, bf16[4,96,1792]{2,1,0:T(8,128)(2,1)}, bf16[4,96,1792]{2,1,0:T(8,128)(2,1)}, bf16[4,96,1792]{2,1,0:T(8,128)(2,1)}) custom-call(s32[9]{0:T(128)} %stack.106.refs_0_.meta, bf16[3,2,256,192]{3,2,1,0:T(8,128)(2,1)} %get-tuple-element.67.refs_1_, bf16[3,2,256,192]{3,2,1,0:T(8,128)(2,1)} %copy.46.refs_2_, ...), custom_call_target="tpu_custom_call" | custom-call | flops 2717908992 | bytes 20000000 | tf_op jit(solution)/shard_map/feed_weights/pallas_call | solution.py:974
  215.4 3.5 %collective-permute-start.43 = (bf16[256,576]{1,0:T(8,128)(2,1)}, bf16[256,576]{1,0:T(8,128)(2,1)}, u32[]{:S(2)}, u32[]{:S(2)}) collective-permute-start(bf16[256,576]{1,0:T(8,128)(2,1)} %get-tuple-element.63), channel_id=1, source_target_pairs={{0,2},{1,0},{2,6},{3,4},{4,3},{5,1},{6,7},{7,5},{8,10},{9,8},{10,1... | collective-permute-start | bytes 884744 | tf_op jit(solution)/shard_map/ppermute | solution.py:417
  219.0 2.9 collective-permute-start.44
  228.0 19.4 %collective-permute-done.43.refs_2_ = bf16[256,576]{1,0:T(8,128)(2,1)} collective-permute-done((bf16[256,576]{1,0:T(8,128)(2,1)}, bf16[256,576]{1,0:T(8,128)(2,1)}, u32[]{:S(2)}, u32[]{:S(2)}) %collective-permute-start.43) | collective-permute-done | bytes 294944 | tf_op jit(solution)/shard_map/ppermute | solution.py:417
  252.6 6.8 %token_grads.1 = bf16[256,768]{1,0:T(8,128)(2,1)} custom-call(s32[9]{0:T(128)} %stack.106.refs_0_.meta, f32[256,768]{1,0:T(8,128)} %get-tuple-element.55.refs_0_, bf16[256,576]{1,0:T(8,128)(2,1)} %copy-done.22, bf16[256,576]{1,0:T(8,128)(2,1)} %collective-permute-done.43.refs_2_, bf16[256,576]{1,0:T(8,128)(2,1)} %collective-permute-done.44.refs_3_, ...), custom_call_target="tpu_custom_call" | custom-call | flops 905969664 | bytes 8000000 | tf_op jit(solution)/shard_map/token_grads/pallas_call | solution.py:988
  261.7 4.5 %collective-permute-start.56 = (bf16[256,768]{1,0:T(8,128)(2,1)}, bf16[256,768]{1,0:T(8,128)(2,1)S(1)}, u32[]{:S(2)}, u32[]{:S(2)}) collective-permute-start(bf16[256,768]{1,0:T(8,128)(2,1)} %token_grads.1), channel_id=1, source_target_pairs={{0,1},{1,2},{2,3},{4,5},{5,6},{6,7},{8,9},{9,10},{10,11},{12,13},{... | collective-permute-start | bytes 1179656 | tf_op jit(solution)/shard_map/ppermute | solution.py:432
  270.7 3.1 collective-permute-done.56
  278.7 4.1 %collective-permute-done.59 = bf16[256,768]{1,0:T(8,128)(2,1)S(1)} collective-permute-done((bf16[256,768]{1,0:T(8,128)(2,1)}, bf16[256,768]{1,0:T(8,128)(2,1)S(1)}, u32[]{:S(2)}, u32[]{:S(2)}) %collective-permute-start.59) | collective-permute-done | bytes 393248 | tf_op jit(solution)/shard_map/ppermute | solution.py:433
  286.7 4.5 %collective-permute-done.36 = bf16[256,768]{1,0:T(8,128)(2,1)S(1)} collective-permute-done((bf16[256,768]{1,0:T(8,128)(2,1)}, bf16[256,768]{1,0:T(8,128)(2,1)S(1)}, u32[]{:S(2)}, u32[]{:S(2)}) %collective-permute-start.36) | collective-permute-done | bytes 393248 | tf_op jit(solution)/shard_map/ppermute | solution.py:433
  296.3 3.4 collective-permute-done.60
  301.7 6.4 %collective-permute-done.37 = bf16[256,768]{1,0:T(8,128)(2,1)S(1)} collective-permute-done((bf16[256,768]{1,0:T(8,128)(2,1)S(1)}, bf16[256,768]{1,0:T(8,128)(2,1)S(1)}, u32[]{:S(2)}, u32[]{:S(2)}) %collective-permute-start.37) | collective-permute-done | bytes 393248 | tf_op jit(solution)/shard_map/ppermute | solution.py:433
  311.5 3.4 collective-permute-start.75
  318.8 8.8 %collective-permute-done.61 = bf16[256,768]{1,0:T(8,128)(2,1)S(1)} collective-permute-done((bf16[256,768]{1,0:T(8,128)(2,1)S(1)}, bf16[256,768]{1,0:T(8,128)(2,1)S(1)}, u32[]{:S(2)}, u32[]{:S(2)}) %collective-permute-start.61) | collective-permute-done | bytes 393248 | tf_op jit(solution)/shard_map/ppermute | solution.py:433
  327.8 5.2 %collective-permute-done.76 = bf16[96,1792]{1,0:T(8,128)(2,1)S(1)} collective-permute-done((bf16[96,1792]{1,0:T(8,128)(2,1)S(1)}, bf16[96,1792]{1,0:T(8,128)(2,1)S(1)}, u32[]{:S(2)}, u32[]{:S(2)}) %collective-permute-start.76) | collective-permute-done | bytes 344096 | tf_op jit(solution)/shard_map/ppermute | solution.py:406
  333.0 3.0 collective-permute-done.77
  339.9 3.8 %collective-permute-done.78 = bf16[96,1792]{1,0:T(8,128)(2,1)S(1)} collective-permute-done((bf16[96,1792]{1,0:T(8,128)(2,1)S(1)}, bf16[96,1792]{1,0:T(8,128)(2,1)S(1)}, u32[]{:S(2)}, u32[]{:S(2)}) %collective-permute-start.78) | collective-permute-done | bytes 344096 | tf_op jit(solution)/shard_map/ppermute | solution.py:401
  (339 shorter events, 132.7 us)
Async XLA Ops:
  11.1 40.0 %collective-permute-start = (bf16[512,768]{1,0:T(8,128)(2,1)S(1)}, bf16[512,768]{1,0:T(8,128)(2,1)S(1)}, u32[]{:S(2)}, u32[]{:S(2)}) collective-permute-start(bf16[512,768]{1,0:T(8,128)(2,1)S(1)} %dynamic-slice_bitcast_fusion), channel_id=1, source_target_pairs={{0,4},{4,0},{1,5},{5,1},{2,6},{6,2},{3,7},{7,3},{8,12},{12,8},{9,1... | collective-permute-start | bytes 2359304 | tf_op jit(solution)/shard_map/ppermute | solution.py:401
  12.7 19.6 %collective-permute-start.10 = (bf16[768]{0:T(1024)(128)(2,1)}, bf16[768]{0:T(1024)(128)(2,1)}, u32[]{:S(2)}, u32[]{:S(2)}) collective-permute-start(bf16[768]{0:T(1024)(128)(2,1)} %param.31), channel_id=1, source_target_pairs={{0,1},{1,0},{2,3},{3,2},{4,5},{5,4},{6,7},{7,6},{8,9},{9,8},{10,11... | collective-permute-start | bytes 4616 | tf_op jit(solution)/shard_map/ppermute | solution.py:401
  14.2 21.5 %collective-permute-start.8 = (bf16[6,192]{1,0:T(8,128)(2,1)S(1)}, bf16[6,192]{1,0:T(8,128)(2,1)S(1)}, u32[]{:S(2)}, u32[]{:S(2)}) collective-permute-start(bf16[6,192]{1,0:T(8,128)(2,1)S(1)} %stack.113), channel_id=1, source_target_pairs={{0,8},{8,0},{16,24},{24,16},{1,9},{9,1},{17,25},{25,17},{2,10},{10... | collective-permute-start | bytes 6920 | tf_op jit(solution)/shard_map/ppermute | solution.py:401
  27.3 25.4 %collective-permute-start.15 = (bf16[4,96,1024]{2,1,0:T(8,128)(2,1)}, bf16[4,96,1024]{2,1,0:T(8,128)(2,1)S(1)}, u32[]{:S(2)}, u32[]{:S(2)}) collective-permute-start(bf16[4,96,1024]{2,1,0:T(8,128)(2,1)} %stack_pieces.3.refs_8_.refs_7_), channel_id=1, source_target_pairs={{0,4},{4,0},{1,5},{5,1},{2,6},{6,2},{3,7},{7,3},{8,12},{12,8},{9,1... | collective-permute-start | bytes 2359304 | tf_op jit(solution)/shard_map/ppermute | solution.py:401
  48.5 19.4 %collective-permute-start.9 = (bf16[2,6,192]{2,1,0:T(8,128)(2,1)S(1)}, bf16[2,6,192]{2,1,0:T(8,128)(2,1)S(1)}, u32[]{:S(2)}, u32[]{:S(2)}) collective-permute-start(bf16[2,6,192]{2,1,0:T(8,128)(2,1)S(1)} %pad_maximum_fusion.7), channel_id=1, source_target_pairs={{0,16},{8,24},{16,0},{24,8},{1,17},{9,25},{17,1},{25,9},{2,18},{10... | collective-permute-start | bytes 13832 | tf_op jit(solution)/shard_map/ppermute | solution.py:401
  50.0 19.4 %collective-permute-start.26 = (bf16[4,96,768]{2,1,0:T(8,128)(2,1)}, bf16[4,96,768]{2,1,0:T(8,128)(2,1)}, u32[]{:S(2)}, u32[]{:S(2)}) collective-permute-start(bf16[4,96,768]{2,1,0:T(8,128)(2,1)} %stack_pieces.4.refs_15_), channel_id=1, source_target_pairs={{0,16},{8,24},{16,0},{24,8},{1,17},{9,25},{17,1},{25,9},{2,18},{10... | collective-permute-start | bytes 1769480 | tf_op jit(solution)/shard_map/ppermute | solution.py:401
  50.5 23.2 %collective-permute-start.25 = (bf16[4,96,768]{2,1,0:T(8,128)(2,1)}, bf16[4,96,768]{2,1,0:T(8,128)(2,1)}, u32[]{:S(2)}, u32[]{:S(2)}) collective-permute-start(bf16[4,96,768]{2,1,0:T(8,128)(2,1)} %stack_pieces.4.refs_15_), channel_id=1, source_target_pairs={{0,4},{4,0},{1,5},{5,1},{2,6},{6,2},{3,7},{7,3},{8,12},{12,8},{9,1... | collective-permute-start | bytes 1769480 | tf_op jit(solution)/shard_map/ppermute | solution.py:401
  51.1 35.9 %collective-permute-start.16 = (bf16[4,96,1024]{2,1,0:T(8,128)(2,1)S(1)}, bf16[4,96,1024]{2,1,0:T(8,128)(2,1)S(1)}, u32[]{:S(2)}, u32[]{:S(2)}) collective-permute-start(bf16[4,96,1024]{2,1,0:T(8,128)(2,1)S(1)} %copy-done.2), channel_id=1, source_target_pairs={{0,16},{8,24},{16,0},{24,8},{1,17},{9,25},{17,1},{25,9},{2,18},{10... | collective-permute-start | bytes 2359304 | tf_op jit(solution)/shard_map/ppermute | solution.py:401
  52.6 45.4 %collective-permute-start.17 = (bf16[4,96,1024]{2,1,0:T(8,128)(2,1)S(1)}, bf16[4,96,1024]{2,1,0:T(8,128)(2,1)S(1)}, u32[]{:S(2)}, u32[]{:S(2)}) collective-permute-start(bf16[4,96,1024]{2,1,0:T(8,128)(2,1)S(1)} %collective-permute-done.15.refs_9_.refs_8_), channel_id=1, source_target_pairs={{0,16},{8,24},{16,0},{24,8},{1,17},{9,25},{17,1},{25,9},{2,18},{10... | collective-permute-start | bytes 2359304 | tf_op jit(solution)/shard_map/ppermute | solution.py:401
  75.7 22.9 %collective-permute-start.18 = (bf16[4,96,1024]{2,1,0:T(8,128)(2,1)S(1)}, bf16[4,96,1024]{2,1,0:T(8,128)(2,1)}, u32[]{:S(2)}, u32[]{:S(2)}) collective-permute-start(bf16[4,96,1024]{2,1,0:T(8,128)(2,1)S(1)} %copy-done.2), channel_id=1, source_target_pairs={{0,8},{8,0},{16,24},{24,16},{1,9},{9,1},{17,25},{25,17},{2,10},{10... | collective-permute-start | bytes 2359304 | tf_op jit(solution)/shard_map/ppermute | solution.py:401
  87.0 19.6 %collective-permute-start.20 = (bf16[4,96,1024]{2,1,0:T(8,128)(2,1)S(1)}, bf16[4,96,1024]{2,1,0:T(8,128)(2,1)}, u32[]{:S(2)}, u32[]{:S(2)}) collective-permute-start(bf16[4,96,1024]{2,1,0:T(8,128)(2,1)S(1)} %collective-permute-done.16.refs_10_.refs_9_), channel_id=1, source_target_pairs={{0,8},{8,0},{16,24},{24,16},{1,9},{9,1},{17,25},{25,17},{2,10},{10... | collective-permute-start | bytes 2359304 | tf_op jit(solution)/shard_map/ppermute | solution.py:401
  98.6 20.6 %collective-permute-start.28 = (bf16[4,96,768]{2,1,0:T(8,128)(2,1)}, bf16[4,96,768]{2,1,0:T(8,128)(2,1)S(1)}, u32[]{:S(2)}, u32[]{:S(2)}) collective-permute-start(bf16[4,96,768]{2,1,0:T(8,128)(2,1)} %stack_pieces.4.refs_15_), channel_id=1, source_target_pairs={{0,8},{8,0},{16,24},{24,16},{1,9},{9,1},{17,25},{25,17},{2,10},{10... | collective-permute-start | bytes 1769480 | tf_op jit(solution)/shard_map/ppermute | solution.py:401
  108.7 33.8 %collective-permute-start.46 = (bf16[96,576]{1,0:T(8,128)(2,1)S(1)}, bf16[96,576]{1,0:T(8,128)(2,1)S(1)}, u32[]{:S(2)}, u32[]{:S(2)}) collective-permute-start(bf16[96,576]{1,0:T(8,128)(2,1)S(1)} %constant_dynamic-slice_fusion.1.refs_0_), channel_id=1, source_target_pairs={{0,1},{1,2},{2,3},{3,0},{4,5},{5,6},{6,7},{7,4},{8,9},{9,10},{10,1... | collective-permute-start | bytes 331784 | tf_op jit(solution)/shard_map/ppermute | solution.py:406
  119.2 23.8 %collective-permute-start.47 = (bf16[96,576]{1,0:T(8,128)(2,1)S(1)}, bf16[96,576]{1,0:T(8,128)(2,1)S(1)}, u32[]{:S(2)}, u32[]{:S(2)}) collective-permute-start(bf16[96,576]{1,0:T(8,128)(2,1)S(1)} %constant_dynamic-slice_fusion.1.refs_0_), channel_id=1, source_target_pairs={{0,2},{1,3},{2,0},{3,1},{4,6},{5,7},{6,4},{7,5},{8,10},{9,11},{10,... | collective-permute-start | bytes 331784 | tf_op jit(solution)/shard_map/ppermute | solution.py:406
  121.7 27.2 %collective-permute-start.48 = (bf16[96,576]{1,0:T(8,128)(2,1)S(1)}, bf16[96,576]{1,0:T(8,128)(2,1)S(1)}, u32[]{:S(2)}, u32[]{:S(2)}) collective-permute-start(bf16[96,576]{1,0:T(8,128)(2,1)S(1)} %constant_dynamic-slice_fusion.1.refs_0_), channel_id=1, source_target_pairs={{0,3},{1,0},{2,1},{3,2},{4,7},{5,4},{6,5},{7,6},{8,11},{9,8},{10,9... | collective-permute-start | bytes 331784 | tf_op jit(solution)/shard_map/ppermute | solution.py:406
  152.9 28.0 %collective-permute-start.49 = (bf16[4,96,576]{2,1,0:T(8,128)(2,1)}, bf16[4,96,576]{2,1,0:T(8,128)(2,1)}, u32[]{:S(2)}, u32[]{:S(2)}) collective-permute-start(bf16[4,96,576]{2,1,0:T(8,128)(2,1)} %stack_pieces.5.refs_5_), channel_id=1, source_target_pairs={{0,4},{4,0},{1,5},{5,1},{2,6},{6,2},{3,7},{7,3},{8,12},{12,8},{9,1... | collective-permute-start | bytes 1327112 | tf_op jit(solution)/shard_map/ppermute | solution.py:401
  153.1 28.4 %collective-permute-start.50 = (bf16[4,96,576]{2,1,0:T(8,128)(2,1)}, bf16[4,96,576]{2,1,0:T(8,128)(2,1)}, u32[]{:S(2)}, u32[]{:S(2)}) collective-permute-start(bf16[4,96,576]{2,1,0:T(8,128)(2,1)} %stack_pieces.5.refs_5_), channel_id=1, source_target_pairs={{0,16},{8,24},{16,0},{24,8},{1,17},{9,25},{17,1},{25,9},{2,18},{10... | collective-permute-start | bytes 1327112 | tf_op jit(solution)/shard_map/ppermute | solution.py:401
  154.1 51.4 %collective-permute-start.66 = (bf16[4,256,768]{2,1,0:T(8,128)(2,1)}, bf16[4,256,768]{2,1,0:T(8,128)(2,1)}, u32[]{:S(2)}, u32[]{:S(2)}) collective-permute-start(bf16[4,256,768]{2,1,0:T(8,128)(2,1)} %get-tuple-element.52.refs_3_), channel_id=1, source_target_pairs={{0,8},{8,0},{16,24},{24,16},{1,9},{9,1},{17,25},{25,17},{2,10},{10... | collective-permute-start | bytes 4718600 | tf_op jit(solution)/shard_map/ppermute | solution.py:401
  154.1 49.8 %collective-permute-start.67 = (bf16[4,256,768]{2,1,0:T(8,128)(2,1)}, bf16[4,256,768]{2,1,0:T(8,128)(2,1)}, u32[]{:S(2)}, u32[]{:S(2)}) collective-permute-start(bf16[4,256,768]{2,1,0:T(8,128)(2,1)} %get-tuple-element.69.refs_5_), channel_id=1, source_target_pairs={{0,8},{8,0},{16,24},{24,16},{1,9},{9,1},{17,25},{25,17},{2,10},{10... | collective-permute-start | bytes 4718600 | tf_op jit(solution)/shard_map/ppermute | solution.py:401
  200.4 21.5 %collective-permute-start.55 = (bf16[4,96,576]{2,1,0:T(8,128)(2,1)S(1)}, bf16[4,96,576]{2,1,0:T(8,128)(2,1)S(1)}, u32[]{:S(2)}, u32[]{:S(2)}) collective-permute-start(bf16[4,96,576]{2,1,0:T(8,128)(2,1)S(1)} %collective-permute-done.51.refs_8_), channel_id=1, source_target_pairs={{0,8},{8,0},{16,24},{24,16},{1,9},{9,1},{17,25},{25,17},{2,10},{10... | collective-permute-start | bytes 1327112 | tf_op jit(solution)/shard_map/ppermute | solution.py:401
  203.9 21.6 %collective-permute-start.42 = (bf16[256,576]{1,0:T(8,128)(2,1)}, bf16[256,576]{1,0:T(8,128)(2,1)S(1)}, u32[]{:S(2)}, u32[]{:S(2)}) collective-permute-start(bf16[256,576]{1,0:T(8,128)(2,1)} %get-tuple-element.62), channel_id=1, source_target_pairs={{0,0},{1,2},{2,4},{3,6},{4,1},{5,3},{6,5},{7,7},{8,8},{9,10},{10,1... | collective-permute-start | bytes 884744 | tf_op jit(solution)/shard_map/ppermute | solution.py:417
  215.4 32.0 %collective-permute-start.43 = (bf16[256,576]{1,0:T(8,128)(2,1)}, bf16[256,576]{1,0:T(8,128)(2,1)}, u32[]{:S(2)}, u32[]{:S(2)}) collective-permute-start(bf16[256,576]{1,0:T(8,128)(2,1)} %get-tuple-element.63), channel_id=1, source_target_pairs={{0,2},{1,0},{2,6},{3,4},{4,3},{5,1},{6,7},{7,5},{8,10},{9,8},{10,1... | collective-permute-start | bytes 884744 | tf_op jit(solution)/shard_map/ppermute | solution.py:417
  219.0 30.7 %collective-permute-start.44 = (bf16[256,576]{1,0:T(8,128)(2,1)}, bf16[256,576]{1,0:T(8,128)(2,1)}, u32[]{:S(2)}, u32[]{:S(2)}) collective-permute-start(bf16[256,576]{1,0:T(8,128)(2,1)} %get-tuple-element.64), channel_id=1, source_target_pairs={{0,4},{1,6},{2,0},{3,2},{4,5},{5,7},{6,1},{7,3},{8,12},{9,14},{10,... | collective-permute-start | bytes 884744 | tf_op jit(solution)/shard_map/ppermute | solution.py:417
  221.8 29.3 %collective-permute-start.45 = (bf16[256,576]{1,0:T(8,128)(2,1)}, bf16[256,576]{1,0:T(8,128)(2,1)S(1)}, u32[]{:S(2)}, u32[]{:S(2)}) collective-permute-start(bf16[256,576]{1,0:T(8,128)(2,1)} %get-tuple-element.65), channel_id=1, source_target_pairs={{0,6},{1,4},{2,2},{3,0},{4,7},{5,5},{6,3},{7,1},{8,14},{9,12},{10,... | collective-permute-start | bytes 884744 | tf_op jit(solution)/shard_map/ppermute | solution.py:417
  224.4 51.5 %collective-permute-start.73 = (bf16[4,96,1792]{2,1,0:T(8,128)(2,1)}, bf16[4,96,1792]{2,1,0:T(8,128)(2,1)}, u32[]{:S(2)}, u32[]{:S(2)}) collective-permute-start(bf16[4,96,1792]{2,1,0:T(8,128)(2,1)} %get-tuple-element.73), channel_id=1, source_target_pairs={{0,16},{8,24},{16,0},{24,8},{1,17},{9,25},{17,1},{25,9},{2,18},{10... | collective-permute-start | bytes 4128776 | tf_op jit(solution)/shard_map/ppermute | solution.py:401
  225.6 36.2 %collective-permute-start.63 = (bf16[208,576]{1,0:T(8,128)(2,1)S(1)}, bf16[208,576]{1,0:T(8,128)(2,1)S(1)}, u32[]{:S(2)}, u32[]{:S(2)}) collective-permute-start(bf16[208,576]{1,0:T(8,128)(2,1)S(1)} %fusion.16), channel_id=1, source_target_pairs={{0,16},{8,24},{16,0},{24,8},{1,17},{9,25},{17,1},{25,9},{2,18},{10... | collective-permute-start | bytes 718856 | tf_op jit(solution)/shard_map/ppermute | solution.py:401
  247.4 21.3 %collective-permute-start.32 = (bf16[256,768]{1,0:T(8,128)(2,1)}, bf16[256,768]{1,0:T(8,128)(2,1)}, u32[]{:S(2)}, u32[]{:S(2)}) collective-permute-start(bf16[256,768]{1,0:T(8,128)(2,1)} %get-tuple-element.54), channel_id=1, source_target_pairs={{0,1},{1,2},{2,3},{4,5},{5,6},{6,7},{8,9},{9,10},{10,11},{12,13},{... | collective-permute-start | bytes 1179656 | tf_op jit(solution)/shard_map/ppermute | solution.py:432
  249.6 20.4 %collective-permute-start.35 = (bf16[256,768]{1,0:T(8,128)(2,1)}, bf16[256,768]{1,0:T(8,128)(2,1)}, u32[]{:S(2)}, u32[]{:S(2)}) collective-permute-start(bf16[256,768]{1,0:T(8,128)(2,1)} %get-tuple-element.54), channel_id=1, source_target_pairs={{1,0},{2,1},{3,2},{5,4},{6,5},{7,6},{9,8},{10,9},{11,10},{13,12},{... | collective-permute-start | bytes 1179656 | tf_op jit(solution)/shard_map/ppermute | solution.py:433
  275.9 33.7 %collective-permute-start.72 = (bf16[4,96,1792]{2,1,0:T(8,128)(2,1)}, bf16[4,96,1792]{2,1,0:T(8,128)(2,1)S(1)}, u32[]{:S(2)}, u32[]{:S(2)}) collective-permute-start(bf16[4,96,1792]{2,1,0:T(8,128)(2,1)} %get-tuple-element.71), channel_id=1, source_target_pairs={{0,16},{8,24},{16,0},{24,8},{1,17},{9,25},{17,1},{25,9},{2,18},{10... | collective-permute-start | bytes 4128776 | tf_op jit(solution)/shard_map/ppermute | solution.py:401
  282.8 26.9 %collective-permute-start.74 = (bf16[4,96,1792]{2,1,0:T(8,128)(2,1)S(1)}, bf16[4,96,1792]{2,1,0:T(8,128)(2,1)S(1)}, u32[]{:S(2)}, u32[]{:S(2)}) collective-permute-start(bf16[4,96,1792]{2,1,0:T(8,128)(2,1)S(1)} %add_convert_fusion.1), channel_id=1, source_target_pairs={{0,4},{4,0},{1,5},{5,1},{2,6},{6,2},{3,7},{7,3},{8,12},{12,8},{9,1... | collective-permute-start | bytes 4128776 | tf_op jit(solution)/shard_map/ppermute | solution.py:401
  300.4 27.2 %collective-permute-start.61 = (bf16[256,768]{1,0:T(8,128)(2,1)S(1)}, bf16[256,768]{1,0:T(8,128)(2,1)S(1)}, u32[]{:S(2)}, u32[]{:S(2)}) collective-permute-start(bf16[256,768]{1,0:T(8,128)(2,1)S(1)} %collective-permute-done.60), channel_id=1, source_target_pairs={{1,0},{5,4},{9,8},{13,12},{17,16},{21,20},{25,24},{29,28}} | collective-permute-start | bytes 1179656 | tf_op jit(solution)/shard_map/ppermute | solution.py:433
  314.9 21.1 %collective-permute-start.77 = (bf16[96,1792]{1,0:T(8,128)(2,1)S(1)}, bf16[96,1792]{1,0:T(8,128)(2,1)S(1)}, u32[]{:S(2)}, u32[]{:S(2)}) collective-permute-start(bf16[96,1792]{1,0:T(8,128)(2,1)S(1)} %get-tuple-element.131), channel_id=1, source_target_pairs={{0,3},{1,0},{2,1},{3,2},{4,7},{5,4},{6,5},{7,6},{8,11},{9,8},{10,9... | collective-permute-start | bytes 1032200 | tf_op jit(solution)/shard_map/ppermute | solution.py:406
  (106 other events, 1252.2 us)

commit v2 on v1

--- a/solution.py
+++ b/solution.py
@@ -417,35 +417,10 @@
     return lax.ppermute(value, ("ctx", "tp"), pairs)
 
 
-def xor_ordered(stack, bits):
-    count = stack.shape[0]
-    order = lax.iota(jnp.int32, count) ^ bits
-    return jnp.take(stack, order, axis=0)
-
-
-def line_gathered(value):
-    z = lax.axis_index("tp")
-    up_pairs, down_pairs = [(0, 1), (1, 2), (2, 3)], [(1, 0), (2, 1), (3, 2)]
-    ups, downs = [], []
-    going_up, going_down = value, value
-    for step in range(3):
-        going_up = lax.ppermute(going_up, "tp", up_pairs[step:])
-        going_down = lax.ppermute(going_down, "tp", down_pairs[: 3 - step])
-        ups.append(going_up)
-        downs.append(going_down)
-    blocks = []
-    for block in range(4):
-        choices = [
-            value if place == block else (ups[place - block - 1] if place > block else downs[block - place - 1])
-            for place in range(4)
-        ]
-        blocks.append(lax.select_n(z, *choices))
-    return blocks
-
-
 ANY = pl.BlockSpec(memory_space=pl.ANY)
 WHOLE = pl.BlockSpec(memory_space=pltpu.VMEM)
 log2_e = math.log2(math.e)
+EXTRA = 8
 
 
 def low(value):
@@ -487,41 +462,35 @@
     )(*pieces)
 
 
-def spread_pack(own_half, x_first):
-    line = stacked([own_half] + [shifted(own_half, "tp", step) for step in (1, 2, 3)])
-    if x_first:
-        x_side = swapped(line, "ctx", 1)
-        y_side, xy_side = swapped(line, "fsdp", 2), swapped(x_side, "fsdp", 2)
-    else:
-        y_side = swapped(line, "fsdp", 2)
-        x_side, xy_side = swapped(line, "ctx", 1), swapped(y_side, "ctx", 1)
-    near = (line, x_side, y_side, xy_side)
-    return near + tuple(swapped(piece, "fsdp", 1) for piece in near)
-
-
-def piece_copies(meta, pieces, columns, target, sems, first):
+def line_stack(own_half):
+    far = swapped(own_half, "tp", 2)
+    return stacked([own_half, swapped(own_half, "tp", 1), far, swapped(far, "tp", 1)])
+
+
+def piece_copies(meta, pieces, taken, columns, target, sems, first):
     x, z, f = meta[0], meta[1], meta[2]
-    rows = pieces[0].shape[1]
     copies = []
-    for place, piece in enumerate(pieces):
+    parts = [(piece, step) for piece in pieces for step in range(piece.shape[0])]
+    for index, (piece, step) in enumerate(parts):
+        place, slot = index // 4, index % 4
         across = (place % 2, 2 * ((place // 2) % 2) + place // 4)
-        start = pl.multiple_of(((f ^ across[1]) * 2 + (x ^ across[0])) * rows, rows)
-        for step in range(4):
-            copies.append(
-                pltpu.make_async_copy(
-                    piece.at[step, :, columns],
-                    target.at[(z + 4 - step) & 3, pl.ds(start, rows), :],
-                    sems.at[first + len(copies)],
-                )
+        start = pl.multiple_of(((f ^ across[1]) * 2 + (x ^ across[0])) * taken, taken)
+        copies.append(
+            pltpu.make_async_copy(
+                piece.at[step, pl.ds(0, taken), columns],
+                target.at[z ^ slot, pl.ds(start, taken), :],
+                sems.at[first + len(copies)],
             )
+        )
     return copies
 
 
 def attend_kernel(
-    meta, own, other, w0, w1, w2, w3, bias, qkv, o0, o1, o2, o3, stats, weight, mask, *, block, heads
+    meta, own, other, w0, w1, w2, w3, bias, qkv, o0, o1, o2, o3, stats, weight, vectors,
+    mask, shards, *, block, heads
 ):
     step = pl.program_id(0)
-    shard = w0.shape[0]
+    shard = w0.shape[0] - EXTRA
     half = own.shape[1]
     scale = log2_e * HEAD_DIM ** (-0.5)
 
@@ -529,7 +498,15 @@
     def _():
         for place, piece in enumerate((w0, w1, w2, w3)):
             start = pl.multiple_of((meta[2] ^ place) * shard, shard)
-            weight[pl.ds(start, shard), :] = piece[...]
+            weight[pl.ds(start, shard), :] = piece[:shard, :]
+            shards[meta[2] ^ place] = piece[shard:, :]
+        vectors[6:8, :] = jnp.zeros((2, 4 * shard), jnp.float32)
+        for place in range(4):
+            for row in range(6):
+                first = row % 3 * shard
+                vectors[row : row + 1, place * shard : (place + 1) * shard] = wide(
+                    shards[place, row // 3 : row // 3 + 1, first : first + shard]
+                )
         for place, rows in enumerate((own, other)):
             source = rows[0] if place == 0 else rows[...]
             qkv[place * half : (place + 1) * half, :] = low(
@@ -585,22 +562,25 @@
                 whole((rows, columns)),
                 *[whole((block, columns // 3))] * 4,
                 pl.BlockSpec((1, 8, block), lambda step, meta: (step, 0, 0)),
+                whole((width, columns)),
+                whole((EXTRA, width)),
             ],
             scratch_shapes=[
-                pltpu.VMEM((width, columns), jnp.bfloat16),
                 pltpu.VMEM((rows, block), jnp.float32),
+                pltpu.VMEM((4, EXTRA, columns), jnp.bfloat16),
             ],
         ),
         out_shape=[struct((rows, columns))]
         + [struct((block, columns // 3))] * 4
-        + [struct((4, 8, block), jnp.float32)],
+        + [struct((4, 8, block), jnp.float32), struct((width, columns))]
+        + [struct((EXTRA, width), jnp.float32)],
         cost_estimate=cost(2 * rows * width * columns + 16 * rows * rows * columns, 8e6, rows * rows * 3),
         name="attend",
     )(meta, tokens, other, *pieces, bias)
 
 
 def attend_back_kernel(
-    meta, qkv, d0, d1, d2, d3, o0, o1, o2, o3, stats, full, p0, p1, p2, p3,
+    meta, qkv, d0, d1, d2, d3, o0, o1, o2, o3, stats, weight, full, p0, p1, p2, p3,
     grads, mask, grad_att, attended, *, block, heads
 ):
     step = pl.program_id(0)
@@ -660,11 +640,13 @@
             )
             full[:, base + 2 * HEAD_DIM : base + 3 * HEAD_DIM] = low(grads[2 * head + 1])
         for place, part in enumerate((p0, p1, p2, p3)):
-            part[...] = full[pl.ds(pl.multiple_of((meta[7] ^ place) * block, block), block), :]
-
-
-def attend_back_call(meta, qkv, grad_parts, parts, stats, heads):
+            span = pl.ds(pl.multiple_of((meta[7] ^ place) * block, block), block)
+            part[...] = low(dot32(full[span, :], weight[...], 1, 1))
+
+
+def attend_back_call(meta, qkv, grad_parts, parts, stats, weight, heads):
     rows, columns = qkv.shape
+    width = weight.shape[0]
     block = rows // 4
     whole = lambda shape: pl.BlockSpec(shape, lambda step, meta: (0,) * len(shape))
     small = whole((block, columns // 3))
@@ -675,8 +657,8 @@
             grid=(4,),
             in_specs=[whole((rows, columns))]
             + [small] * 8
-            + [pl.BlockSpec((1, 8, block), lambda step, meta: (step, 0, 0))],
-            out_specs=[whole((rows, columns))] + [whole((block, columns))] * 4,
+            + [pl.BlockSpec((1, 8, block), lambda step, meta: (step, 0, 0)), whole(weight.shape)],
+            out_specs=[whole((rows, columns))] + [whole((block, width))] * 4,
             scratch_shapes=[
                 pltpu.VMEM((2 * heads, rows, HEAD_DIM), jnp.float32),
                 pltpu.VMEM((rows, block), jnp.float32),
@@ -684,10 +666,10 @@
                 pltpu.VMEM((block, columns // 3), jnp.bfloat16),
             ],
         ),
-        out_shape=[struct((rows, columns))] + [struct((block, columns))] * 4,
+        out_shape=[struct((rows, columns))] + [struct((block, width))] * 4,
         cost_estimate=cost(40 * rows * rows * columns, 8e6, rows * rows * 3),
         name="attend_back",
-    )(meta, qkv, *grad_parts, *parts, stats)
+    )(meta, qkv, *grad_parts, *parts, stats, weight)
 
 
 def norm_parts(inputs):
@@ -711,14 +693,17 @@
 
 
 def first_kernel(meta, *refs, width):
-    att, tok, vectors, up_bias = refs[:4], refs[4], refs[5], refs[6]
-    pieces = refs[7:15]
-    hat, inverse, active, slope, out_w, up_w, sems = refs[15:]
+    att, tok, vectors, lines, pieces = refs[:4], refs[4], refs[5], refs[6], refs[7:15]
+    hat, inverse, both, slope, out_w, up_w, sems = refs[15:]
     hidden = up_w.shape[2]
-    copies = piece_copies(meta, pieces, pl.ds(hidden, out_w.shape[2]), out_w, sems, 0)
-    copies += piece_copies(meta, pieces, pl.ds(0, hidden), up_w, sems, 32)
+    taken = pieces[0].shape[1]
+    copies = piece_copies(meta, pieces, taken, pl.ds(hidden, out_w.shape[2]), out_w, sems, 0)
+    copies += piece_copies(meta, pieces, taken, pl.ds(0, hidden), up_w, sems, 32)
     for copy in copies:
         copy.start()
+    for step in range(4):
+        both[step, :, hidden : hidden + width] = att[step][...]
+        both[step, :, hidden + width :] = jnp.zeros_like(both[step, :, hidden + width :])
     for copy in copies:
         copy.wait()
     branch = vectors[BIAS_OUT : BIAS_OUT + 1, :]
@@ -729,25 +714,24 @@
     inverse[...] = inverse_one
     normed = low(hat_one * vectors[GAIN_ONE : GAIN_ONE + 1, :] + vectors[SHIFT_ONE : SHIFT_ONE + 1, :])
     for place in range(4):
-        inputs = dot32(normed, up_w[place], 1, 0) + up_bias[place : place + 1, :]
+        inputs = dot32(normed, up_w[place], 1, 0) + wide(lines[meta[1] ^ place, 0:1, :])
         cumulative = 0.5 * (1.0 + lax.erf(inputs * (0.5**0.5)))
         density = jnp.exp(-0.5 * inputs * inputs) * ((0.5 / math.pi) ** 0.5)
-        active[place] = low(inputs * cumulative)
+        both[place, :, :hidden] = low(inputs * cumulative)
         slope[place] = low(cumulative + inputs * density)
 
 
 def second_kernel(meta, *refs, width):
-    hat, inverse, active, slope, cot, vectors = refs[:6]
-    pieces_a, pieces_b = refs[6:14], refs[14:22]
-    outputs = refs[22:34]
-    output, resid, g0, g1, g2, g3, hidden_grad, keep, send, small, = outputs[:10]
-    out_w, up_w, down_w, blocks, sems = refs[32:]
-    model = hat.shape[1]
-    rows = hat.shape[0]
+    hat, inverse, both, slope, cot, vectors = refs[:6]
+    pieces_a, pieces_b = refs[6:14], refs[14:24]
+    output, resid, g0, g1, g2, g3, mixed, keep = refs[24:32]
+    out_w, up_w, down_w, blocks, small, small_blocks, sems = refs[32:]
+    rows, model = hat.shape
     hidden = up_w.shape[2]
-    down_copies = piece_copies(meta, pieces_b, pl.ds(0, hidden), down_w, sems, 0)
-    copies = piece_copies(meta, pieces_a, pl.ds(0, hidden), up_w, sems, 32)
-    copies += piece_copies(meta, pieces_a, pl.ds(hidden, out_w.shape[2]), out_w, sems, 64)
+    taken = pieces_a[0].shape[1]
+    down_copies = piece_copies(meta, pieces_b, taken, pl.ds(0, hidden), down_w, sems, 0)
+    copies = piece_copies(meta, pieces_a, taken, pl.ds(0, hidden), up_w, sems, 32)
+    copies += piece_copies(meta, pieces_a, taken, pl.ds(hidden, out_w.shape[2]), out_w, sems, 64)
     for copy in down_copies + copies:
         copy.start()
     row = lambda place: vectors[place : place + 1, :]
@@ -757,7 +741,7 @@
         copy.wait()
     second = row(BIAS_DOWN)
     for place in range(4):
-        second = second + dot32(active[place], down_w[place], 1, 1)
+        second = second + dot32(both[place, :, :hidden], down_w[place], 1, 1)
     hat_two, inverse_two = norm_parts(normed_one + second)
     output[...] = low(hat_two * row(GAIN_TWO) + row(SHIFT_TWO))
     position = meta[4] * rows + lax.broadcasted_iota(jnp.int32, (rows, model), 0)
@@ -770,9 +754,11 @@
     sums = lambda array: jnp.sum(array, axis=0, keepdims=True)
     for place in range(4):
         grad_hidden = low(dot32(grad_second, down_w[place], 1, 0) * wide(slope[place]))
-        hidden_grad[place] = grad_hidden
+        mixed[place, :rows, :] = grad_hidden
+        mixed[place, rows:, :] = low(
+            jnp.broadcast_to(sums(wide(grad_hidden)), (EXTRA, hidden))
+        )
         grad_normed = grad_normed + dot32(grad_hidden, up_w[place], 1, 1)
-        small[6 + place : 7 + place, :] = sums(wide(grad_hidden))
     grad_one = norm_back(grad_normed, hat_one, inverse_one, row(GAIN_ONE))
     resid[...] = grad_one
     grad_branch = low(grad_one)
@@ -784,64 +770,88 @@
     small[3:4, :] = sums(wide(grad_second))
     small[4:5, :] = sums(grad_output * hat_two)
     small[5:6, :] = sums(grad_output)
-    small[10:16, :] = jnp.zeros((6, model), jnp.float32)
+    small[6:8, :] = jnp.zeros((2, model), jnp.float32)
     shard = model // 4
+    for place in range(4):
+        small_blocks[place] = low(small[:, place * shard : (place + 1) * shard])
     for kind, array in enumerate((grad_second, low(normed_one), grad_branch)):
         for place in range(4):
             blocks[place] = array[:, place * shard : (place + 1) * shard]
         for far in range(2):
-            keep[kind, far] = blocks[meta[2] ^ (2 * far)]
-            send[kind, far] = blocks[meta[2] ^ (2 * far + 1)]
+            keep[kind, far, :rows, :] = blocks[meta[2] ^ (2 * far)]
+            keep[kind, far, rows:, :] = small_blocks[meta[2] ^ (2 * far)]
+            columns = slice(kind * shard, (kind + 1) * shard)
+            mixed[4 + far, :rows, columns] = blocks[meta[2] ^ (2 * far + 1)]
+            mixed[4 + far, rows:, columns] = small_blocks[meta[2] ^ (2 * far + 1)]
+    for far in range(2):
+        mixed[4 + far, :, 3 * shard :] = jnp.zeros((rows + EXTRA, hidden - 3 * shard), jnp.bfloat16)
 
 
 def weights_kernel(meta, *refs, width):
-    keep, got = refs[0], refs[1]
-    active, active_sib, grad, grad_sib = refs[2:6]
-    att, att_sib = refs[6:10], refs[10:14]
-    near_mine, near_theirs, far_mine, far_theirs = refs[14:18]
-    turned, whole = refs[18:]
+    keep, both, both_sib, mixed, mixed_sib = refs[:5]
+    near_up, far_up, mine_down, theirs_down, turned, whole = refs[5:]
     shard = keep.shape[3]
-    rows = keep.shape[2]
+    rows = both.shape[1]
     half = shard // 2
-    hidden = active.shape[2]
-    mine = pl.multiple_of(meta[0] * half, half)
-    theirs = pl.multiple_of((1 - meta[0]) * half, half)
-
-    def store(value, target, first):
-        columns = value.shape[1]
-        whole[:, :columns] = value
-        for far, pair in enumerate(((near_mine, near_theirs), (far_mine, far_theirs))):
-            for start, out in zip((mine, theirs), pair):
-                out[target, :, first : first + columns] = low(
-                    whole[pl.ds(far * shard + start, half), :columns]
-                )
-
-    for kind, (own, sib, first) in enumerate(
-        ((active, active_sib, hidden), (grad, grad_sib, 0), (att, att_sib, 2 * hidden))
-    ):
+    hidden = mixed.shape[2]
+    padded = both.shape[2] - hidden
+    starts = [pl.multiple_of(side * half, half) for side in (meta[0], 1 - meta[0])]
+
+    def slot(block):
+        apart = block ^ meta[1]
+        return 2 * (apart & 1) + (apart >> 1)
+
+    for kind in range(3):
         for far in range(2):
             span = slice(far * shard, (far + 1) * shard)
-            turned[span, :rows] = keep[kind, far].T
-            turned[span, rows:] = got[kind, far].T
+            turned[span, :rows] = keep[kind, far, :rows, :].T
+            turned[span, rows:] = mixed_sib[4 + far, :rows, kind * shard : (kind + 1) * shard].T
         for place in range(4):
-            left = own[place][...] if kind == 2 else own[place]
-            right = sib[place][...] if kind == 2 else sib[place]
+            if kind == 1:
+                left, right = mixed[place, :rows, :], mixed_sib[place, :rows, :]
+            else:
+                columns = slice(0, hidden) if kind == 0 else slice(hidden, None)
+                left, right = both[place, :, columns], both_sib[place, :, columns]
             value = dot32(turned[:, :rows], left, 1, 0) + dot32(turned[:, rows:], right, 1, 0)
-            store(value, (meta[4] ^ place) if kind == 2 else place, first)
-
-
-def tokens_kernel(meta, *refs):
-    resid, parts, pieces = refs[0], refs[1:5], refs[5:13]
-    out, weight, sems = refs[13:]
-    copies = piece_copies(meta, pieces, pl.ds(0, weight.shape[2]), weight, sems, 0)
-    for copy in copies:
-        copy.start()
-    total = resid[...]
-    for copy in copies:
-        copy.wait()
-    for step in range(4):
-        total = total + dot32(parts[step][...], weight[meta[4] ^ step], 1, 1)
-    out[...] = low(total)
+            target = slot(meta[4] ^ place if kind == 2 else place)
+            count = value.shape[1]
+            whole[:, :count] = value
+            for far in range(2):
+                for side, start in enumerate(starts):
+                    part = low(whole[pl.ds(far * shard + start, half), :count])
+                    if kind == 0:
+                        kept = mine_down.shape[3]
+                        (mine_down, theirs_down)[side][far, target, :half, :] = part[:, :kept]
+                        (near_up, far_up)[far][side, target, :half, hidden + padded :] = part[:, kept:]
+                    elif kind == 1:
+                        (near_up, far_up)[far][side, target, :half, :hidden] = part
+                    else:
+                        (near_up, far_up)[far][side, target, :half, hidden : hidden + padded] = part
+    for far in range(2):
+        vector_sums = low(wide(keep[0, far, rows:, :]) + wide(mixed_sib[4 + far, rows:, :shard]))
+        for place in range(4):
+            hidden_sums = low(wide(mixed[place, rows:, :]) + wide(mixed_sib[place, rows:, :]))
+            for side in range(2):
+                out = (mine_down, theirs_down)[side]
+                out[far, place, half:, :] = jnp.zeros((EXTRA, out.shape[3]), jnp.bfloat16)
+                out = (near_up, far_up)[far]
+                out[side, slot(place), half:, :hidden] = hidden_sums
+                out[side, place, half:, hidden : hidden + shard] = vector_sums
+                rest = slice(hidden + shard, None)
+                out[side, place, half:, rest] = jnp.zeros_like(out[side, place, half:, rest])
+
+
+def projections_kernel(meta, own, other, grads, kept, sent, whole):
+    half, shard = other.shape[0], other.shape[1] // 4
+    count = grads.shape[1]
+    whole[...] = dot32(own[0], grads[:half, :], 0, 0) + dot32(other[...], grads[half:, :], 0, 0)
+    sums = jnp.broadcast_to(jnp.sum(wide(grads[...]), axis=0, keepdims=True), (EXTRA, count))
+    for far in range(2):
+        for out, place in ((kept, meta[2] ^ (2 * far)), (sent, meta[2] ^ (2 * far + 1))):
+            value = whole[pl.ds(pl.multiple_of(place * shard, shard), shard), :]
+            out[far, :shard, :count] = value.astype(out.dtype)
+            out[far, shard:, :count] = sums.astype(out.dtype)
+            out[far, :, count:] = jnp.zeros_like(out[far, :, count:])
 
 
 def per_device_rows(
@@ -876,12 +886,24 @@
     own_seq, own_place = z % 2, z // 2
     quarter = 2 * x + own_place
     length_of = lambda place: lax.dynamic_index_in_dim(lengths, place, 0, keepdims=False)
-    meta = jnp.stack(
-        [x, z, f, length_of(x), quarter, own_seq, own_place, z ^ (2 * x), length_of(own_seq)]
-    ).astype(jnp.int32)
-    smem = pl.BlockSpec(memory_space=pltpu.SMEM)
-
-    other = swapped(lax.dynamic_index_in_dim(tokens, 1 - x, 0, keepdims=False), "ctx", 1)
+    entries = (x, z, f, length_of(x), quarter, own_seq, own_place, z ^ (2 * x), length_of(own_seq))
+    places = lax.iota(jnp.int32, len(entries))
+    meta = sum(jnp.where(places == place, entry, 0) for place, entry in enumerate(entries))
+    meta = meta.astype(jnp.int32)
+    tied = lambda *values: lax.optimization_barrier(values)
+
+    take_half = lambda pack: lax.dynamic_slice_in_dim(pack, x * half, half, 0)
+    wider = lambda array, columns: jnp.pad(array, ((0, 0), (0, columns - array.shape[1])))
+    columns_a = hidden + padded
+    half_a = wider(take_half(jnp.concatenate([w_up, w_out.T], axis=1)), columns_a)
+    half_b = jnp.concatenate(
+        [take_half(w_down.T), b_up[None], jnp.zeros((EXTRA - 1, hidden), jnp.bfloat16)]
+    )
+
+    other = lax.dynamic_index_in_dim(tokens, 1 - x, 0, keepdims=False)
+    other, half_a = tied(other, half_a)
+    other = swapped(other, "ctx", 1)
+    line_a = line_stack(half_a)
     per_head = lambda weights: jnp.concatenate(
         [
             weight[..., head * HEAD_DIM : (head + 1) * HEAD_DIM]
@@ -890,33 +912,40 @@
         ],
         axis=-1,
     )
-    qkv_shard = per_head((w_query, w_key, w_value))
+    vectors = jnp.concatenate([b_out, ln1_gain, ln1_shift, b_down, ln2_gain, ln2_shift])
+    qkv_shard = jnp.concatenate(
+        [
+            per_head((w_query, w_key, w_value)),
+            jnp.pad(vectors.reshape(2, 3 * width), ((0, EXTRA - 2), (0, 0))),
+        ]
+    )
     qkv_bias = wide(per_head((b_query, jnp.zeros_like(b_query), b_value)))[None, :]
     qkv_y = swapped(qkv_shard, "fsdp", 2)
     qkv_pieces = (qkv_shard, swapped(qkv_shard, "fsdp", 1), qkv_y, swapped(qkv_y, "fsdp", 1))
 
-    vectors = jnp.stack([b_out, ln1_gain, ln1_shift, b_down, ln2_gain, ln2_shift])
-    pair = jnp.stack([vectors, swapped(vectors, "fsdp", 1)])
-    gathered = jnp.concatenate([pair, swapped(pair, "fsdp", 2)])
-    vectors = wide(xor_ordered(gathered, f).transpose(1, 0, 2).reshape(6, model))
-    up_near = jnp.stack([b_up, swapped(b_up, "tp", 1)])
-    up_bias = wide(xor_ordered(jnp.concatenate([up_near, swapped(up_near, "tp", 2)]), z))
-
-    take_half = lambda pack: lax.dynamic_slice_in_dim(pack, x * half, half, 0)
-    pack_a = jnp.concatenate(
-        [w_up, w_out.T, jnp.zeros((shard, padded - width), jnp.bfloat16)], axis=1
-    )
-    pieces_a = spread_pack(take_half(pack_a), True)
-    pieces_b = spread_pack(take_half(w_down.T), False)
-    pieces_c = spread_pack(take_half(qkv_shard), True)
-
-    qkv, *parts, stats = attend_call(meta, tokens, other, qkv_pieces, qkv_bias, heads)
+    core = lambda array: swapped(array, "fsdp", 1)
+    meta, qkv_bias, other, line_a, half_b, *qkv_pieces = tied(
+        meta, qkv_bias, other, line_a, half_b, *qkv_pieces
+    )
+    x_a, y_a = swapped(line_a, "ctx", 1), swapped(line_a, "fsdp", 2)
+    qkv, *parts, stats, weight, vectors = attend_call(
+        meta, tokens, other, qkv_pieces, qkv_bias, heads
+    )
+    b_pieces = [swapped(half_b, "tp", bit) for bit in (1, 2, 3)]
+
+    x_a, y_a, line_a, *rest = tied(x_a, y_a, line_a, *b_pieces, *parts)
+    b_pieces, parts = rest[:3], rest[3:]
+    line_b = stacked([half_b, *b_pieces])
     att = [to_owner(part, step) for step, part in enumerate(parts)]
+    x_y_a = swapped(x_a, "fsdp", 2)
+    x_y_a, x_a, y_a, line_a, *att = tied(x_y_a, x_a, y_a, line_a, *att)
+    near_a = (line_a, x_a, y_a, x_y_a)
+    pieces_a = (*near_a, *map(core, near_a))
+    x_b, y_b = swapped(line_b, "ctx", 1), swapped(line_b, "fsdp", 2)
 
     def row_spec(array):
         return pl.BlockSpec((1, rows, model), lambda step, meta: (meta[5], meta[6], 0))
 
-    one = lambda *refs: refs
     vm = lambda shape, dtype=jnp.bfloat16: pltpu.VMEM(shape, dtype)
     weights_scratch = [vm((4, model, padded)), vm((4, model, hidden))]
     grid = lambda inputs, outputs, scratch: pltpu.PrefetchScalarGridSpec(
@@ -928,14 +957,15 @@
     first_out = [
         struct((rows, model), jnp.float32),
         struct((rows, 1), jnp.float32),
-        struct((4, rows, hidden)),
+        struct((4, rows, columns_a)),
         struct((4, rows, hidden)),
     ]
-    hat, inverse, active, slope = pl.pallas_call(
+    hat, inverse, both, slope = pl.pallas_call(
         lambda *refs: first_kernel(*refs, width=width),
         grid_spec=grid(
             [full((rows, width))] * 4
-            + [row_spec(tokens), full((6, model)), full((4, hidden))]
+            + [row_spec(tokens), full((EXTRA, model))]
+            + [pl.BlockSpec((4, EXTRA, hidden), lambda step, meta: (0, half // EXTRA, 0))]
             + [ANY] * 8,
             specs(first_out),
             weights_scratch + [pltpu.SemaphoreType.DMA((64,))],
@@ -943,93 +973,128 @@
         out_shape=first_out,
         cost_estimate=cost(2 * rows * model * (model + 4 * hidden), 12e6, rows * hidden * 8),
         name="feed_first",
-    )(meta, *att, tokens, vectors, up_bias, *pieces_a)
+    )(meta, *att, tokens, vectors, line_b, *pieces_a)
+
+    both, x_b, y_b, line_b = tied(both, x_b, y_b, line_b)
+    x_y_b = [swapped(x_b[:2], "fsdp", 2), swapped(y_b[2:], "ctx", 1)]
+    cores_b = [core(line_b), core(x_b), core(y_b)]
+    rest = tied(*x_y_b, *cores_b)
+    x_y_b, cores_b = rest[:2], rest[2:]
+    both_sib = core(both)
+    pieces_b = (line_b, x_b, y_b, *x_y_b, *cores_b, *map(core, x_y_b))
 
     second_out = [
         struct((rows, model)),
         struct((rows, model), jnp.float32),
         *[struct((rows, width))] * 4,
-        struct((4, rows, hidden)),
-        struct((3, 2, rows, shard)),
-        struct((3, 2, rows, shard)),
-        struct((16, model), jnp.float32),
+        struct((6, rows + EXTRA, hidden)),
+        struct((3, 2, rows + EXTRA, shard)),
     ]
-    output, resid, g0, g1, g2, g3, hidden_grad, keep, send, small = pl.pallas_call(
+    output, resid, g0, g1, g2, g3, mixed, keep = pl.pallas_call(
         lambda *refs: second_kernel(*refs, width=width),
         grid_spec=grid(
-            specs(first_out) + [row_spec(cotangent), full((6, model))] + [ANY] * 16,
+            [full(item.shape) for item in (hat, inverse, both, slope)]
+            + [row_spec(cotangent), full((EXTRA, model))]
+            + [ANY] * 18,
             specs(second_out),
             weights_scratch
-            + [vm((4, model, hidden)), vm((4, rows, shard)), pltpu.SemaphoreType.DMA((96,))],
+            + [
+                vm((4, model, hidden)),
+                vm((4, rows, shard)),
+                vm((EXTRA, model), jnp.float32),
+                vm((4, EXTRA, shard)),
+                pltpu.SemaphoreType.DMA((96,)),
+            ],
         ),
         out_shape=second_out,
         cost_estimate=cost(2 * rows * model * (model + 12 * hidden), 20e6),
         name="feed_second",
-    )(meta, hat, inverse, active, slope, cotangent, vectors, *pieces_a, *pieces_b)
+    )(meta, hat, inverse, both, slope, cotangent, vectors, *pieces_a, *pieces_b)
 
     grad_att = [to_owner(part, step, True) for step, part in enumerate((g0, g1, g2, g3))]
 
-    core = lambda array: swapped(array, "fsdp", 1)
-    half_pack = struct((4, half, 2 * hidden + padded))
-    near_mine, near_theirs, far_mine, far_theirs = pl.pallas_call(
+    first_x = 2 * padded
+    pack = struct((2, 4, half + EXTRA, first_x))
+    pack_up = struct((2, 4, half + EXTRA, columns_a + hidden - first_x))
+    mixed_sib = core(mixed)
+    near_up, far_up, mine_down, theirs_down = pl.pallas_call(
         lambda *refs: weights_kernel(*refs, width=width),
         grid_spec=grid(
-            [full(keep.shape)] * 2 + [full(active.shape)] * 4 + [full((rows, width))] * 8,
-            specs([half_pack] * 4),
+            specs([keep, both, both_sib, mixed, mixed_sib]),
+            specs([pack_up] * 2 + [pack] * 2),
             [vm((2 * shard, 2 * rows)), vm((2 * shard, hidden), jnp.float32)],
         ),
-        out_shape=[half_pack] * 4,
+        out_shape=[pack_up] * 2 + [pack] * 2,
         cost_estimate=cost(8 * rows * shard * (8 * hidden + 4 * width), 20e6),
         name="feed_weights",
-    )(meta, keep, core(send), active, core(active), hidden_grad, core(hidden_grad), *att, *map(core, att))
-
-    grad_full, *grad_parts = attend_back_call(meta, qkv, grad_att, parts, stats, heads)
+    )(meta, keep, both, both_sib, mixed, mixed_sib)
+
+    far_up, theirs_down, *grad_att = tied(far_up, theirs_down, *grad_att)
+    got_up, got_down = swapped(far_up, "fsdp", 2), swapped(theirs_down, "ctx", 1)
+    far_z, near_z = swapped(output, "tp", 2), swapped(output, "tp", 1)
+    grad_full, *grad_parts = attend_back_call(meta, qkv, grad_att, parts, stats, weight, heads)
+
+    got_down, near_z, far_z, *grad_parts = tied(got_down, near_z, far_z, *grad_parts)
     grad_rows = [to_owner(part, step) for step, part in enumerate(grad_parts)]
-    token_rows = pl.pallas_call(
-        tokens_kernel,
+    got_down, grad_full, grad_rows[0] = tied(got_down, grad_full, grad_rows[0])
+    kept, sent = pl.pallas_call(
+        projections_kernel,
         grid_spec=grid(
-            [full((rows, model))] + [full((rows, 3 * width))] * 4 + [ANY] * 8,
-            full((rows, model)),
-            [vm((4, model, 3 * width)), pltpu.SemaphoreType.DMA((32,))],
+            [pl.BlockSpec((1, local_rows, model), lambda step, meta: (meta[0], 0, 0))]
+            + [full((local_rows, model)), full(grad_full.shape)],
+            [full((2, shard + EXTRA, 640 * width // 192))] * 2,
+            [vm((model, 3 * width), jnp.float32)],
         ),
-        out_shape=struct((rows, model)),
-        cost_estimate=cost(24 * rows * model * width, 8e6),
-        name="token_grads",
-    )(meta, resid, *grad_rows, *pieces_c)
-
-    def spread_rows(block, dtype):
-        blocks = [item.astype(dtype) for item in line_gathered(block)]
+        out_shape=[
+            struct((2, shard + EXTRA, 640 * width // 192), dtype) for dtype in (jnp.float32, jnp.bfloat16)
+        ],
+        cost_estimate=cost(12 * local_rows * model * width, 8e6),
+        name="projection_weights",
+    )(meta, tokens, other, grad_full)
+    second_down = swapped(low(wide(mine_down[1]) + wide(got_down[1])), "fsdp", 2)
+    got_up, second_down, kept, sent, far_z, *grad_rows = tied(
+        got_up, second_down, kept, sent, far_z, *grad_rows
+    )
+    second_up = swapped(low(wide(near_up[1]) + wide(got_up[1])), "ctx", 1)
+    token_rows = resid
+    for part in grad_rows:
+        token_rows = token_rows + wide(part)
+
+    def spread_rows(pieces, dtype):
+        blocks = [
+            lax.select_n(z, *[pieces[block ^ place] for place in range(4)]).astype(dtype)
+            for block in range(4)
+        ]
         return jnp.stack([jnp.concatenate([blocks[seq], blocks[2 + seq]]) for seq in range(2)])
 
-    output_full = spread_rows(output, jnp.bfloat16)
-    grad_tokens = spread_rows(token_rows, jnp.float32)
-
-    theirs = low(wide(near_theirs) + wide(swapped(far_theirs, "fsdp", 2)))
-    mine = wide(near_mine) + wide(swapped(far_mine, "fsdp", 2))
-    mine = low(mine + wide(swapped(theirs, "ctx", 1)))
-    total = wide(lax.dynamic_index_in_dim(mine, z, 0, keepdims=False))
-    for step in (1, 2, 3):
-        piece = lax.dynamic_index_in_dim(mine, (z + step) % 4, 0, keepdims=False)
-        total = total + wide(shifted(piece, "tp", step))
-    total = low(total)
+    token_rows = low(token_rows)
+    up_lines = wide(near_up[0]) + wide(got_up[0]) + wide(second_up)
+    down_lines = wide(mine_down[0]) + wide(got_down[0]) + wide(second_down)
+    lines = jnp.concatenate([up_lines, down_lines], axis=2)
+    lines, line_sent = lines[:2], low(lines[2:])
+    lines = lines + wide(swapped(line_sent, "tp", 1))
+    output_full = spread_rows([output, near_z, far_z, swapped(far_z, "tp", 1)], jnp.bfloat16)
+    far_z, near_z = swapped(token_rows, "tp", 2), swapped(token_rows, "tp", 1)
+    grad_tokens = spread_rows([token_rows, near_z, far_z, swapped(far_z, "tp", 1)], jnp.float32)
+    total = low(lines[0] + wide(swapped(low(lines[1]), "tp", 2)))
     other_half = swapped(total, "ctx", 1)
-    total = wide(jnp.concatenate([jnp.where(x == 0, total, other_half), jnp.where(x == 0, other_half, total)]))
+    small = wide(total[half:])
+    total = wide(
+        jnp.concatenate(
+            [
+                jnp.where(x == 0, total[:half], other_half[:half]),
+                jnp.where(x == 0, other_half[:half], total[:half]),
+            ]
+        )
+    )
     grad_w_up = total[:, :hidden]
-    grad_w_down = total[:, hidden : 2 * hidden].T
-    grad_w_out = total[:, 2 * hidden : 2 * hidden + width].T
-
-    own_half = lax.dynamic_index_in_dim(tokens, x, 0, keepdims=False)
-    grad_w_qkv = dot32(own_half, grad_full[:local_rows], 0, 0) + dot32(other, grad_full[local_rows:], 0, 0)
-    grad_w_qkv = jnp.concatenate(
-        [
-            grad_w_qkv.reshape(4, shard, 3 * width),
-            jnp.broadcast_to(jnp.sum(wide(grad_full), axis=0), (4, 16, 3 * width)),
-        ],
-        axis=1,
-    )
-    at = lambda array, place: lax.dynamic_index_in_dim(array, place, 0, keepdims=False)
-    sent = low(jnp.stack([at(grad_w_qkv, f ^ 1), at(grad_w_qkv, f ^ 3)]))
-    kept = jnp.stack([at(grad_w_qkv, f), at(grad_w_qkv, f ^ 2)]) + wide(swapped(sent, "fsdp", 1))
+    tail = slice(columns_a, columns_a + hidden - first_x)
+    grad_w_down = jnp.concatenate([total[:, tail.stop :], total[:, tail]], axis=1).T
+    grad_w_out = total[:, hidden : hidden + width].T
+    grad_b_up = small[0, :hidden]
+    small_own = small[:, hidden : hidden + shard]
+
+    kept = kept + wide(core(sent))
     kept = low(kept[0] + wide(swapped(low(kept[1]), "fsdp", 2)))
     kept = wide(kept) + wide(swapped(kept, "ctx", 1))
 
@@ -1044,11 +1109,6 @@
 
     grad_w_query, grad_w_key, grad_w_value = (unpack(kept[:shard], part) for part in range(3))
     grad_b_query, grad_b_value = (unpack(kept[shard : shard + 1], part)[0] for part in (0, 2))
-
-    for axis, bit in (("fsdp", 1), ("fsdp", 2), ("ctx", 1), ("tp", 1), ("tp", 2)):
-        small = small + swapped(small, axis, bit)
-    small_own = lax.dynamic_slice_in_dim(small[:6], f * shard, shard, 1)
-    grad_b_up = lax.dynamic_index_in_dim(small, 6 + z, 0, keepdims=False)
     return (
         output_full,
         grad_tokens,

time: 352 us -> 325 us (0.923); the launches traced: 346 us -> 324 us
  local copies, waits for them, and re-layouts: 26.1 us -> 13.8 us
  matrix products: 3.83 us -> 0 us
    ppermute x24 -> x0, waiting for transfers between devices: 45.9 us -> none  [the longest x6 27.3 us: line_gathered(): going_down = lax.ppermute(going_down, 'tp', down_pairs[:3 - step])]
    ppermute x48 -> x44, waiting for transfers between devices: 32.3 us -> 74.8 us  [swapped(): lax.ppermute(value, axis, [(place, place ^ bit) for place in range(count)])]
    ppermute x24 -> x0, starting transfers between devices: 41.6 us -> none  [the longest x12 24.3 us: shifted(): lax.ppermute(value, axis, [(place, (place + steps) % count) for place in...]
    ppermute x48 -> x44, starting transfers between devices: 30 us -> 66.9 us  [swapped(): lax.ppermute(value, axis, [(place, place ^ bit) for place in range(count)])]
    ppermute x12, starting transfers between devices: 31.9 us -> 36.6 us  [to_owner(): return lax.ppermute(value, ('ctx', 'tp'), pairs)]
    dot_general x2 -> x0, matrix products: 3.83 us -> none  [dot32(): lax.dot_general(left, right, (((left_dim,), (right_dim,)), ((), ())), pre...]
  transfers between devices with their start and end apart: 84 -> 56, of which waited for: 25 -> 17; matrix products, arithmetic and copies ran while one was open for 12% -> 6% of each run, Pallas kernels for 22% -> 19%
where the time goes in v2:
time: 325 us; the launch traced here: 324 us
  waiting for transfers between devices  109 us (34%)
  starting transfers between devices  103 us (32%)
  Pallas kernels  77.2 us (24%)
  other arithmetic  19.4 us (6%)
  local copies, waits for them, and re-layouts  13.8 us (4%)
    ppermute x44, waiting for transfers between devices, swapped(): lax.ppermute(value, axis, [(place, place ^ bit) for place in range(count)])  74.8 us
    ppermute x44, starting transfers between devices, swapped(): lax.ppermute(value, axis, [(place, place ^ bit) for place in range(count)])  66.9 us
    ppermute x12, starting transfers between devices, to_owner(): return lax.ppermute(value, ('ctx', 'tp'), pairs)  36.6 us
    ppermute x12, waiting for transfers between devices, to_owner(): return lax.ppermute(value, ('ctx', 'tp'), pairs)  33.7 us
    pallas_call x1, Pallas kernels, attend_back_call(): pl.pallas_call(lambda *refs: attend_back_kernel(*refs, block=block, heads...  17.2 us
    pallas_call x1, Pallas kernels, per_device_rows(): pl.pallas_call(lambda *refs: second_kernel(*refs, width=width), grid_spec...  14.9 us
    pallas_call x1, Pallas kernels, attend_call(): pl.pallas_call(lambda *refs: attend_kernel(*refs, block=block, heads=head...  14.8 us
    pallas_call x1, Pallas kernels, per_device_rows(): pl.pallas_call(lambda *refs: first_kernel(*refs, width=width), grid_spec=...  10.7 us
  transfers between devices with their start and end apart: 56, of which 17 were waited for; matrix products, arithmetic and copies ran while one was open for 6% of the time, Pallas kernels for 19%

profile of v2, /device:TPU:0, one launch (start us, length us, event | category | flops | bytes accessed | tf_op | source)
XLA Modules:
  0.0 323.9 jit_solution(7854943642880066992)
XLA Ops:
  4.2 4.1 %collective-permute-start.2 = (bf16[96,1024]{1,0:T(8,128)(2,1)S(1)}, bf16[96,1024]{1,0:T(8,128)(2,1)S(1)}, u32[]{:S(2)}, u32[]{:S(2)}) collective-permute-start(bf16[96,1024]{1,0:T(8,128)(2,1)S(1)} %pad.8.refs_0_), channel_id=1, source_target_pairs={{0,2},{1,3},{2,0},{3,1},{4,6},{5,7},{6,4},{7,5},{8,10},{9,11},{10,... | collective-permute-start | bytes 589832 | tf_op jit(solution)/shard_map/ppermute | solution.py:401
  14.4 5.0 %collective-permute-done.5.refs_5_ = bf16[200,576]{1,0:T(8,128)(2,1)} collective-permute-done((bf16[200,576]{1,0:T(8,128)(2,1)S(1)}, bf16[200,576]{1,0:T(8,128)(2,1)}, u32[]{:S(2)}, u32[]{:S(2)}) %collective-permute-start.5) | collective-permute-done | bytes 230432 | tf_op jit(solution)/shard_map/ppermute | solution.py:401
  22.6 6.7 %collective-permute-done.3.refs_3_ = bf16[96,1024]{1,0:T(8,128)(2,1)S(1)} collective-permute-done((bf16[96,1024]{1,0:T(8,128)(2,1)S(1)}, bf16[96,1024]{1,0:T(8,128)(2,1)S(1)}, u32[]{:S(2)}, u32[]{:S(2)}) %collective-permute-start.3) | collective-permute-done | bytes 196640 | tf_op jit(solution)/shard_map/ppermute | solution.py:401
  30.0 2.2 stack_pieces.2.refs_8_.refs_7_
  34.6 2.5 collective-permute-start.11
  37.8 14.8 %attend.1 = (bf16[1024,576]{1,0:T(8,128)(2,1)}, bf16[256,192]{1,0:T(8,128)(2,1)}, bf16[256,192]{1,0:T(8,128)(2,1)}, bf16[256,192]{1,0:T(8,128)(2,1)}, bf16[256,1...) custom-call(s32[9]{0:T(128)} %fusion.21.refs_0_.meta, ...), custom_call_target="tpu_custom_call" | custom-call | flops 10569646080 | bytes 8000000 | tf_op jit(solution)/shard_map/attend/pallas_call | solution.py:550
  54.9 4.3 %collective-permute-start.14 = (bf16[256,192]{1,0:T(8,128)(2,1)}, bf16[256,192]{1,0:T(8,128)(2,1)S(1)}, u32[]{:S(2)}, u32[]{:S(2)}) collective-permute-start(bf16[256,192]{1,0:T(8,128)(2,1)} %get-tuple-element.130.refs_7_), channel_id=1, source_target_pairs={{0,2},{1,0},{2,6},{3,4},{4,3},{5,1},{6,7},{7,5},{8,10},{9,8},{10,1... | collective-permute-start | bytes 294920 | tf_op jit(solution)/shard_map/ppermute | solution.py:417
  62.5 9.3 %collective-permute-done.14.refs_2_ = bf16[256,192]{1,0:T(8,128)(2,1)S(1)} collective-permute-done((bf16[256,192]{1,0:T(8,128)(2,1)}, bf16[256,192]{1,0:T(8,128)(2,1)S(1)}, u32[]{:S(2)}, u32[]{:S(2)}) %collective-permute-start.14) | collective-permute-done | bytes 98336 | tf_op jit(solution)/shard_map/ppermute | solution.py:417
  75.0 3.1 collective-permute-start.21
  79.4 10.7 %feed_first.1 = (f32[256,768]{1,0:T(8,128)}, f32[256,1]{1,0:T(8,128)}, bf16[4,256,1024]{2,1,0:T(8,128)(2,1)}, bf16[4,256,768]{2,1,0:T(8,128)(2,1)}) custom-call(s32[9]{0:T(128)} %fusion.21.refs_0_.meta, bf16[256,192]{1,0:T(8,128)(2,1)} %copy-done.28, bf16[256,192]{1,0:T(8,128)(2,1)} %copy-done.29, bf16[256,192]{1,0:T(8,128)(2,1)} %copy-done.30, ...), custom_call_target="tpu_custom_call" | custom-call | flops 1509949440 | bytes 12000000 | tf_op jit(solution)/shard_map/feed_first/pallas_call | solution.py:963
  90.1 3.0 collective-permute-done.21.refs_16_
  98.7 8.4 %collective-permute-done.23.refs_18_ = bf16[2,104,768]{2,1,0:T(8,128)(2,1)S(1)} collective-permute-done((bf16[2,104,768]{2,1,0:T(8,128)(2,1)S(1)}, bf16[2,104,768]{2,1,0:T(8,128)(2,1)S(1)}, u32[]{:S(2)}, u32[]{:S(2)}) %collective-permute-start.23) | collective-permute-done | bytes 319520 | tf_op jit(solution)/shard_map/ppermute | solution.py:401
  110.9 14.9 %feed_second.1 = (bf16[256,768]{1,0:T(8,128)(2,1)}, f32[256,768]{1,0:T(8,128)}, bf16[256,192]{1,0:T(8,128)(2,1)}, bf16[256,192]{1,0:T(8,128)(2,1)}, bf16[256,192...) custom-call(s32[9]{0:T(128)} %fusion.21.refs_0_.meta, ...), custom_call_target="tpu_custom_call" | custom-call | flops 3925868544 | bytes 20000000 | tf_op jit(solution)/shard_map/feed_second/pallas_call | solution.py:993
  127.9 2.2 collective-permute-start.33
  130.9 2.9 collective-permute-done.30.refs_3_
  135.0 3.6 %collective-permute-start.35 = (bf16[256,192]{1,0:T(8,128)(2,1)}, bf16[256,192]{1,0:T(8,128)(2,1)S(1)}, u32[]{:S(2)}, u32[]{:S(2)}) collective-permute-start(bf16[256,192]{1,0:T(8,128)(2,1)} %get-tuple-element.166), channel_id=1, source_target_pairs={{6,0},{4,1},{2,2},{0,3},{7,4},{5,5},{3,6},{1,7},{14,8},{12,9},{10,... | collective-permute-start | bytes 294920 | tf_op jit(solution)/shard_map/ppermute | solution.py:417
  140.3 10.3 %feed_weights.1 = (bf16[2,4,104,1280]{3,2,1,0:T(8,128)(2,1)}, bf16[2,4,104,1280]{3,2,1,0:T(8,128)(2,1)}, bf16[2,4,104,512]{3,2,1,0:T(8,128)(2,1)}, bf16[2,4,104,512]{3,2,1,0:T(8,128)(2,1)}) custom-call(s32[9]{0:T(128)} %fusion.21.refs_0_.meta, bf16[3,2,264,192]{3,2,1,0:T(8,128)(2,1)} %get-tuple-element.159.refs_1_, ...), custom_call_target="tpu_custom_call" | custom-call | flops 2717908992 | bytes 20000000 | tf_op jit(solution)/shard_map/feed_weights/pallas_call | solution.py:1020
  153.9 17.2 %attend_back.1 = (bf16[1024,576]{1,0:T(8,128)(2,1)}, bf16[256,768]{1,0:T(8,128)(2,1)}, bf16[256,768]{1,0:T(8,128)(2,1)}, bf16[256,768]{1,0:T(8,128)(2,1)}, bf16[256,768]{1,0:T(8,128)(2,1)}) custom-call(s32[9]{0:T(128)} %fusion.21.refs_0_.meta, bf16[1024,576]{1,0:T(8,128)(2,1)} %get-tuple-element.168.refs_1_, bf16[256,192]{1,0:T(8,128)(2,1)} %copy-done.44, ...), custom_call_target="tpu_custom_call" | custom-call | flops 24159191040 | bytes 8000000 | tf_op jit(solution)/shard_map/attend_back/pallas_call | solution.py:653
  172.2 4.5 %collective-permute-start.40 = (bf16[256,768]{1,0:T(8,128)(2,1)}, bf16[256,768]{1,0:T(8,128)(2,1)}, u32[]{:S(2)}, u32[]{:S(2)}) collective-permute-start(bf16[256,768]{1,0:T(8,128)(2,1)} %get-tuple-element.184), channel_id=1, source_target_pairs={{0,0},{1,2},{2,4},{3,6},{4,1},{5,3},{6,5},{7,7},{8,8},{9,10},{10,1... | collective-permute-start | bytes 1179656 | tf_op jit(solution)/shard_map/ppermute | solution.py:417
  179.1 9.8 %collective-permute-start.42 = (bf16[256,768]{1,0:T(8,128)(2,1)}, bf16[256,768]{1,0:T(8,128)(2,1)}, u32[]{:S(2)}, u32[]{:S(2)}) collective-permute-start(bf16[256,768]{1,0:T(8,128)(2,1)} %get-tuple-element.191), channel_id=1, source_target_pairs={{0,2},{1,0},{2,6},{3,4},{4,3},{5,1},{6,7},{7,5},{8,10},{9,8},{10,1... | collective-permute-start | bytes 1179656 | tf_op jit(solution)/shard_map/ppermute | solution.py:417
  188.9 3.0 collective-permute-start.43
  191.9 2.2 collective-permute-start.44
  194.1 5.1 %projection_weights.1 = (f32[2,200,640]{2,1,0:T(8,128)}, bf16[2,200,640]{2,1,0:T(8,128)(2,1)}) custom-call(s32[9]{0:T(128)} %fusion.21.refs_0_.meta, bf16[2,512,768]{2,1,0:T(8,128)(2,1)} %own.1, bf16[512,768]{1,0:T(8,128)(2,1)} %copy-done.12, bf16[1024,576]{1,0:T(8,128)(2,1)} %get-tuple-element.186.grads), custom_call_target="tpu_custom_call" | custom-call | flops 905969664 | bytes 8000000 | tf_op jit(solution)/shard_map/projection_weights/pallas_call | solution.py:1040
  199.2 24.3 %collective-permute-done.42 = bf16[256,768]{1,0:T(8,128)(2,1)} collective-permute-done((bf16[256,768]{1,0:T(8,128)(2,1)}, bf16[256,768]{1,0:T(8,128)(2,1)}, u32[]{:S(2)}, u32[]{:S(2)}) %collective-permute-start.42) | collective-permute-done | bytes 393248 | tf_op jit(solution)/shard_map/ppermute | solution.py:417
  225.4 17.6 %collective-permute-start.46 = (bf16[256,768]{1,0:T(8,128)(2,1)S(1)}, bf16[256,768]{1,0:T(8,128)(2,1)S(1)}, u32[]{:S(2)}, u32[]{:S(2)}) collective-permute-start(bf16[256,768]{1,0:T(8,128)(2,1)S(1)} %add_convert_fusion.2), channel_id=1, source_target_pairs={{0,1},{1,0},{2,3},{3,2},{4,5},{5,4},{6,7},{7,6},{8,9},{9,8},{10,11... | collective-permute-start | bytes 1179656 | tf_op jit(solution)/shard_map/ppermute | solution.py:401
  245.4 7.6 %collective-permute-start.48 = (bf16[256,768]{1,0:T(8,128)(2,1)S(1)}, bf16[256,768]{1,0:T(8,128)(2,1)S(1)}, u32[]{:S(2)}, u32[]{:S(2)}) collective-permute-start(bf16[256,768]{1,0:T(8,128)(2,1)S(1)} %collective-permute-done.47), channel_id=1, source_target_pairs={{0,1},{1,0},{2,3},{3,2},{4,5},{5,4},{6,7},{7,6},{8,9},{9,8},{10,11... | collective-permute-start | bytes 1179656 | tf_op jit(solution)/shard_map/ppermute | solution.py:401
  253.0 8.4 %collective-permute-done.45 = bf16[256,768]{1,0:T(8,128)(2,1)S(1)} collective-permute-done((bf16[256,768]{1,0:T(8,128)(2,1)}, bf16[256,768]{1,0:T(8,128)(2,1)S(1)}, u32[]{:S(2)}, u32[]{:S(2)}) %collective-permute-start.45) | collective-permute-done | bytes 393248 | tf_op jit(solution)/shard_map/ppermute | solution.py:401
  267.1 3.5 %collective-permute-done.50 = bf16[200,640]{1,0:T(8,128)(2,1)S(1)} collective-permute-done((bf16[200,640]{1,0:T(8,128)(2,1)S(1)}, bf16[200,640]{1,0:T(8,128)(2,1)S(1)}, u32[]{:S(2)}, u32[]{:S(2)}) %collective-permute-start.50) | collective-permute-done | bytes 256032 | tf_op jit(solution)/shard_map/ppermute | solution.py:401
  270.7 7.2 %collective-permute-start.51 = (bf16[200,640]{1,0:T(8,128)(2,1)S(1)}, bf16[200,640]{1,0:T(8,128)(2,1)S(1)}, u32[]{:S(2)}, u32[]{:S(2)}) collective-permute-start(bf16[200,640]{1,0:T(8,128)(2,1)S(1)} %fusion.7), channel_id=1, source_target_pairs={{0,4},{4,0},{1,5},{5,1},{2,6},{6,2},{3,7},{7,3},{8,12},{12,8},{9,1... | collective-permute-start | bytes 768008 | tf_op jit(solution)/shard_map/ppermute | solution.py:401
  283.5 12.9 %collective-permute-done.53 = bf16[2,104,1792]{2,1,0:T(8,128)(2,1)S(1)} collective-permute-done((bf16[2,104,1792]{2,1,0:T(8,128)(2,1)S(1)}, bf16[2,104,1792]{2,1,0:T(8,128)(2,1)S(1)}, u32[]{:S(2)}, u32[]{:S(2)}) %collective-permute-start.53) | collective-permute-done | bytes 745504 | tf_op jit(solution)/shard_map/ppermute | solution.py:401
  299.7 11.9 %collective-permute-done.54 = bf16[104,1792]{1,0:T(8,128)(2,1)S(1)} collective-permute-done((bf16[104,1792]{1,0:T(8,128)(2,1)S(1)}, bf16[104,1792]{1,0:T(8,128)(2,1)S(1)}, u32[]{:S(2)}, u32[]{:S(2)}) %collective-permute-start.54) | collective-permute-done | bytes 372768 | tf_op jit(solution)/shard_map/ppermute | solution.py:401
  314.1 7.1 %collective-permute-done.55 = bf16[104,1792]{1,0:T(8,128)(2,1)S(1)} collective-permute-done((bf16[104,1792]{1,0:T(8,128)(2,1)S(1)}, bf16[104,1792]{1,0:T(8,128)(2,1)S(1)}, u32[]{:S(2)}, u32[]{:S(2)}) %collective-permute-start.55) | collective-permute-done | bytes 372768 | tf_op jit(solution)/shard_map/ppermute | solution.py:401
  (246 shorter events, 72.2 us)
Async XLA Ops:
  4.2 17.7 %collective-permute-start.2 = (bf16[96,1024]{1,0:T(8,128)(2,1)S(1)}, bf16[96,1024]{1,0:T(8,128)(2,1)S(1)}, u32[]{:S(2)}, u32[]{:S(2)}) collective-permute-start(bf16[96,1024]{1,0:T(8,128)(2,1)S(1)} %pad.8.refs_0_), channel_id=1, source_target_pairs={{0,2},{1,3},{2,0},{3,1},{4,6},{5,7},{6,4},{7,5},{8,10},{9,11},{10,... | collective-permute-start | bytes 589832 | tf_op jit(solution)/shard_map/ppermute | solution.py:401
  9.9 22.2 %collective-permute-start = (bf16[512,768]{1,0:T(8,128)(2,1)S(1)}, bf16[512,768]{1,0:T(8,128)(2,1)S(1)}, u32[]{:S(2)}, u32[]{:S(2)}) collective-permute-start(bf16[512,768]{1,0:T(8,128)(2,1)S(1)} %dynamic-slice_bitcast_fusion), channel_id=1, source_target_pairs={{0,4},{4,0},{1,5},{5,1},{2,6},{6,2},{3,7},{7,3},{8,12},{12,8},{9,1... | collective-permute-start | bytes 2359304 | tf_op jit(solution)/shard_map/ppermute | solution.py:401
  13.7 18.4 %collective-permute-start.4 = (bf16[200,576]{1,0:T(8,128)(2,1)S(1)}, bf16[200,576]{1,0:T(8,128)(2,1)}, u32[]{:S(2)}, u32[]{:S(2)}) collective-permute-start(bf16[200,576]{1,0:T(8,128)(2,1)S(1)} %fusion.11.refs_3_), channel_id=1, source_target_pairs={{0,8},{8,0},{16,24},{24,16},{1,9},{9,1},{17,25},{25,17},{2,10},{10... | collective-permute-start | bytes 691208 | tf_op jit(solution)/shard_map/ppermute | solution.py:401
  32.2 20.5 %collective-permute-start.7 = (bf16[4,96,1024]{2,1,0:T(8,128)(2,1)}, bf16[4,96,1024]{2,1,0:T(8,128)(2,1)S(1)}, u32[]{:S(2)}, u32[]{:S(2)}) collective-permute-start(bf16[4,96,1024]{2,1,0:T(8,128)(2,1)} %stack_pieces.2.refs_8_.refs_7_), channel_id=1, source_target_pairs={{0,4},{4,0},{1,5},{5,1},{2,6},{6,2},{3,7},{7,3},{8,12},{12,8},{9,1... | collective-permute-start | bytes 2359304 | tf_op jit(solution)/shard_map/ppermute | solution.py:401
  32.8 19.9 %collective-permute-start.8 = (bf16[4,96,1024]{2,1,0:T(8,128)(2,1)}, bf16[4,96,1024]{2,1,0:T(8,128)(2,1)S(1)}, u32[]{:S(2)}, u32[]{:S(2)}) collective-permute-start(bf16[4,96,1024]{2,1,0:T(8,128)(2,1)} %stack_pieces.2.refs_8_.refs_7_), channel_id=1, source_target_pairs={{0,16},{8,24},{16,0},{24,8},{1,17},{9,25},{17,1},{25,9},{2,18},{10... | collective-permute-start | bytes 2359304 | tf_op jit(solution)/shard_map/ppermute | solution.py:401
  34.3 18.3 %collective-permute-start.10 = (bf16[104,768]{1,0:T(8,128)(2,1)S(1)}, bf16[104,768]{1,0:T(8,128)(2,1)}, u32[]{:S(2)}, u32[]{:S(2)}) collective-permute-start(bf16[104,768]{1,0:T(8,128)(2,1)S(1)} %maximum_maximum_fusion.refs_0_), channel_id=1, source_target_pairs={{0,2},{1,3},{2,0},{3,1},{4,6},{5,7},{6,4},{7,5},{8,10},{9,11},{10,... | collective-permute-start | bytes 479240 | tf_op jit(solution)/shard_map/ppermute | solution.py:401
  34.6 18.0 %collective-permute-start.11 = (bf16[104,768]{1,0:T(8,128)(2,1)S(1)}, bf16[104,768]{1,0:T(8,128)(2,1)}, u32[]{:S(2)}, u32[]{:S(2)}) collective-permute-start(bf16[104,768]{1,0:T(8,128)(2,1)S(1)} %maximum_maximum_fusion.refs_0_), channel_id=1, source_target_pairs={{0,3},{1,2},{2,1},{3,0},{4,7},{5,6},{6,5},{7,4},{8,11},{9,10},{10,... | collective-permute-start | bytes 479240 | tf_op jit(solution)/shard_map/ppermute | solution.py:401
  37.1 15.6 %collective-permute-start.9 = (bf16[104,768]{1,0:T(8,128)(2,1)S(1)}, bf16[104,768]{1,0:T(8,128)(2,1)}, u32[]{:S(2)}, u32[]{:S(2)}) collective-permute-start(bf16[104,768]{1,0:T(8,128)(2,1)S(1)} %maximum_maximum_fusion.refs_0_), channel_id=1, source_target_pairs={{0,1},{1,0},{2,3},{3,2},{4,5},{5,4},{6,7},{7,6},{8,9},{9,8},{10,11... | collective-permute-start | bytes 479240 | tf_op jit(solution)/shard_map/ppermute | solution.py:401
  52.7 19.1 %collective-permute-start.12 = (bf16[4,96,1024]{2,1,0:T(8,128)(2,1)S(1)}, bf16[4,96,1024]{2,1,0:T(8,128)(2,1)S(1)}, u32[]{:S(2)}, u32[]{:S(2)}) collective-permute-start(bf16[4,96,1024]{2,1,0:T(8,128)(2,1)S(1)} %collective-permute-done.7.refs_9_.refs_8_), channel_id=1, source_target_pairs={{0,16},{8,24},{16,0},{24,8},{1,17},{9,25},{17,1},{25,9},{2,18},{10... | collective-permute-start | bytes 2359304 | tf_op jit(solution)/shard_map/ppermute | solution.py:401
  54.9 16.9 %collective-permute-start.14 = (bf16[256,192]{1,0:T(8,128)(2,1)}, bf16[256,192]{1,0:T(8,128)(2,1)S(1)}, u32[]{:S(2)}, u32[]{:S(2)}) collective-permute-start(bf16[256,192]{1,0:T(8,128)(2,1)} %get-tuple-element.130.refs_7_), channel_id=1, source_target_pairs={{0,2},{1,0},{2,6},{3,4},{4,3},{5,1},{6,7},{7,5},{8,10},{9,8},{10,1... | collective-permute-start | bytes 294920 | tf_op jit(solution)/shard_map/ppermute | solution.py:417
  75.0 18.0 %collective-permute-start.21 = (bf16[4,104,768]{2,1,0:T(8,128)(2,1)}, bf16[4,104,768]{2,1,0:T(8,128)(2,1)}, u32[]{:S(2)}, u32[]{:S(2)}) collective-permute-start(bf16[4,104,768]{2,1,0:T(8,128)(2,1)} %stack_pieces.3.refs_7_.refs_15_), channel_id=1, source_target_pairs={{0,4},{4,0},{1,5},{5,1},{2,6},{6,2},{3,7},{7,3},{8,12},{12,8},{9,1... | collective-permute-start | bytes 1916936 | tf_op jit(solution)/shard_map/ppermute | solution.py:401
  78.1 16.4 %collective-permute-start.22 = (bf16[4,104,768]{2,1,0:T(8,128)(2,1)}, bf16[4,104,768]{2,1,0:T(8,128)(2,1)}, u32[]{:S(2)}, u32[]{:S(2)}) collective-permute-start(bf16[4,104,768]{2,1,0:T(8,128)(2,1)} %stack_pieces.3.refs_7_.refs_15_), channel_id=1, source_target_pairs={{0,16},{8,24},{16,0},{24,8},{1,17},{9,25},{17,1},{25,9},{2,18},{10... | collective-permute-start | bytes 1916936 | tf_op jit(solution)/shard_map/ppermute | solution.py:401
  126.4 24.2 %collective-permute-start.32 = (bf16[256,192]{1,0:T(8,128)(2,1)}, bf16[256,192]{1,0:T(8,128)(2,1)S(1)}, u32[]{:S(2)}, u32[]{:S(2)}) collective-permute-start(bf16[256,192]{1,0:T(8,128)(2,1)} %get-tuple-element.163), channel_id=1, source_target_pairs={{0,0},{2,1},{4,2},{6,3},{1,4},{3,5},{5,6},{7,7},{8,8},{10,9},{12,1... | collective-permute-start | bytes 294920 | tf_op jit(solution)/shard_map/ppermute | solution.py:417
  127.9 22.8 %collective-permute-start.33 = (bf16[256,192]{1,0:T(8,128)(2,1)}, bf16[256,192]{1,0:T(8,128)(2,1)S(1)}, u32[]{:S(2)}, u32[]{:S(2)}) collective-permute-start(bf16[256,192]{1,0:T(8,128)(2,1)} %get-tuple-element.164), channel_id=1, source_target_pairs={{2,0},{0,1},{6,2},{4,3},{3,4},{1,5},{7,6},{5,7},{10,8},{8,9},{14,1... | collective-permute-start | bytes 294920 | tf_op jit(solution)/shard_map/ppermute | solution.py:417
  130.1 20.6 %collective-permute-start.34 = (bf16[256,192]{1,0:T(8,128)(2,1)}, bf16[256,192]{1,0:T(8,128)(2,1)S(1)}, u32[]{:S(2)}, u32[]{:S(2)}) collective-permute-start(bf16[256,192]{1,0:T(8,128)(2,1)} %get-tuple-element.165), channel_id=1, source_target_pairs={{4,0},{6,1},{0,2},{2,3},{5,4},{7,5},{1,6},{3,7},{12,8},{14,9},{8,1... | collective-permute-start | bytes 294920 | tf_op jit(solution)/shard_map/ppermute | solution.py:417
  135.0 15.8 %collective-permute-start.35 = (bf16[256,192]{1,0:T(8,128)(2,1)}, bf16[256,192]{1,0:T(8,128)(2,1)S(1)}, u32[]{:S(2)}, u32[]{:S(2)}) collective-permute-start(bf16[256,192]{1,0:T(8,128)(2,1)} %get-tuple-element.166), channel_id=1, source_target_pairs={{6,0},{4,1},{2,2},{0,3},{7,4},{5,5},{3,6},{1,7},{14,8},{12,9},{10,... | collective-permute-start | bytes 294920 | tf_op jit(solution)/shard_map/ppermute | solution.py:417
  138.6 32.5 %collective-permute-start.37 = (bf16[256,768]{1,0:T(8,128)(2,1)}, bf16[256,768]{1,0:T(8,128)(2,1)}, u32[]{:S(2)}, u32[]{:S(2)}) collective-permute-start(bf16[256,768]{1,0:T(8,128)(2,1)} %get-tuple-element.158), channel_id=1, source_target_pairs={{0,1},{1,0},{2,3},{3,2},{4,5},{5,4},{6,7},{7,6},{8,9},{9,8},{10,11... | collective-permute-start | bytes 1179656 | tf_op jit(solution)/shard_map/ppermute | solution.py:401
  150.6 20.4 %collective-permute-start.38 = (bf16[256,768]{1,0:T(8,128)(2,1)}, bf16[256,768]{1,0:T(8,128)(2,1)}, u32[]{:S(2)}, u32[]{:S(2)}) collective-permute-start(bf16[256,768]{1,0:T(8,128)(2,1)} %get-tuple-element.158), channel_id=1, source_target_pairs={{0,2},{1,3},{2,0},{3,1},{4,6},{5,7},{6,4},{7,5},{8,10},{9,11},{10,... | collective-permute-start | bytes 1179656 | tf_op jit(solution)/shard_map/ppermute | solution.py:401
  151.5 20.7 %collective-permute-start.36 = (bf16[2,4,104,512]{3,2,1,0:T(8,128)(2,1)}, bf16[2,4,104,512]{3,2,1,0:T(8,128)(2,1)}, u32[]{:S(2)}, u32[]{:S(2)}) collective-permute-start(bf16[2,4,104,512]{3,2,1,0:T(8,128)(2,1)} %get-tuple-element.167), channel_id=1, source_target_pairs={{0,4},{4,0},{1,5},{5,1},{2,6},{6,2},{3,7},{7,3},{8,12},{12,8},{9,1... | collective-permute-start | bytes 2555912 | tf_op jit(solution)/shard_map/ppermute | solution.py:401
  153.0 70.5 %collective-permute-start.39 = (bf16[2,4,104,1280]{3,2,1,0:T(8,128)(2,1)}, bf16[2,4,104,1280]{3,2,1,0:T(8,128)(2,1)S(1)}, u32[]{:S(2)}, u32[]{:S(2)}) collective-permute-start(bf16[2,4,104,1280]{3,2,1,0:T(8,128)(2,1)} %get-tuple-element.180), channel_id=1, source_target_pairs={{0,16},{8,24},{16,0},{24,8},{1,17},{9,25},{17,1},{25,9},{2,18},{10... | collective-permute-start | bytes 6389768 | tf_op jit(solution)/shard_map/ppermute | solution.py:401
  178.6 45.0 %collective-permute-start.41 = (bf16[4,104,512]{2,1,0:T(8,128)(2,1)}, bf16[4,104,512]{2,1,0:T(8,128)(2,1)}, u32[]{:S(2)}, u32[]{:S(2)}) collective-permute-start(bf16[4,104,512]{2,1,0:T(8,128)(2,1)} %fusion.9), channel_id=1, source_target_pairs={{0,16},{8,24},{16,0},{24,8},{1,17},{9,25},{17,1},{25,9},{2,18},{10... | collective-permute-start | bytes 1277960 | tf_op jit(solution)/shard_map/ppermute | solution.py:401
  179.1 44.4 %collective-permute-start.42 = (bf16[256,768]{1,0:T(8,128)(2,1)}, bf16[256,768]{1,0:T(8,128)(2,1)}, u32[]{:S(2)}, u32[]{:S(2)}) collective-permute-start(bf16[256,768]{1,0:T(8,128)(2,1)} %get-tuple-element.191), channel_id=1, source_target_pairs={{0,2},{1,0},{2,6},{3,4},{4,3},{5,1},{6,7},{7,5},{8,10},{9,8},{10,1... | collective-permute-start | bytes 1179656 | tf_op jit(solution)/shard_map/ppermute | solution.py:417
  188.9 34.6 %collective-permute-start.43 = (bf16[256,768]{1,0:T(8,128)(2,1)}, bf16[256,768]{1,0:T(8,128)(2,1)}, u32[]{:S(2)}, u32[]{:S(2)}) collective-permute-start(bf16[256,768]{1,0:T(8,128)(2,1)} %get-tuple-element.192), channel_id=1, source_target_pairs={{0,4},{1,6},{2,0},{3,2},{4,5},{5,7},{6,1},{7,3},{8,12},{9,14},{10,... | collective-permute-start | bytes 1179656 | tf_op jit(solution)/shard_map/ppermute | solution.py:417
  191.9 31.6 %collective-permute-start.44 = (bf16[256,768]{1,0:T(8,128)(2,1)}, bf16[256,768]{1,0:T(8,128)(2,1)}, u32[]{:S(2)}, u32[]{:S(2)}) collective-permute-start(bf16[256,768]{1,0:T(8,128)(2,1)} %get-tuple-element.193), channel_id=1, source_target_pairs={{0,6},{1,4},{2,2},{3,0},{4,7},{5,5},{6,3},{7,1},{8,14},{9,12},{10,... | collective-permute-start | bytes 1179656 | tf_op jit(solution)/shard_map/ppermute | solution.py:417
  225.3 20.0 %collective-permute-start.47 = (bf16[256,768]{1,0:T(8,128)(2,1)S(1)}, bf16[256,768]{1,0:T(8,128)(2,1)S(1)}, u32[]{:S(2)}, u32[]{:S(2)}) collective-permute-start(bf16[256,768]{1,0:T(8,128)(2,1)S(1)} %add_convert_fusion.2), channel_id=1, source_target_pairs={{0,2},{1,3},{2,0},{3,1},{4,6},{5,7},{6,4},{7,5},{8,10},{9,11},{10,... | collective-permute-start | bytes 1179656 | tf_op jit(solution)/shard_map/ppermute | solution.py:401
  225.4 52.5 %collective-permute-start.46 = (bf16[256,768]{1,0:T(8,128)(2,1)S(1)}, bf16[256,768]{1,0:T(8,128)(2,1)S(1)}, u32[]{:S(2)}, u32[]{:S(2)}) collective-permute-start(bf16[256,768]{1,0:T(8,128)(2,1)S(1)} %add_convert_fusion.2), channel_id=1, source_target_pairs={{0,1},{1,0},{2,3},{3,2},{4,5},{5,4},{6,7},{7,6},{8,9},{9,8},{10,11... | collective-permute-start | bytes 1179656 | tf_op jit(solution)/shard_map/ppermute | solution.py:401
  243.1 19.9 %collective-permute-start.49 = (bf16[2,200,640]{2,1,0:T(8,128)(2,1)S(1)}, bf16[2,200,640]{2,1,0:T(8,128)(2,1)S(1)}, u32[]{:S(2)}, u32[]{:S(2)}) collective-permute-start(bf16[2,200,640]{2,1,0:T(8,128)(2,1)S(1)} %copy-done.43), channel_id=1, source_target_pairs={{0,8},{8,0},{16,24},{24,16},{1,9},{9,1},{17,25},{25,17},{2,10},{10... | collective-permute-start | bytes 1536008 | tf_op jit(solution)/shard_map/ppermute | solution.py:401
  243.1 18.4 %collective-permute-start.45 = (bf16[256,768]{1,0:T(8,128)(2,1)}, bf16[256,768]{1,0:T(8,128)(2,1)S(1)}, u32[]{:S(2)}, u32[]{:S(2)}) collective-permute-start(bf16[256,768]{1,0:T(8,128)(2,1)} %collective-permute-done.38), channel_id=1, source_target_pairs={{0,1},{1,0},{2,3},{3,2},{4,5},{5,4},{6,7},{7,6},{8,9},{9,8},{10,11... | collective-permute-start | bytes 1179656 | tf_op jit(solution)/shard_map/ppermute | solution.py:401
  244.7 35.4 %collective-permute-start.52 = (bf16[4,104,1280]{2,1,0:T(8,128)(2,1)S(1)}, bf16[4,104,1280]{2,1,0:T(8,128)(2,1)S(1)}, u32[]{:S(2)}, u32[]{:S(2)}) collective-permute-start(bf16[4,104,1280]{2,1,0:T(8,128)(2,1)S(1)} %fusion.3), channel_id=1, source_target_pairs={{0,4},{4,0},{1,5},{5,1},{2,6},{6,2},{3,7},{7,3},{8,12},{12,8},{9,1... | collective-permute-start | bytes 3194888 | tf_op jit(solution)/shard_map/ppermute | solution.py:401
  245.4 32.5 %collective-permute-start.48 = (bf16[256,768]{1,0:T(8,128)(2,1)S(1)}, bf16[256,768]{1,0:T(8,128)(2,1)S(1)}, u32[]{:S(2)}, u32[]{:S(2)}) collective-permute-start(bf16[256,768]{1,0:T(8,128)(2,1)S(1)} %collective-permute-done.47), channel_id=1, source_target_pairs={{0,1},{1,0},{2,3},{3,2},{4,5},{5,4},{6,7},{7,6},{8,9},{9,8},{10,11... | collective-permute-start | bytes 1179656 | tf_op jit(solution)/shard_map/ppermute | solution.py:401
  280.6 15.8 %collective-permute-start.53 = (bf16[2,104,1792]{2,1,0:T(8,128)(2,1)S(1)}, bf16[2,104,1792]{2,1,0:T(8,128)(2,1)S(1)}, u32[]{:S(2)}, u32[]{:S(2)}) collective-permute-start(bf16[2,104,1792]{2,1,0:T(8,128)(2,1)S(1)} %fusion.2), channel_id=1, source_target_pairs={{0,1},{1,0},{2,3},{3,2},{4,5},{5,4},{6,7},{7,6},{8,9},{9,8},{10,11... | collective-permute-start | bytes 2236424 | tf_op jit(solution)/shard_map/ppermute | solution.py:401
  296.6 15.0 %collective-permute-start.54 = (bf16[104,1792]{1,0:T(8,128)(2,1)S(1)}, bf16[104,1792]{1,0:T(8,128)(2,1)S(1)}, u32[]{:S(2)}, u32[]{:S(2)}) collective-permute-start(bf16[104,1792]{1,0:T(8,128)(2,1)S(1)} %fusion.10), channel_id=1, source_target_pairs={{0,2},{1,3},{2,0},{3,1},{4,6},{5,7},{6,4},{7,5},{8,10},{9,11},{10,... | collective-permute-start | bytes 1118216 | tf_op jit(solution)/shard_map/ppermute | solution.py:401
  (72 other events, 756.9 us)

commit v3 on v2

--- a/solution.py
+++ b/solution.py
@@ -412,7 +412,7 @@
         for z in range(4):
             block = z ^ step
             source = x * 4 + z
-            target = (block >> 1) * 4 + 2 * (block & 1) + x
+            target = (block >> 1) * 4 + (block ^ (2 * x))
             pairs.append((target, source) if back else (source, target))
     return lax.ppermute(value, ("ctx", "tp"), pairs)
 
@@ -460,11 +460,6 @@
         cost_estimate=cost(0, 4 * math.prod(shape)),
         name="stack_pieces",
     )(*pieces)
-
-
-def line_stack(own_half):
-    far = swapped(own_half, "tp", 2)
-    return stacked([own_half, swapped(own_half, "tp", 1), far, swapped(far, "tp", 1)])
 
 
 def piece_copies(meta, pieces, taken, columns, target, sems, first):
@@ -883,7 +878,7 @@
     shard = w_query.shape[0]
     half = shard // 2
     padded = -(-width // 128) * 128
-    own_seq, own_place = z % 2, z // 2
+    own_seq, own_place = (z // 2) ^ x, z % 2
     quarter = 2 * x + own_place
     length_of = lambda place: lax.dynamic_index_in_dim(lengths, place, 0, keepdims=False)
     entries = (x, z, f, length_of(x), quarter, own_seq, own_place, z ^ (2 * x), length_of(own_seq))
@@ -903,7 +898,7 @@
     other = lax.dynamic_index_in_dim(tokens, 1 - x, 0, keepdims=False)
     other, half_a = tied(other, half_a)
     other = swapped(other, "ctx", 1)
-    line_a = line_stack(half_a)
+    far_a, near_half = swapped(half_a, "tp", 2), swapped(half_a, "tp", 1)
     per_head = lambda weights: jnp.concatenate(
         [
             weight[..., head * HEAD_DIM : (head + 1) * HEAD_DIM]
@@ -920,7 +915,8 @@
         ]
     )
     qkv_bias = wide(per_head((b_query, jnp.zeros_like(b_query), b_value)))[None, :]
-    qkv_y = swapped(qkv_shard, "fsdp", 2)
+    qkv_y, far_a, meta = tied(swapped(qkv_shard, "fsdp", 2), far_a, meta)
+    line_a = stacked([half_a, near_half, far_a, swapped(far_a, "tp", 1)])
     qkv_pieces = (qkv_shard, swapped(qkv_shard, "fsdp", 1), qkv_y, swapped(qkv_y, "fsdp", 1))
 
     core = lambda array: swapped(array, "fsdp", 1)
@@ -938,10 +934,10 @@
     line_b = stacked([half_b, *b_pieces])
     att = [to_owner(part, step) for step, part in enumerate(parts)]
     x_y_a = swapped(x_a, "fsdp", 2)
-    x_y_a, x_a, y_a, line_a, *att = tied(x_y_a, x_a, y_a, line_a, *att)
+    x_y_a, x_a, y_a, line_a, line_b, *att = tied(x_y_a, x_a, y_a, line_a, line_b, *att)
     near_a = (line_a, x_a, y_a, x_y_a)
     pieces_a = (*near_a, *map(core, near_a))
-    x_b, y_b = swapped(line_b, "ctx", 1), swapped(line_b, "fsdp", 2)
+    x_b, y_b, line_core = swapped(line_b, "ctx", 1), swapped(line_b, "fsdp", 2), core(line_b)
 
     def row_spec(array):
         return pl.BlockSpec((1, rows, model), lambda step, meta: (meta[5], meta[6], 0))
@@ -975,13 +971,10 @@
         name="feed_first",
     )(meta, *att, tokens, vectors, line_b, *pieces_a)
 
-    both, x_b, y_b, line_b = tied(both, x_b, y_b, line_b)
+    both, x_b, y_b, line_b, line_core = tied(both, x_b, y_b, line_b, line_core)
     x_y_b = [swapped(x_b[:2], "fsdp", 2), swapped(y_b[2:], "ctx", 1)]
-    cores_b = [core(line_b), core(x_b), core(y_b)]
-    rest = tied(*x_y_b, *cores_b)
-    x_y_b, cores_b = rest[:2], rest[2:]
-    both_sib = core(both)
-    pieces_b = (line_b, x_b, y_b, *x_y_b, *cores_b, *map(core, x_y_b))
+    *x_y_b, x_core, y_core, both_sib = tied(*x_y_b, core(x_b), core(y_b), core(both))
+    pieces_b = (line_b, x_b, y_b, *x_y_b, line_core, x_core, y_core, *map(core, x_y_b))
 
     second_out = [
         struct((rows, model)),
@@ -1029,14 +1022,15 @@
         name="feed_weights",
     )(meta, keep, both, both_sib, mixed, mixed_sib)
 
-    far_up, theirs_down, *grad_att = tied(far_up, theirs_down, *grad_att)
+    near_out = swapped(output, "tp", 1)
+    far_up, theirs_down, output, *grad_att = tied(far_up, theirs_down, output, *grad_att)
     got_up, got_down = swapped(far_up, "fsdp", 2), swapped(theirs_down, "ctx", 1)
-    far_z, near_z = swapped(output, "tp", 2), swapped(output, "tp", 1)
+    far_out = swapped(output, "tp", 2)
     grad_full, *grad_parts = attend_back_call(meta, qkv, grad_att, parts, stats, weight, heads)
 
-    got_down, near_z, far_z, *grad_parts = tied(got_down, near_z, far_z, *grad_parts)
+    near_out, far_out, *grad_parts = tied(near_out, far_out, *grad_parts)
     grad_rows = [to_owner(part, step) for step, part in enumerate(grad_parts)]
-    got_down, grad_full, grad_rows[0] = tied(got_down, grad_full, grad_rows[0])
+    grad_full, grad_rows[0] = tied(grad_full, grad_rows[0])
     kept, sent = pl.pallas_call(
         projections_kernel,
         grid_spec=grid(
@@ -1051,32 +1045,43 @@
         cost_estimate=cost(12 * local_rows * model * width, 8e6),
         name="projection_weights",
     )(meta, tokens, other, grad_full)
-    second_down = swapped(low(wide(mine_down[1]) + wide(got_down[1])), "fsdp", 2)
-    got_up, second_down, kept, sent, far_z, *grad_rows = tied(
-        got_up, second_down, kept, sent, far_z, *grad_rows
-    )
-    second_up = swapped(low(wide(near_up[1]) + wide(got_up[1])), "ctx", 1)
+    up_sent, down_sent, kept, sent, *grad_rows = tied(
+        low(wide(near_up[1]) + wide(got_up[1])),
+        low(wide(mine_down[1]) + wide(got_down[1])),
+        kept,
+        sent,
+        *grad_rows,
+    )
+    second_up, second_down = swapped(up_sent, "ctx", 1), swapped(down_sent, "fsdp", 2)
     token_rows = resid
     for part in grad_rows:
         token_rows = token_rows + wide(part)
 
     def spread_rows(pieces, dtype):
         blocks = [
-            lax.select_n(z, *[pieces[block ^ place] for place in range(4)]).astype(dtype)
+            lax.select_n(z ^ (2 * x), *[pieces[block ^ place] for place in range(4)]).astype(dtype)
             for block in range(4)
         ]
-        return jnp.stack([jnp.concatenate([blocks[seq], blocks[2 + seq]]) for seq in range(2)])
+        return jnp.stack([jnp.concatenate(blocks[2 * seq : 2 * seq + 2]) for seq in range(2)])
 
     token_rows = low(token_rows)
+    far_z, near_z, sent, second_up, second_down = tied(
+        swapped(token_rows, "tp", 2), token_rows, sent, second_up, second_down
+    )
     up_lines = wide(near_up[0]) + wide(got_up[0]) + wide(second_up)
     down_lines = wide(mine_down[0]) + wide(got_down[0]) + wide(second_down)
     lines = jnp.concatenate([up_lines, down_lines], axis=2)
     lines, line_sent = lines[:2], low(lines[2:])
     lines = lines + wide(swapped(line_sent, "tp", 1))
-    output_full = spread_rows([output, near_z, far_z, swapped(far_z, "tp", 1)], jnp.bfloat16)
-    far_z, near_z = swapped(token_rows, "tp", 2), swapped(token_rows, "tp", 1)
-    grad_tokens = spread_rows([token_rows, near_z, far_z, swapped(far_z, "tp", 1)], jnp.float32)
-    total = low(lines[0] + wide(swapped(low(lines[1]), "tp", 2)))
+    near_z = swapped(near_z, "tp", 1)
+    last_z, _ = tied(far_z, line_sent)
+    last_z = swapped(last_z, "tp", 1)
+    grad_tokens = spread_rows([token_rows, near_z, far_z, last_z], jnp.float32)
+    line_last, far_out = tied(swapped(low(lines[1]), "tp", 2), far_out)
+    output_full = spread_rows(
+        [output, near_out, far_out, swapped(far_out, "tp", 1)], jnp.bfloat16
+    )
+    total = low(lines[0] + wide(line_last))
     other_half = swapped(total, "ctx", 1)
     small = wide(total[half:])
     total = wide(

time: 325 us -> 305 us (0.938)
  waiting for transfers between devices: 109 us -> 89.5 us
    ppermute x12, waiting for transfers between devices: 33.7 us -> 5.55 us  [to_owner(): return lax.ppermute(value, ('ctx', 'tp'), pairs)]
    ppermute x44, starting transfers between devices: 66.9 us -> 47.3 us  [swapped(): lax.ppermute(value, axis, [(place, place ^ bit) for place in range(count)])]
    ppermute x12, starting transfers between devices: 36.6 us -> 53.8 us  [to_owner(): return lax.ppermute(value, ('ctx', 'tp'), pairs)]
    ppermute x44, waiting for transfers between devices: 74.8 us -> 83.9 us  [swapped(): lax.ppermute(value, axis, [(place, place ^ bit) for place in range(count)])]
    unnamed x98 -> x114, local copies, waits for them, and re-layouts: 6.75 us -> 5.62 us
  transfers between devices with their start and end apart: 56 -> 56, of which waited for: 17 -> 21; matrix products, arithmetic and copies ran while one was open for 6% -> 7% of each run, Pallas kernels for 19% -> 21%
where the time goes in v3:
time: 305 us; the launch traced here: 303 us
  starting transfers between devices  101 us (33%)
  waiting for transfers between devices  89.5 us (29%)
  Pallas kernels  77.2 us (25%)
  other arithmetic  22.4 us (7%)
  local copies, waits for them, and re-layouts  11.7 us (4%)
    ppermute x44, waiting for transfers between devices, swapped(): lax.ppermute(value, axis, [(place, place ^ bit) for place in range(count)])  83.9 us
    ppermute x12, starting transfers between devices, to_owner(): return lax.ppermute(value, ('ctx', 'tp'), pairs)  53.8 us
    ppermute x44, starting transfers between devices, swapped(): lax.ppermute(value, axis, [(place, place ^ bit) for place in range(count)])  47.3 us
    pallas_call x1, Pallas kernels, attend_back_call(): pl.pallas_call(lambda *refs: attend_back_kernel(*refs, block=block, heads...  17.1 us
    pallas_call x1, Pallas kernels, per_device_rows(): pl.pallas_call(lambda *refs: second_kernel(*refs, width=width), grid_spec...  14.8 us
    pallas_call x1, Pallas kernels, attend_call(): pl.pallas_call(lambda *refs: attend_kernel(*refs, block=block, heads=head...  14.8 us
    pallas_call x1, Pallas kernels, per_device_rows(): pl.pallas_call(lambda *refs: first_kernel(*refs, width=width), grid_spec=...  10.5 us
    pallas_call x1, Pallas kernels, per_device_rows(): pl.pallas_call(lambda *refs: weights_kernel(*refs, width=width), grid_spe...  10.4 us
  transfers between devices with their start and end apart: 56, of which 21 were waited for; matrix products, arithmetic and copies ran while one was open for 7% of the time, Pallas kernels for 21%

profile of v3, /device:TPU:0, one launch (start us, length us, event | category | flops | bytes accessed | tf_op | source)
XLA Modules:
  0.0 303.5 jit_solution(5089608756128380514)
XLA Ops:
  4.2 4.1 %collective-permute-start.1 = (bf16[96,1024]{1,0:T(8,128)(2,1)S(1)}, bf16[96,1024]{1,0:T(8,128)(2,1)S(1)}, u32[]{:S(2)}, u32[]{:S(2)}) collective-permute-start(bf16[96,1024]{1,0:T(8,128)(2,1)S(1)} %pad.9.refs_0_), channel_id=1, source_target_pairs={{0,2},{1,3},{2,0},{3,1},{4,6},{5,7},{6,4},{7,5},{8,10},{9,11},{10,... | collective-permute-start | bytes 589832 | tf_op jit(solution)/shard_map/ppermute | solution.py:401
  20.8 6.7 %collective-permute-done.4.refs_3_ = bf16[96,1024]{1,0:T(8,128)(2,1)S(1)} collective-permute-done((bf16[96,1024]{1,0:T(8,128)(2,1)S(1)}, bf16[96,1024]{1,0:T(8,128)(2,1)S(1)}, u32[]{:S(2)}, u32[]{:S(2)}) %collective-permute-start.4) | collective-permute-done | bytes 196640 | tf_op jit(solution)/shard_map/ppermute | solution.py:401
  28.2 2.1 stack_pieces.2.refs_8_.refs_7_
  36.0 14.8 %attend.1 = (bf16[1024,576]{1,0:T(8,128)(2,1)}, bf16[256,192]{1,0:T(8,128)(2,1)}, bf16[256,192]{1,0:T(8,128)(2,1)}, bf16[256,192]{1,0:T(8,128)(2,1)}, bf16[256,1...) custom-call(s32[9]{0:T(128)} %fusion.21.refs_0_.meta, ...), custom_call_target="tpu_custom_call" | custom-call | flops 10569646080 | bytes 8000000 | tf_op jit(solution)/shard_map/attend/pallas_call | solution.py:545
  54.4 6.5 %collective-permute-start.15 = (bf16[256,192]{1,0:T(8,128)(2,1)}, bf16[256,192]{1,0:T(8,128)(2,1)}, u32[]{:S(2)}, u32[]{:S(2)}) collective-permute-start(bf16[256,192]{1,0:T(8,128)(2,1)} %get-tuple-element.148.refs_8_), channel_id=1, source_target_pairs={{0,6},{1,7},{2,0},{3,1},{4,4},{5,5},{6,2},{7,3},{8,14},{9,15},{10,... | collective-permute-start | bytes 294920 | tf_op jit(solution)/shard_map/ppermute | solution.py:417
  62.6 2.0 stack_pieces.3.refs_7_.refs_15_
  64.7 4.5 %collective-permute-done.15.refs_3_ = bf16[256,192]{1,0:T(8,128)(2,1)} collective-permute-done((bf16[256,192]{1,0:T(8,128)(2,1)}, bf16[256,192]{1,0:T(8,128)(2,1)}, u32[]{:S(2)}, u32[]{:S(2)}) %collective-permute-start.15) | collective-permute-done | bytes 98336 | tf_op jit(solution)/shard_map/ppermute | solution.py:417
  75.8 10.5 %feed_first.1 = (f32[256,768]{1,0:T(8,128)}, f32[256,1]{1,0:T(8,128)}, bf16[4,256,1024]{2,1,0:T(8,128)(2,1)}, bf16[4,256,768]{2,1,0:T(8,128)(2,1)}) custom-call(s32[9]{0:T(128)} %fusion.21.refs_0_.meta, bf16[256,192]{1,0:T(8,128)(2,1)} %copy-done.40, bf16[256,192]{1,0:T(8,128)(2,1)} %copy-done.41, bf16[256,192]{1,0:T(8,128)(2,1)} %collective-permute-done.15.refs_3_, ...), custom_call_target="tpu_custom_call" | custom-call | flops 1509949440 | bytes 12000000 | tf_op jit(solution)/shard_map/feed_first/pallas_call | solution.py:959
  91.8 7.9 %collective-permute-done.24.refs_18_ = bf16[2,104,768]{2,1,0:T(8,128)(2,1)S(1)} collective-permute-done((bf16[2,104,768]{2,1,0:T(8,128)(2,1)S(1)}, bf16[2,104,768]{2,1,0:T(8,128)(2,1)S(1)}, u32[]{:S(2)}, u32[]{:S(2)}) %collective-permute-start.24) | collective-permute-done | bytes 319520 | tf_op jit(solution)/shard_map/ppermute | solution.py:401
  104.0 14.8 %feed_second.1 = (bf16[256,768]{1,0:T(8,128)(2,1)}, f32[256,768]{1,0:T(8,128)}, bf16[256,192]{1,0:T(8,128)(2,1)}, bf16[256,192]{1,0:T(8,128)(2,1)}, bf16[256,192...) custom-call(s32[9]{0:T(128)} %fusion.21.refs_0_.meta, ...), custom_call_target="tpu_custom_call" | custom-call | flops 3925868544 | bytes 20000000 | tf_op jit(solution)/shard_map/feed_second/pallas_call | solution.py:986
  120.6 2.2 collective-permute-start.33
  122.7 6.0 %collective-permute-start.34 = (bf16[256,192]{1,0:T(8,128)(2,1)}, bf16[256,192]{1,0:T(8,128)(2,1)}, u32[]{:S(2)}, u32[]{:S(2)}) collective-permute-start(bf16[256,192]{1,0:T(8,128)(2,1)} %get-tuple-element.181), channel_id=1, source_target_pairs={{6,0},{7,1},{0,2},{1,3},{4,4},{5,5},{2,6},{3,7},{14,8},{15,9},{8,1... | collective-permute-start | bytes 294920 | tf_op jit(solution)/shard_map/ppermute | solution.py:417
  128.7 3.2 %collective-permute-start.35 = (bf16[256,192]{1,0:T(8,128)(2,1)}, bf16[256,192]{1,0:T(8,128)(2,1)}, u32[]{:S(2)}, u32[]{:S(2)}) collective-permute-start(bf16[256,192]{1,0:T(8,128)(2,1)} %get-tuple-element.182), channel_id=1, source_target_pairs={{7,0},{6,1},{1,2},{0,3},{5,4},{4,5},{3,6},{2,7},{15,8},{14,9},{9,1... | collective-permute-start | bytes 294920 | tf_op jit(solution)/shard_map/ppermute | solution.py:417
  133.4 10.4 %feed_weights.1 = (bf16[2,4,104,1280]{3,2,1,0:T(8,128)(2,1)}, bf16[2,4,104,1280]{3,2,1,0:T(8,128)(2,1)}, bf16[2,4,104,512]{3,2,1,0:T(8,128)(2,1)}, bf16[2,4,104,512]{3,2,1,0:T(8,128)(2,1)}) custom-call(s32[9]{0:T(128)} %fusion.21.refs_0_.meta, bf16[3,2,264,192]{3,2,1,0:T(8,128)(2,1)} %get-tuple-element.173.refs_1_, ...), custom_call_target="tpu_custom_call" | custom-call | flops 2717908992 | bytes 20000000 | tf_op jit(solution)/shard_map/feed_weights/pallas_call | solution.py:1013
  143.9 3.5 %collective-permute-start.39 = (bf16[2,4,104,512]{3,2,1,0:T(8,128)(2,1)}, bf16[2,4,104,512]{3,2,1,0:T(8,128)(2,1)}, u32[]{:S(2)}, u32[]{:S(2)}) collective-permute-start(bf16[2,4,104,512]{3,2,1,0:T(8,128)(2,1)} %get-tuple-element.200), channel_id=1, source_target_pairs={{0,4},{4,0},{1,5},{5,1},{2,6},{6,2},{3,7},{7,3},{8,12},{12,8},{9,1... | collective-permute-start | bytes 2555912 | tf_op jit(solution)/shard_map/ppermute | solution.py:401
  148.2 17.1 %attend_back.1 = (bf16[1024,576]{1,0:T(8,128)(2,1)}, bf16[256,768]{1,0:T(8,128)(2,1)}, bf16[256,768]{1,0:T(8,128)(2,1)}, bf16[256,768]{1,0:T(8,128)(2,1)}, bf16[256,768]{1,0:T(8,128)(2,1)}) custom-call(s32[9]{0:T(128)} %fusion.21.refs_0_.meta, bf16[1024,576]{1,0:T(8,128)(2,1)} %get-tuple-element.184.refs_1_, bf16[256,192]{1,0:T(8,128)(2,1)} %copy-done.54, ...), custom_call_target="tpu_custom_call" | custom-call | flops 24159191040 | bytes 8000000 | tf_op jit(solution)/shard_map/attend_back/pallas_call | solution.py:648
  167.6 4.6 %collective-permute-start.42 = (bf16[256,768]{1,0:T(8,128)(2,1)}, bf16[256,768]{1,0:T(8,128)(2,1)}, u32[]{:S(2)}, u32[]{:S(2)}) collective-permute-start(bf16[256,768]{1,0:T(8,128)(2,1)} %get-tuple-element.208), channel_id=1, source_target_pairs={{0,6},{1,7},{2,0},{3,1},{4,4},{5,5},{6,2},{7,3},{8,14},{9,15},{10,... | collective-permute-start | bytes 1179656 | tf_op jit(solution)/shard_map/ppermute | solution.py:417
  172.3 22.8 %collective-permute-start.43 = (bf16[256,768]{1,0:T(8,128)(2,1)}, bf16[256,768]{1,0:T(8,128)(2,1)}, u32[]{:S(2)}, u32[]{:S(2)}) collective-permute-start(bf16[256,768]{1,0:T(8,128)(2,1)} %get-tuple-element.209), channel_id=1, source_target_pairs={{0,7},{1,6},{2,1},{3,0},{4,5},{5,4},{6,3},{7,2},{8,15},{9,14},{10,... | collective-permute-start | bytes 1179656 | tf_op jit(solution)/shard_map/ppermute | solution.py:417
  195.1 5.3 %projection_weights.1 = (f32[2,200,640]{2,1,0:T(8,128)}, bf16[2,200,640]{2,1,0:T(8,128)(2,1)}) custom-call(s32[9]{0:T(128)} %fusion.21.refs_0_.meta, bf16[2,512,768]{2,1,0:T(8,128)(2,1)} %own.1, bf16[512,768]{1,0:T(8,128)(2,1)} %copy-done.17, bf16[1024,576]{1,0:T(8,128)(2,1)} %get-tuple-element.203.grads), custom_call_target="tpu_custom_call" | custom-call | flops 905969664 | bytes 8000000 | tf_op jit(solution)/shard_map/projection_weights/pallas_call | solution.py:1034
  206.0 2.6 collective-permute-start.46
  208.6 2.2 add_convert_fusion.2
  210.8 3.9 %collective-permute-start.44 = (bf16[256,768]{1,0:T(8,128)(2,1)}, bf16[256,768]{1,0:T(8,128)(2,1)}, u32[]{:S(2)}, u32[]{:S(2)}) collective-permute-start(bf16[256,768]{1,0:T(8,128)(2,1)} %add_convert_fusion.2), channel_id=1, source_target_pairs={{0,2},{1,3},{2,0},{3,1},{4,6},{5,7},{6,4},{7,5},{8,10},{9,11},{10,... | collective-permute-start | bytes 1179656 | tf_op jit(solution)/shard_map/ppermute | solution.py:401
  214.7 15.3 %collective-permute-done.44 = bf16[256,768]{1,0:T(8,128)(2,1)} collective-permute-done((bf16[256,768]{1,0:T(8,128)(2,1)}, bf16[256,768]{1,0:T(8,128)(2,1)}, u32[]{:S(2)}, u32[]{:S(2)}) %collective-permute-start.44) | collective-permute-done | bytes 393248 | tf_op jit(solution)/shard_map/ppermute | solution.py:401
  233.8 2.7 collective-permute-start.51
  236.6 2.0 collective-permute-start.47
  238.6 8.2 %collective-permute-done.51 = bf16[256,768]{1,0:T(8,128)(2,1)} collective-permute-done((bf16[256,768]{1,0:T(8,128)(2,1)}, bf16[256,768]{1,0:T(8,128)(2,1)}, u32[]{:S(2)}, u32[]{:S(2)}) %collective-permute-start.51) | collective-permute-done | bytes 393248 | tf_op jit(solution)/shard_map/ppermute | solution.py:401
  246.8 8.4 %collective-permute-done.50 = bf16[256,768]{1,0:T(8,128)(2,1)} collective-permute-done((bf16[256,768]{1,0:T(8,128)(2,1)}, bf16[256,768]{1,0:T(8,128)(2,1)}, u32[]{:S(2)}, u32[]{:S(2)}) %collective-permute-start.50) | collective-permute-done | bytes 393248 | tf_op jit(solution)/shard_map/ppermute | solution.py:401
  256.9 1.9 maximum_convert_fusion
  259.7 9.8 %collective-permute-done.47 = bf16[2,104,1792]{2,1,0:T(8,128)(2,1)S(1)} collective-permute-done((bf16[2,104,1792]{2,1,0:T(8,128)(2,1)}, bf16[2,104,1792]{2,1,0:T(8,128)(2,1)S(1)}, u32[]{:S(2)}, u32[]{:S(2)}) %collective-permute-start.47) | collective-permute-done | bytes 745504 | tf_op jit(solution)/shard_map/ppermute | solution.py:401
  270.5 4.1 %collective-permute-start.48 = (bf16[104,1792]{1,0:T(8,128)(2,1)S(1)}, bf16[104,1792]{1,0:T(8,128)(2,1)S(1)}, u32[]{:S(2)}, u32[]{:S(2)}) collective-permute-start(bf16[104,1792]{1,0:T(8,128)(2,1)S(1)} %fusion.10), channel_id=1, source_target_pairs={{0,2},{1,3},{2,0},{3,1},{4,6},{5,7},{6,4},{7,5},{8,10},{9,11},{10,... | collective-permute-start | bytes 1118216 | tf_op jit(solution)/shard_map/ppermute | solution.py:401
  280.3 7.6 %collective-permute-done.48 = bf16[104,1792]{1,0:T(8,128)(2,1)S(1)} collective-permute-done((bf16[104,1792]{1,0:T(8,128)(2,1)S(1)}, bf16[104,1792]{1,0:T(8,128)(2,1)S(1)}, u32[]{:S(2)}, u32[]{:S(2)}) %collective-permute-start.48) | collective-permute-done | bytes 372768 | tf_op jit(solution)/shard_map/ppermute | solution.py:401
  290.5 8.2 %collective-permute-done.55 = bf16[104,1792]{1,0:T(8,128)(2,1)S(1)} collective-permute-done((bf16[104,1792]{1,0:T(8,128)(2,1)S(1)}, bf16[104,1792]{1,0:T(8,128)(2,1)S(1)}, u32[]{:S(2)}, u32[]{:S(2)}) %collective-permute-start.55) | collective-permute-done | bytes 372768 | tf_op jit(solution)/shard_map/ppermute | solution.py:401
  (262 shorter events, 75.7 us)
Async XLA Ops:
  4.2 13.3 %collective-permute-start.1 = (bf16[96,1024]{1,0:T(8,128)(2,1)S(1)}, bf16[96,1024]{1,0:T(8,128)(2,1)S(1)}, u32[]{:S(2)}, u32[]{:S(2)}) collective-permute-start(bf16[96,1024]{1,0:T(8,128)(2,1)S(1)} %pad.9.refs_0_), channel_id=1, source_target_pairs={{0,2},{1,3},{2,0},{3,1},{4,6},{5,7},{6,4},{7,5},{8,10},{9,11},{10,... | collective-permute-start | bytes 589832 | tf_op jit(solution)/shard_map/ppermute | solution.py:401
  9.9 20.4 %collective-permute-start.2 = (bf16[512,768]{1,0:T(8,128)(2,1)S(1)}, bf16[512,768]{1,0:T(8,128)(2,1)S(1)}, u32[]{:S(2)}, u32[]{:S(2)}) collective-permute-start(bf16[512,768]{1,0:T(8,128)(2,1)S(1)} %dynamic-slice_bitcast_fusion), channel_id=1, source_target_pairs={{0,4},{4,0},{1,5},{5,1},{2,6},{6,2},{3,7},{7,3},{8,12},{12,8},{9,1... | collective-permute-start | bytes 2359304 | tf_op jit(solution)/shard_map/ppermute | solution.py:401
  13.7 16.6 %collective-permute-start.5 = (bf16[200,576]{1,0:T(8,128)(2,1)S(1)}, bf16[200,576]{1,0:T(8,128)(2,1)}, u32[]{:S(2)}, u32[]{:S(2)}) collective-permute-start(bf16[200,576]{1,0:T(8,128)(2,1)S(1)} %fusion.11.refs_3_), channel_id=1, source_target_pairs={{0,8},{8,0},{16,24},{24,16},{1,9},{9,1},{17,25},{25,17},{2,10},{10... | collective-permute-start | bytes 691208 | tf_op jit(solution)/shard_map/ppermute | solution.py:401
  30.4 20.5 %collective-permute-start.7 = (bf16[4,96,1024]{2,1,0:T(8,128)(2,1)}, bf16[4,96,1024]{2,1,0:T(8,128)(2,1)S(1)}, u32[]{:S(2)}, u32[]{:S(2)}) collective-permute-start(bf16[4,96,1024]{2,1,0:T(8,128)(2,1)} %stack_pieces.2.refs_8_.refs_7_), channel_id=1, source_target_pairs={{0,4},{4,0},{1,5},{5,1},{2,6},{6,2},{3,7},{7,3},{8,12},{12,8},{9,1... | collective-permute-start | bytes 2359304 | tf_op jit(solution)/shard_map/ppermute | solution.py:401
  31.0 19.9 %collective-permute-start.8 = (bf16[4,96,1024]{2,1,0:T(8,128)(2,1)}, bf16[4,96,1024]{2,1,0:T(8,128)(2,1)S(1)}, u32[]{:S(2)}, u32[]{:S(2)}) collective-permute-start(bf16[4,96,1024]{2,1,0:T(8,128)(2,1)} %stack_pieces.2.refs_8_.refs_7_), channel_id=1, source_target_pairs={{0,16},{8,24},{16,0},{24,8},{1,17},{9,25},{17,1},{25,9},{2,18},{10... | collective-permute-start | bytes 2359304 | tf_op jit(solution)/shard_map/ppermute | solution.py:401
  32.5 18.3 %collective-permute-start.10 = (bf16[104,768]{1,0:T(8,128)(2,1)S(1)}, bf16[104,768]{1,0:T(8,128)(2,1)}, u32[]{:S(2)}, u32[]{:S(2)}) collective-permute-start(bf16[104,768]{1,0:T(8,128)(2,1)S(1)} %maximum_maximum_fusion.refs_0_), channel_id=1, source_target_pairs={{0,2},{1,3},{2,0},{3,1},{4,6},{5,7},{6,4},{7,5},{8,10},{9,11},{10,... | collective-permute-start | bytes 479240 | tf_op jit(solution)/shard_map/ppermute | solution.py:401
  33.9 16.9 %collective-permute-start.11 = (bf16[104,768]{1,0:T(8,128)(2,1)S(1)}, bf16[104,768]{1,0:T(8,128)(2,1)}, u32[]{:S(2)}, u32[]{:S(2)}) collective-permute-start(bf16[104,768]{1,0:T(8,128)(2,1)S(1)} %maximum_maximum_fusion.refs_0_), channel_id=1, source_target_pairs={{0,3},{1,2},{2,1},{3,0},{4,7},{5,6},{6,5},{7,4},{8,11},{9,10},{10,... | collective-permute-start | bytes 479240 | tf_op jit(solution)/shard_map/ppermute | solution.py:401
  35.3 15.6 %collective-permute-start.9 = (bf16[104,768]{1,0:T(8,128)(2,1)S(1)}, bf16[104,768]{1,0:T(8,128)(2,1)}, u32[]{:S(2)}, u32[]{:S(2)}) collective-permute-start(bf16[104,768]{1,0:T(8,128)(2,1)S(1)} %maximum_maximum_fusion.refs_0_), channel_id=1, source_target_pairs={{0,1},{1,0},{2,3},{3,2},{4,5},{5,4},{6,7},{7,6},{8,9},{9,8},{10,11... | collective-permute-start | bytes 479240 | tf_op jit(solution)/shard_map/ppermute | solution.py:401
  50.9 18.2 %collective-permute-start.12 = (bf16[4,96,1024]{2,1,0:T(8,128)(2,1)S(1)}, bf16[4,96,1024]{2,1,0:T(8,128)(2,1)S(1)}, u32[]{:S(2)}, u32[]{:S(2)}) collective-permute-start(bf16[4,96,1024]{2,1,0:T(8,128)(2,1)S(1)} %collective-permute-done.7.refs_9_.refs_8_), channel_id=1, source_target_pairs={{0,16},{8,24},{16,0},{24,8},{1,17},{9,25},{17,1},{25,9},{2,18},{10... | collective-permute-start | bytes 2359304 | tf_op jit(solution)/shard_map/ppermute | solution.py:401
  54.4 14.8 %collective-permute-start.15 = (bf16[256,192]{1,0:T(8,128)(2,1)}, bf16[256,192]{1,0:T(8,128)(2,1)}, u32[]{:S(2)}, u32[]{:S(2)}) collective-permute-start(bf16[256,192]{1,0:T(8,128)(2,1)} %get-tuple-element.148.refs_8_), channel_id=1, source_target_pairs={{0,6},{1,7},{2,0},{3,1},{4,4},{5,5},{6,2},{7,3},{8,14},{9,15},{10,... | collective-permute-start | bytes 294920 | tf_op jit(solution)/shard_map/ppermute | solution.py:417
  70.2 16.7 %collective-permute-start.21 = (bf16[4,104,768]{2,1,0:T(8,128)(2,1)}, bf16[4,104,768]{2,1,0:T(8,128)(2,1)}, u32[]{:S(2)}, u32[]{:S(2)}) collective-permute-start(bf16[4,104,768]{2,1,0:T(8,128)(2,1)} %stack_pieces.3.refs_7_.refs_15_), channel_id=1, source_target_pairs={{0,4},{4,0},{1,5},{5,1},{2,6},{6,2},{3,7},{7,3},{8,12},{12,8},{9,1... | collective-permute-start | bytes 1916936 | tf_op jit(solution)/shard_map/ppermute | solution.py:401
  71.5 16.6 %collective-permute-start.22 = (bf16[4,104,768]{2,1,0:T(8,128)(2,1)}, bf16[4,104,768]{2,1,0:T(8,128)(2,1)S(1)}, u32[]{:S(2)}, u32[]{:S(2)}) collective-permute-start(bf16[4,104,768]{2,1,0:T(8,128)(2,1)} %stack_pieces.3.refs_7_.refs_15_), channel_id=1, source_target_pairs={{0,16},{8,24},{16,0},{24,8},{1,17},{9,25},{17,1},{25,9},{2,18},{10... | collective-permute-start | bytes 1916936 | tf_op jit(solution)/shard_map/ppermute | solution.py:401
  73.1 15.1 %collective-permute-start.23 = (bf16[4,104,768]{2,1,0:T(8,128)(2,1)}, bf16[4,104,768]{2,1,0:T(8,128)(2,1)}, u32[]{:S(2)}, u32[]{:S(2)}) collective-permute-start(bf16[4,104,768]{2,1,0:T(8,128)(2,1)} %stack_pieces.3.refs_7_.refs_15_), channel_id=1, source_target_pairs={{0,8},{8,0},{16,24},{24,16},{1,9},{9,1},{17,25},{25,17},{2,10},{10... | collective-permute-start | bytes 1916936 | tf_op jit(solution)/shard_map/ppermute | solution.py:401
  118.8 13.2 %collective-permute-start.31 = (bf16[6,264,768]{2,1,0:T(8,128)(2,1)}, bf16[6,264,768]{2,1,0:T(8,128)(2,1)S(1)}, u32[]{:S(2)}, u32[]{:S(2)}) collective-permute-start(bf16[6,264,768]{2,1,0:T(8,128)(2,1)} %get-tuple-element.175.refs_4_), channel_id=1, source_target_pairs={{0,8},{8,0},{16,24},{24,16},{1,9},{9,1},{17,25},{25,17},{2,10},{10... | collective-permute-start | bytes 7299080 | tf_op jit(solution)/shard_map/ppermute | solution.py:401
  119.0 24.8 %collective-permute-start.32 = (bf16[256,192]{1,0:T(8,128)(2,1)}, bf16[256,192]{1,0:T(8,128)(2,1)S(1)}, u32[]{:S(2)}, u32[]{:S(2)}) collective-permute-start(bf16[256,192]{1,0:T(8,128)(2,1)} %get-tuple-element.179), channel_id=1, source_target_pairs={{0,0},{1,1},{6,2},{7,3},{2,4},{3,5},{4,6},{5,7},{8,8},{9,9},{14,10... | collective-permute-start | bytes 294920 | tf_op jit(solution)/shard_map/ppermute | solution.py:417
  120.6 23.3 %collective-permute-start.33 = (bf16[256,192]{1,0:T(8,128)(2,1)}, bf16[256,192]{1,0:T(8,128)(2,1)S(1)}, u32[]{:S(2)}, u32[]{:S(2)}) collective-permute-start(bf16[256,192]{1,0:T(8,128)(2,1)} %get-tuple-element.180), channel_id=1, source_target_pairs={{1,0},{0,1},{7,2},{6,3},{3,4},{2,5},{5,6},{4,7},{9,8},{8,9},{15,10... | collective-permute-start | bytes 294920 | tf_op jit(solution)/shard_map/ppermute | solution.py:417
  122.7 21.1 %collective-permute-start.34 = (bf16[256,192]{1,0:T(8,128)(2,1)}, bf16[256,192]{1,0:T(8,128)(2,1)}, u32[]{:S(2)}, u32[]{:S(2)}) collective-permute-start(bf16[256,192]{1,0:T(8,128)(2,1)} %get-tuple-element.181), channel_id=1, source_target_pairs={{6,0},{7,1},{0,2},{1,3},{4,4},{5,5},{2,6},{3,7},{14,8},{15,9},{8,1... | collective-permute-start | bytes 294920 | tf_op jit(solution)/shard_map/ppermute | solution.py:417
  128.7 15.1 %collective-permute-start.35 = (bf16[256,192]{1,0:T(8,128)(2,1)}, bf16[256,192]{1,0:T(8,128)(2,1)}, u32[]{:S(2)}, u32[]{:S(2)}) collective-permute-start(bf16[256,192]{1,0:T(8,128)(2,1)} %get-tuple-element.182), channel_id=1, source_target_pairs={{7,0},{6,1},{1,2},{0,3},{5,4},{4,5},{3,6},{2,7},{15,8},{14,9},{9,1... | collective-permute-start | bytes 294920 | tf_op jit(solution)/shard_map/ppermute | solution.py:417
  132.0 33.3 %collective-permute-start.36 = (bf16[256,768]{1,0:T(8,128)(2,1)}, bf16[256,768]{1,0:T(8,128)(2,1)S(1)}, u32[]{:S(2)}, u32[]{:S(2)}) collective-permute-start(bf16[256,768]{1,0:T(8,128)(2,1)} %get-tuple-element.183), channel_id=1, source_target_pairs={{0,1},{1,0},{2,3},{3,2},{4,5},{5,4},{6,7},{7,6},{8,9},{9,8},{10,11... | collective-permute-start | bytes 1179656 | tf_op jit(solution)/shard_map/ppermute | solution.py:401
  143.9 21.4 %collective-permute-start.37 = (bf16[256,768]{1,0:T(8,128)(2,1)S(1)}, bf16[256,768]{1,0:T(8,128)(2,1)S(1)}, u32[]{:S(2)}, u32[]{:S(2)}) collective-permute-start(bf16[256,768]{1,0:T(8,128)(2,1)S(1)} %copy-done.21), channel_id=1, source_target_pairs={{0,2},{1,3},{2,0},{3,1},{4,6},{5,7},{6,4},{7,5},{8,10},{9,11},{10,... | collective-permute-start | bytes 1179656 | tf_op jit(solution)/shard_map/ppermute | solution.py:401
  143.9 56.5 %collective-permute-start.39 = (bf16[2,4,104,512]{3,2,1,0:T(8,128)(2,1)}, bf16[2,4,104,512]{3,2,1,0:T(8,128)(2,1)}, u32[]{:S(2)}, u32[]{:S(2)}) collective-permute-start(bf16[2,4,104,512]{3,2,1,0:T(8,128)(2,1)} %get-tuple-element.200), channel_id=1, source_target_pairs={{0,4},{4,0},{1,5},{5,1},{2,6},{6,2},{3,7},{7,3},{8,12},{12,8},{9,1... | collective-permute-start | bytes 2555912 | tf_op jit(solution)/shard_map/ppermute | solution.py:401
  147.4 54.1 %collective-permute-start.38 = (bf16[2,4,104,1280]{3,2,1,0:T(8,128)(2,1)}, bf16[2,4,104,1280]{3,2,1,0:T(8,128)(2,1)}, u32[]{:S(2)}, u32[]{:S(2)}) collective-permute-start(bf16[2,4,104,1280]{3,2,1,0:T(8,128)(2,1)} %get-tuple-element.197), channel_id=1, source_target_pairs={{0,16},{8,24},{16,0},{24,8},{1,17},{9,25},{17,1},{25,9},{2,18},{10... | collective-permute-start | bytes 6389768 | tf_op jit(solution)/shard_map/ppermute | solution.py:401
  167.0 36.2 %collective-permute-start.41 = (bf16[256,768]{1,0:T(8,128)(2,1)}, bf16[256,768]{1,0:T(8,128)(2,1)}, u32[]{:S(2)}, u32[]{:S(2)}) collective-permute-start(bf16[256,768]{1,0:T(8,128)(2,1)} %get-tuple-element.207), channel_id=1, source_target_pairs={{0,1},{1,0},{2,7},{3,6},{4,3},{5,2},{6,5},{7,4},{8,9},{9,8},{10,15... | collective-permute-start | bytes 1179656 | tf_op jit(solution)/shard_map/ppermute | solution.py:417
  167.6 35.6 %collective-permute-start.42 = (bf16[256,768]{1,0:T(8,128)(2,1)}, bf16[256,768]{1,0:T(8,128)(2,1)}, u32[]{:S(2)}, u32[]{:S(2)}) collective-permute-start(bf16[256,768]{1,0:T(8,128)(2,1)} %get-tuple-element.208), channel_id=1, source_target_pairs={{0,6},{1,7},{2,0},{3,1},{4,4},{5,5},{6,2},{7,3},{8,14},{9,15},{10,... | collective-permute-start | bytes 1179656 | tf_op jit(solution)/shard_map/ppermute | solution.py:417
  172.3 32.0 %collective-permute-start.43 = (bf16[256,768]{1,0:T(8,128)(2,1)}, bf16[256,768]{1,0:T(8,128)(2,1)}, u32[]{:S(2)}, u32[]{:S(2)}) collective-permute-start(bf16[256,768]{1,0:T(8,128)(2,1)} %get-tuple-element.209), channel_id=1, source_target_pairs={{0,7},{1,6},{2,1},{3,0},{4,5},{5,4},{6,3},{7,2},{8,15},{9,14},{10,... | collective-permute-start | bytes 1179656 | tf_op jit(solution)/shard_map/ppermute | solution.py:417
  204.2 25.8 %collective-permute-start.45 = (bf16[4,104,1280]{2,1,0:T(8,128)(2,1)S(1)}, bf16[4,104,1280]{2,1,0:T(8,128)(2,1)S(1)}, u32[]{:S(2)}, u32[]{:S(2)}) collective-permute-start(bf16[4,104,1280]{2,1,0:T(8,128)(2,1)S(1)} %fusion.3), channel_id=1, source_target_pairs={{0,4},{4,0},{1,5},{5,1},{2,6},{6,2},{3,7},{7,3},{8,12},{12,8},{9,1... | collective-permute-start | bytes 3194888 | tf_op jit(solution)/shard_map/ppermute | solution.py:401
  206.0 24.0 %collective-permute-start.46 = (bf16[4,104,512]{2,1,0:T(8,128)(2,1)S(1)}, bf16[4,104,512]{2,1,0:T(8,128)(2,1)S(1)}, u32[]{:S(2)}, u32[]{:S(2)}) collective-permute-start(bf16[4,104,512]{2,1,0:T(8,128)(2,1)S(1)} %fusion.9), channel_id=1, source_target_pairs={{0,16},{8,24},{16,0},{24,8},{1,17},{9,25},{17,1},{25,9},{2,18},{10... | collective-permute-start | bytes 1277960 | tf_op jit(solution)/shard_map/ppermute | solution.py:401
  210.8 19.2 %collective-permute-start.44 = (bf16[256,768]{1,0:T(8,128)(2,1)}, bf16[256,768]{1,0:T(8,128)(2,1)}, u32[]{:S(2)}, u32[]{:S(2)}) collective-permute-start(bf16[256,768]{1,0:T(8,128)(2,1)} %add_convert_fusion.2), channel_id=1, source_target_pairs={{0,2},{1,3},{2,0},{3,1},{4,6},{5,7},{6,4},{7,5},{8,10},{9,11},{10,... | collective-permute-start | bytes 1179656 | tf_op jit(solution)/shard_map/ppermute | solution.py:401
  236.5 18.7 %collective-permute-start.50 = (bf16[256,768]{1,0:T(8,128)(2,1)}, bf16[256,768]{1,0:T(8,128)(2,1)}, u32[]{:S(2)}, u32[]{:S(2)}) collective-permute-start(bf16[256,768]{1,0:T(8,128)(2,1)} %add_convert_fusion.2), channel_id=1, source_target_pairs={{0,1},{1,0},{2,3},{3,2},{4,5},{5,4},{6,7},{7,6},{8,9},{9,8},{10,11... | collective-permute-start | bytes 1179656 | tf_op jit(solution)/shard_map/ppermute | solution.py:401
  236.6 32.9 %collective-permute-start.47 = (bf16[2,104,1792]{2,1,0:T(8,128)(2,1)}, bf16[2,104,1792]{2,1,0:T(8,128)(2,1)S(1)}, u32[]{:S(2)}, u32[]{:S(2)}) collective-permute-start(bf16[2,104,1792]{2,1,0:T(8,128)(2,1)} %fusion.2), channel_id=1, source_target_pairs={{0,1},{1,0},{2,3},{3,2},{4,5},{5,4},{6,7},{7,6},{8,9},{9,8},{10,11... | collective-permute-start | bytes 2236424 | tf_op jit(solution)/shard_map/ppermute | solution.py:401
  238.6 20.2 %collective-permute-start.52 = (bf16[2,200,640]{2,1,0:T(8,128)(2,1)}, bf16[2,200,640]{2,1,0:T(8,128)(2,1)S(1)}, u32[]{:S(2)}, u32[]{:S(2)}) collective-permute-start(bf16[2,200,640]{2,1,0:T(8,128)(2,1)} %get-tuple-element.225), channel_id=1, source_target_pairs={{0,8},{8,0},{16,24},{24,16},{1,9},{9,1},{17,25},{25,17},{2,10},{10... | collective-permute-start | bytes 1536008 | tf_op jit(solution)/shard_map/ppermute | solution.py:401
  270.5 17.4 %collective-permute-start.48 = (bf16[104,1792]{1,0:T(8,128)(2,1)S(1)}, bf16[104,1792]{1,0:T(8,128)(2,1)S(1)}, u32[]{:S(2)}, u32[]{:S(2)}) collective-permute-start(bf16[104,1792]{1,0:T(8,128)(2,1)S(1)} %fusion.10), channel_id=1, source_target_pairs={{0,2},{1,3},{2,0},{3,1},{4,6},{5,7},{6,4},{7,5},{8,10},{9,11},{10,... | collective-permute-start | bytes 1118216 | tf_op jit(solution)/shard_map/ppermute | solution.py:401
  (80 other events, 782.8 us)

commit v4 on v3

--- a/solution.py
+++ b/solution.py
@@ -815,9 +815,9 @@
                 for side, start in enumerate(starts):
                     part = low(whole[pl.ds(far * shard + start, half), :count])
                     if kind == 0:
-                        kept = mine_down.shape[3]
-                        (mine_down, theirs_down)[side][far, target, :half, :] = part[:, :kept]
-                        (near_up, far_up)[far][side, target, :half, hidden + padded :] = part[:, kept:]
+                        split = hidden - mine_down.shape[3]
+                        (mine_down, theirs_down)[side][far, target, :half, :] = part[:, split:]
+                        (near_up, far_up)[far][side, target, :half, hidden + padded :] = part[:, :split]
                     elif kind == 1:
                         (near_up, far_up)[far][side, target, :half, :hidden] = part
                     else:
@@ -1045,7 +1045,8 @@
         cost_estimate=cost(12 * local_rows * model * width, 8e6),
         name="projection_weights",
     )(meta, tokens, other, grad_full)
-    up_sent, down_sent, kept, sent, *grad_rows = tied(
+    far_out, up_sent, down_sent, kept, sent, *grad_rows = tied(
+        far_out,
         low(wide(near_up[1]) + wide(got_up[1])),
         low(wide(mine_down[1]) + wide(got_down[1])),
         kept,
@@ -1053,10 +1054,6 @@
         *grad_rows,
     )
     second_up, second_down = swapped(up_sent, "ctx", 1), swapped(down_sent, "fsdp", 2)
-    token_rows = resid
-    for part in grad_rows:
-        token_rows = token_rows + wide(part)
-
     def spread_rows(pieces, dtype):
         blocks = [
             lax.select_n(z ^ (2 * x), *[pieces[block ^ place] for place in range(4)]).astype(dtype)
@@ -1064,23 +1061,29 @@
         ]
         return jnp.stack([jnp.concatenate(blocks[2 * seq : 2 * seq + 2]) for seq in range(2)])
 
+    token_rows = resid
+    for part in grad_rows:
+        token_rows = token_rows + wide(part)
+
     token_rows = low(token_rows)
-    far_z, near_z, sent, second_up, second_down = tied(
-        swapped(token_rows, "tp", 2), token_rows, sent, second_up, second_down
-    )
+    far_z, last_out, near_z, sent, second_up, second_down = tied(
+        swapped(token_rows, "tp", 2),
+        swapped(far_out, "tp", 1),
+        token_rows,
+        sent,
+        second_up,
+        second_down,
+    )
+    output_full = spread_rows([output, near_out, far_out, last_out], jnp.bfloat16)
     up_lines = wide(near_up[0]) + wide(got_up[0]) + wide(second_up)
     down_lines = wide(mine_down[0]) + wide(got_down[0]) + wide(second_down)
     lines = jnp.concatenate([up_lines, down_lines], axis=2)
     lines, line_sent = lines[:2], low(lines[2:])
-    lines = lines + wide(swapped(line_sent, "tp", 1))
-    near_z = swapped(near_z, "tp", 1)
-    last_z, _ = tied(far_z, line_sent)
-    last_z = swapped(last_z, "tp", 1)
+    line_got, last_z = tied(swapped(line_sent, "tp", 1), far_z)
+    lines = lines + wide(line_got)
+    near_z, last_z = swapped(near_z, "tp", 1), swapped(last_z, "tp", 1)
     grad_tokens = spread_rows([token_rows, near_z, far_z, last_z], jnp.float32)
-    line_last, far_out = tied(swapped(low(lines[1]), "tp", 2), far_out)
-    output_full = spread_rows(
-        [output, near_out, far_out, swapped(far_out, "tp", 1)], jnp.bfloat16
-    )
+    line_last = swapped(low(lines[1]), "tp", 2)
     total = low(lines[0] + wide(line_last))
     other_half = swapped(total, "ctx", 1)
     small = wide(total[half:])
@@ -1093,8 +1096,7 @@
         )
     )
     grad_w_up = total[:, :hidden]
-    tail = slice(columns_a, columns_a + hidden - first_x)
-    grad_w_down = jnp.concatenate([total[:, tail.stop :], total[:, tail]], axis=1).T
+    grad_w_down = total[:, columns_a:].T
     grad_w_out = total[:, hidden : hidden + width].T
     grad_b_up = small[0, :hidden]
     small_own = small[:, hidden : hidden + shard]

time: 305 us -> 284 us (0.931)
  waiting for transfers between devices: 89.5 us -> 67.6 us
    ppermute x44, waiting for transfers between devices: 83.9 us -> 63.1 us  [swapped(): lax.ppermute(value, axis, [(place, place ^ bit) for place in range(count)])]
  transfers between devices with their start and end apart: 56 -> 56, of which waited for: 21 -> 18; matrix products, arithmetic and copies ran while one was open for 7% -> 8% of each run, Pallas kernels for 21% -> 22%
where the time goes in v4:
time: 284 us; the launch traced here: 282 us
  starting transfers between devices  102 us (36%)
  Pallas kernels  77.1 us (27%)
  waiting for transfers between devices  67.6 us (24%)
  other arithmetic  23.3 us (8%)
  local copies, waits for them, and re-layouts  10.7 us (4%)
    ppermute x44, waiting for transfers between devices, swapped(): lax.ppermute(value, axis, [(place, place ^ bit) for place in range(count)])  63.1 us
    ppermute x12, starting transfers between devices, to_owner(): return lax.ppermute(value, ('ctx', 'tp'), pairs)  53.9 us
    ppermute x44, starting transfers between devices, swapped(): lax.ppermute(value, axis, [(place, place ^ bit) for place in range(count)])  48.3 us
    pallas_call x1, Pallas kernels, attend_back_call(): pl.pallas_call(lambda *refs: attend_back_kernel(*refs, block=block, heads...  17 us
    pallas_call x1, Pallas kernels, per_device_rows(): pl.pallas_call(lambda *refs: second_kernel(*refs, width=width), grid_spec...  14.8 us
    pallas_call x1, Pallas kernels, attend_call(): pl.pallas_call(lambda *refs: attend_kernel(*refs, block=block, heads=head...  14.8 us
    pallas_call x1, Pallas kernels, per_device_rows(): pl.pallas_call(lambda *refs: first_kernel(*refs, width=width), grid_spec=...  10.5 us
    pallas_call x1, Pallas kernels, per_device_rows(): pl.pallas_call(lambda *refs: weights_kernel(*refs, width=width), grid_spe...  10.4 us
  transfers between devices with their start and end apart: 56, of which 18 were waited for; matrix products, arithmetic and copies ran while one was open for 8% of the time, Pallas kernels for 22%

profile of v4, /device:TPU:0, one launch (start us, length us, event | category | flops | bytes accessed | tf_op | source)
XLA Modules:
  0.0 282.5 jit_solution(11716102507178888546)
XLA Ops:
  4.2 4.1 %collective-permute-start.1 = (bf16[96,1024]{1,0:T(8,128)(2,1)S(1)}, bf16[96,1024]{1,0:T(8,128)(2,1)S(1)}, u32[]{:S(2)}, u32[]{:S(2)}) collective-permute-start(bf16[96,1024]{1,0:T(8,128)(2,1)S(1)} %pad.9.refs_0_), channel_id=1, source_target_pairs={{0,2},{1,3},{2,0},{3,1},{4,6},{5,7},{6,4},{7,5},{8,10},{9,11},{10,... | collective-permute-start | bytes 589832 | tf_op jit(solution)/shard_map/ppermute | solution.py:401
  14.3 1.8 fusion.21.refs_0_.meta
  20.8 6.7 %collective-permute-done.4.refs_3_ = bf16[96,1024]{1,0:T(8,128)(2,1)S(1)} collective-permute-done((bf16[96,1024]{1,0:T(8,128)(2,1)S(1)}, bf16[96,1024]{1,0:T(8,128)(2,1)S(1)}, u32[]{:S(2)}, u32[]{:S(2)}) %collective-permute-start.4) | collective-permute-done | bytes 196640 | tf_op jit(solution)/shard_map/ppermute | solution.py:401
  28.2 2.2 stack_pieces.2.refs_8_.refs_7_
  36.0 14.8 %attend.1 = (bf16[1024,576]{1,0:T(8,128)(2,1)}, bf16[256,192]{1,0:T(8,128)(2,1)}, bf16[256,192]{1,0:T(8,128)(2,1)}, bf16[256,192]{1,0:T(8,128)(2,1)}, bf16[256,1...) custom-call(s32[9]{0:T(128)} %fusion.21.refs_0_.meta, ...), custom_call_target="tpu_custom_call" | custom-call | flops 10569646080 | bytes 8000000 | tf_op jit(solution)/shard_map/attend/pallas_call | solution.py:545
  54.4 6.5 %collective-permute-start.15 = (bf16[256,192]{1,0:T(8,128)(2,1)}, bf16[256,192]{1,0:T(8,128)(2,1)}, u32[]{:S(2)}, u32[]{:S(2)}) collective-permute-start(bf16[256,192]{1,0:T(8,128)(2,1)} %get-tuple-element.149.refs_8_), channel_id=1, source_target_pairs={{0,6},{1,7},{2,0},{3,1},{4,4},{5,5},{6,2},{7,3},{8,14},{9,15},{10,... | collective-permute-start | bytes 294920 | tf_op jit(solution)/shard_map/ppermute | solution.py:417
  62.7 2.0 stack_pieces.3.refs_7_.refs_15_
  64.7 4.4 %collective-permute-done.15.refs_3_ = bf16[256,192]{1,0:T(8,128)(2,1)} collective-permute-done((bf16[256,192]{1,0:T(8,128)(2,1)}, bf16[256,192]{1,0:T(8,128)(2,1)}, u32[]{:S(2)}, u32[]{:S(2)}) %collective-permute-start.15) | collective-permute-done | bytes 98336 | tf_op jit(solution)/shard_map/ppermute | solution.py:417
  75.8 10.5 %feed_first.1 = (f32[256,768]{1,0:T(8,128)}, f32[256,1]{1,0:T(8,128)}, bf16[4,256,1024]{2,1,0:T(8,128)(2,1)}, bf16[4,256,768]{2,1,0:T(8,128)(2,1)}) custom-call(s32[9]{0:T(128)} %fusion.21.refs_0_.meta, bf16[256,192]{1,0:T(8,128)(2,1)} %copy-done.37, bf16[256,192]{1,0:T(8,128)(2,1)} %copy-done.38, bf16[256,192]{1,0:T(8,128)(2,1)} %collective-permute-done.15.refs_3_, ...), custom_call_target="tpu_custom_call" | custom-call | flops 1509949440 | bytes 12000000 | tf_op jit(solution)/shard_map/feed_first/pallas_call | solution.py:959
  91.8 7.9 %collective-permute-done.24.refs_18_ = bf16[2,104,768]{2,1,0:T(8,128)(2,1)S(1)} collective-permute-done((bf16[2,104,768]{2,1,0:T(8,128)(2,1)S(1)}, bf16[2,104,768]{2,1,0:T(8,128)(2,1)S(1)}, u32[]{:S(2)}, u32[]{:S(2)}) %collective-permute-start.24) | collective-permute-done | bytes 319520 | tf_op jit(solution)/shard_map/ppermute | solution.py:401
  104.0 14.8 %feed_second.1 = (bf16[256,768]{1,0:T(8,128)(2,1)}, f32[256,768]{1,0:T(8,128)}, bf16[256,192]{1,0:T(8,128)(2,1)}, bf16[256,192]{1,0:T(8,128)(2,1)}, bf16[256,192...) custom-call(s32[9]{0:T(128)} %fusion.21.refs_0_.meta, ...), custom_call_target="tpu_custom_call" | custom-call | flops 3925868544 | bytes 20000000 | tf_op jit(solution)/shard_map/feed_second/pallas_call | solution.py:986
  120.6 2.2 collective-permute-start.33
  122.7 6.0 %collective-permute-start.34 = (bf16[256,192]{1,0:T(8,128)(2,1)}, bf16[256,192]{1,0:T(8,128)(2,1)}, u32[]{:S(2)}, u32[]{:S(2)}) collective-permute-start(bf16[256,192]{1,0:T(8,128)(2,1)} %get-tuple-element.182), channel_id=1, source_target_pairs={{6,0},{7,1},{0,2},{1,3},{4,4},{5,5},{2,6},{3,7},{14,8},{15,9},{8,1... | collective-permute-start | bytes 294920 | tf_op jit(solution)/shard_map/ppermute | solution.py:417
  128.8 3.2 %collective-permute-start.35 = (bf16[256,192]{1,0:T(8,128)(2,1)}, bf16[256,192]{1,0:T(8,128)(2,1)}, u32[]{:S(2)}, u32[]{:S(2)}) collective-permute-start(bf16[256,192]{1,0:T(8,128)(2,1)} %get-tuple-element.183), channel_id=1, source_target_pairs={{7,0},{6,1},{1,2},{0,3},{5,4},{4,5},{3,6},{2,7},{15,8},{14,9},{9,1... | collective-permute-start | bytes 294920 | tf_op jit(solution)/shard_map/ppermute | solution.py:417
  133.4 10.4 %feed_weights.1 = (bf16[2,4,104,1280]{3,2,1,0:T(8,128)(2,1)}, bf16[2,4,104,1280]{3,2,1,0:T(8,128)(2,1)}, bf16[2,4,104,512]{3,2,1,0:T(8,128)(2,1)}, bf16[2,4,104,512]{3,2,1,0:T(8,128)(2,1)}) custom-call(s32[9]{0:T(128)} %fusion.21.refs_0_.meta, bf16[3,2,264,192]{3,2,1,0:T(8,128)(2,1)} %get-tuple-element.174.refs_1_, ...), custom_call_target="tpu_custom_call" | custom-call | flops 2717908992 | bytes 20000000 | tf_op jit(solution)/shard_map/feed_weights/pallas_call | solution.py:1013
  143.9 3.5 %collective-permute-start.39 = (bf16[2,4,104,512]{3,2,1,0:T(8,128)(2,1)}, bf16[2,4,104,512]{3,2,1,0:T(8,128)(2,1)}, u32[]{:S(2)}, u32[]{:S(2)}) collective-permute-start(bf16[2,4,104,512]{3,2,1,0:T(8,128)(2,1)} %get-tuple-element.201), channel_id=1, source_target_pairs={{0,4},{4,0},{1,5},{5,1},{2,6},{6,2},{3,7},{7,3},{8,12},{12,8},{9,1... | collective-permute-start | bytes 2555912 | tf_op jit(solution)/shard_map/ppermute | solution.py:401
  148.2 17.0 %attend_back.1 = (bf16[1024,576]{1,0:T(8,128)(2,1)}, bf16[256,768]{1,0:T(8,128)(2,1)}, bf16[256,768]{1,0:T(8,128)(2,1)}, bf16[256,768]{1,0:T(8,128)(2,1)}, bf16[256,768]{1,0:T(8,128)(2,1)}) custom-call(s32[9]{0:T(128)} %fusion.21.refs_0_.meta, bf16[1024,576]{1,0:T(8,128)(2,1)} %get-tuple-element.185.refs_1_, bf16[256,192]{1,0:T(8,128)(2,1)} %copy-done.52, ...), custom_call_target="tpu_custom_call" | custom-call | flops 24159191040 | bytes 8000000 | tf_op jit(solution)/shard_map/attend_back/pallas_call | solution.py:648
  167.5 4.6 %collective-permute-start.42 = (bf16[256,768]{1,0:T(8,128)(2,1)}, bf16[256,768]{1,0:T(8,128)(2,1)}, u32[]{:S(2)}, u32[]{:S(2)}) collective-permute-start(bf16[256,768]{1,0:T(8,128)(2,1)} %get-tuple-element.209), channel_id=1, source_target_pairs={{0,6},{1,7},{2,0},{3,1},{4,4},{5,5},{6,2},{7,3},{8,14},{9,15},{10,... | collective-permute-start | bytes 1179656 | tf_op jit(solution)/shard_map/ppermute | solution.py:417
  172.2 23.0 %collective-permute-start.43 = (bf16[256,768]{1,0:T(8,128)(2,1)}, bf16[256,768]{1,0:T(8,128)(2,1)S(1)}, u32[]{:S(2)}, u32[]{:S(2)}) collective-permute-start(bf16[256,768]{1,0:T(8,128)(2,1)} %get-tuple-element.210), channel_id=1, source_target_pairs={{0,7},{1,6},{2,1},{3,0},{4,5},{5,4},{6,3},{7,2},{8,15},{9,14},{10,... | collective-permute-start | bytes 1179656 | tf_op jit(solution)/shard_map/ppermute | solution.py:417
  195.2 5.2 %projection_weights.1 = (f32[2,200,640]{2,1,0:T(8,128)}, bf16[2,200,640]{2,1,0:T(8,128)(2,1)}) custom-call(s32[9]{0:T(128)} %fusion.21.refs_0_.meta, bf16[2,512,768]{2,1,0:T(8,128)(2,1)} %own.1, bf16[512,768]{1,0:T(8,128)(2,1)} %copy-done.15, bf16[1024,576]{1,0:T(8,128)(2,1)} %get-tuple-element.204.grads), custom_call_target="tpu_custom_call" | custom-call | flops 905969664 | bytes 8000000 | tf_op jit(solution)/shard_map/projection_weights/pallas_call | solution.py:1034
  201.7 2.5 fusion.3
  205.9 3.7 %collective-permute-start.47 = (bf16[4,104,512]{2,1,0:T(8,128)(2,1)S(1)}, bf16[4,104,512]{2,1,0:T(8,128)(2,1)}, u32[]{:S(2)}, u32[]{:S(2)}) collective-permute-start(bf16[4,104,512]{2,1,0:T(8,128)(2,1)S(1)} %fusion.9), channel_id=1, source_target_pairs={{0,16},{8,24},{16,0},{24,8},{1,17},{9,25},{17,1},{25,9},{2,18},{10... | collective-permute-start | bytes 1277960 | tf_op jit(solution)/shard_map/ppermute | solution.py:401
  211.0 2.9 %collective-permute-start.44 = (bf16[256,768]{1,0:T(8,128)(2,1)S(1)}, bf16[256,768]{1,0:T(8,128)(2,1)}, u32[]{:S(2)}, u32[]{:S(2)}) collective-permute-start(bf16[256,768]{1,0:T(8,128)(2,1)S(1)} %add_convert_fusion.2), channel_id=1, source_target_pairs={{0,2},{1,3},{2,0},{3,1},{4,6},{5,7},{6,4},{7,5},{8,10},{9,11},{10,... | collective-permute-start | bytes 1179656 | tf_op jit(solution)/shard_map/ppermute | solution.py:401
  213.9 16.5 %collective-permute-done.44 = bf16[256,768]{1,0:T(8,128)(2,1)} collective-permute-done((bf16[256,768]{1,0:T(8,128)(2,1)S(1)}, bf16[256,768]{1,0:T(8,128)(2,1)}, u32[]{:S(2)}, u32[]{:S(2)}) %collective-permute-start.44) | collective-permute-done | bytes 393248 | tf_op jit(solution)/shard_map/ppermute | solution.py:401
  233.5 1.9 bitcast_add_fusion
  235.5 1.8 collective-permute-start.49
  242.6 12.6 %collective-permute-done.49 = bf16[2,104,1792]{2,1,0:T(8,128)(2,1)S(1)} collective-permute-done((bf16[2,104,1792]{2,1,0:T(8,128)(2,1)S(1)}, bf16[2,104,1792]{2,1,0:T(8,128)(2,1)S(1)}, u32[]{:S(2)}, u32[]{:S(2)}) %collective-permute-start.49) | collective-permute-done | bytes 745504 | tf_op jit(solution)/shard_map/ppermute | solution.py:401
  256.4 4.1 %collective-permute-start.54 = (bf16[104,1792]{1,0:T(8,128)(2,1)S(1)}, bf16[104,1792]{1,0:T(8,128)(2,1)S(1)}, u32[]{:S(2)}, u32[]{:S(2)}) collective-permute-start(bf16[104,1792]{1,0:T(8,128)(2,1)S(1)} %fusion.10), channel_id=1, source_target_pairs={{0,2},{1,3},{2,0},{3,1},{4,6},{5,7},{6,4},{7,5},{8,10},{9,11},{10,... | collective-permute-start | bytes 1118216 | tf_op jit(solution)/shard_map/ppermute | solution.py:401
  260.5 2.8 collective-permute-start.50
  267.3 4.5 %collective-permute-done.54 = bf16[104,1792]{1,0:T(8,128)(2,1)S(1)} collective-permute-done((bf16[104,1792]{1,0:T(8,128)(2,1)S(1)}, bf16[104,1792]{1,0:T(8,128)(2,1)S(1)}, u32[]{:S(2)}, u32[]{:S(2)}) %collective-permute-start.54) | collective-permute-done | bytes 372768 | tf_op jit(solution)/shard_map/ppermute | solution.py:401
  274.0 3.3 %collective-permute-done.50 = bf16[256,768]{1,0:T(8,128)(2,1)S(1)} collective-permute-done((bf16[256,768]{1,0:T(8,128)(2,1)}, bf16[256,768]{1,0:T(8,128)(2,1)S(1)}, u32[]{:S(2)}, u32[]{:S(2)}) %collective-permute-start.50) | collective-permute-done | bytes 393248 | tf_op jit(solution)/shard_map/ppermute | solution.py:401
  278.6 1.9 maximum_convert_fusion
  (254 shorter events, 71.5 us)
Async XLA Ops:
  9.9 20.4 %collective-permute-start.2 = (bf16[512,768]{1,0:T(8,128)(2,1)S(1)}, bf16[512,768]{1,0:T(8,128)(2,1)S(1)}, u32[]{:S(2)}, u32[]{:S(2)}) collective-permute-start(bf16[512,768]{1,0:T(8,128)(2,1)S(1)} %dynamic-slice_bitcast_fusion), channel_id=1, source_target_pairs={{0,4},{4,0},{1,5},{5,1},{2,6},{6,2},{3,7},{7,3},{8,12},{12,8},{9,1... | collective-permute-start | bytes 2359304 | tf_op jit(solution)/shard_map/ppermute | solution.py:401
  13.7 16.7 %collective-permute-start.5 = (bf16[200,576]{1,0:T(8,128)(2,1)S(1)}, bf16[200,576]{1,0:T(8,128)(2,1)}, u32[]{:S(2)}, u32[]{:S(2)}) collective-permute-start(bf16[200,576]{1,0:T(8,128)(2,1)S(1)} %fusion.11.refs_3_), channel_id=1, source_target_pairs={{0,8},{8,0},{16,24},{24,16},{1,9},{9,1},{17,25},{25,17},{2,10},{10... | collective-permute-start | bytes 691208 | tf_op jit(solution)/shard_map/ppermute | solution.py:401
  30.4 20.5 %collective-permute-start.7 = (bf16[4,96,1024]{2,1,0:T(8,128)(2,1)}, bf16[4,96,1024]{2,1,0:T(8,128)(2,1)S(1)}, u32[]{:S(2)}, u32[]{:S(2)}) collective-permute-start(bf16[4,96,1024]{2,1,0:T(8,128)(2,1)} %stack_pieces.2.refs_8_.refs_7_), channel_id=1, source_target_pairs={{0,4},{4,0},{1,5},{5,1},{2,6},{6,2},{3,7},{7,3},{8,12},{12,8},{9,1... | collective-permute-start | bytes 2359304 | tf_op jit(solution)/shard_map/ppermute | solution.py:401
  31.0 19.9 %collective-permute-start.8 = (bf16[4,96,1024]{2,1,0:T(8,128)(2,1)}, bf16[4,96,1024]{2,1,0:T(8,128)(2,1)S(1)}, u32[]{:S(2)}, u32[]{:S(2)}) collective-permute-start(bf16[4,96,1024]{2,1,0:T(8,128)(2,1)} %stack_pieces.2.refs_8_.refs_7_), channel_id=1, source_target_pairs={{0,16},{8,24},{16,0},{24,8},{1,17},{9,25},{17,1},{25,9},{2,18},{10... | collective-permute-start | bytes 2359304 | tf_op jit(solution)/shard_map/ppermute | solution.py:401
  32.5 18.3 %collective-permute-start.10 = (bf16[104,768]{1,0:T(8,128)(2,1)S(1)}, bf16[104,768]{1,0:T(8,128)(2,1)}, u32[]{:S(2)}, u32[]{:S(2)}) collective-permute-start(bf16[104,768]{1,0:T(8,128)(2,1)S(1)} %maximum_maximum_fusion.refs_0_), channel_id=1, source_target_pairs={{0,2},{1,3},{2,0},{3,1},{4,6},{5,7},{6,4},{7,5},{8,10},{9,11},{10,... | collective-permute-start | bytes 479240 | tf_op jit(solution)/shard_map/ppermute | solution.py:401
  33.9 16.9 %collective-permute-start.11 = (bf16[104,768]{1,0:T(8,128)(2,1)S(1)}, bf16[104,768]{1,0:T(8,128)(2,1)}, u32[]{:S(2)}, u32[]{:S(2)}) collective-permute-start(bf16[104,768]{1,0:T(8,128)(2,1)S(1)} %maximum_maximum_fusion.refs_0_), channel_id=1, source_target_pairs={{0,3},{1,2},{2,1},{3,0},{4,7},{5,6},{6,5},{7,4},{8,11},{9,10},{10,... | collective-permute-start | bytes 479240 | tf_op jit(solution)/shard_map/ppermute | solution.py:401
  35.3 15.6 %collective-permute-start.9 = (bf16[104,768]{1,0:T(8,128)(2,1)S(1)}, bf16[104,768]{1,0:T(8,128)(2,1)}, u32[]{:S(2)}, u32[]{:S(2)}) collective-permute-start(bf16[104,768]{1,0:T(8,128)(2,1)S(1)} %maximum_maximum_fusion.refs_0_), channel_id=1, source_target_pairs={{0,1},{1,0},{2,3},{3,2},{4,5},{5,4},{6,7},{7,6},{8,9},{9,8},{10,11... | collective-permute-start | bytes 479240 | tf_op jit(solution)/shard_map/ppermute | solution.py:401
  50.9 18.2 %collective-permute-start.12 = (bf16[4,96,1024]{2,1,0:T(8,128)(2,1)S(1)}, bf16[4,96,1024]{2,1,0:T(8,128)(2,1)S(1)}, u32[]{:S(2)}, u32[]{:S(2)}) collective-permute-start(bf16[4,96,1024]{2,1,0:T(8,128)(2,1)S(1)} %collective-permute-done.7.refs_9_.refs_8_), channel_id=1, source_target_pairs={{0,16},{8,24},{16,0},{24,8},{1,17},{9,25},{17,1},{25,9},{2,18},{10... | collective-permute-start | bytes 2359304 | tf_op jit(solution)/shard_map/ppermute | solution.py:401
  54.4 14.8 %collective-permute-start.15 = (bf16[256,192]{1,0:T(8,128)(2,1)}, bf16[256,192]{1,0:T(8,128)(2,1)}, u32[]{:S(2)}, u32[]{:S(2)}) collective-permute-start(bf16[256,192]{1,0:T(8,128)(2,1)} %get-tuple-element.149.refs_8_), channel_id=1, source_target_pairs={{0,6},{1,7},{2,0},{3,1},{4,4},{5,5},{6,2},{7,3},{8,14},{9,15},{10,... | collective-permute-start | bytes 294920 | tf_op jit(solution)/shard_map/ppermute | solution.py:417
  70.3 16.7 %collective-permute-start.21 = (bf16[4,104,768]{2,1,0:T(8,128)(2,1)}, bf16[4,104,768]{2,1,0:T(8,128)(2,1)}, u32[]{:S(2)}, u32[]{:S(2)}) collective-permute-start(bf16[4,104,768]{2,1,0:T(8,128)(2,1)} %stack_pieces.3.refs_7_.refs_15_), channel_id=1, source_target_pairs={{0,4},{4,0},{1,5},{5,1},{2,6},{6,2},{3,7},{7,3},{8,12},{12,8},{9,1... | collective-permute-start | bytes 1916936 | tf_op jit(solution)/shard_map/ppermute | solution.py:401
  71.5 16.6 %collective-permute-start.22 = (bf16[4,104,768]{2,1,0:T(8,128)(2,1)}, bf16[4,104,768]{2,1,0:T(8,128)(2,1)S(1)}, u32[]{:S(2)}, u32[]{:S(2)}) collective-permute-start(bf16[4,104,768]{2,1,0:T(8,128)(2,1)} %stack_pieces.3.refs_7_.refs_15_), channel_id=1, source_target_pairs={{0,16},{8,24},{16,0},{24,8},{1,17},{9,25},{17,1},{25,9},{2,18},{10... | collective-permute-start | bytes 1916936 | tf_op jit(solution)/shard_map/ppermute | solution.py:401
  73.1 15.1 %collective-permute-start.23 = (bf16[4,104,768]{2,1,0:T(8,128)(2,1)}, bf16[4,104,768]{2,1,0:T(8,128)(2,1)}, u32[]{:S(2)}, u32[]{:S(2)}) collective-permute-start(bf16[4,104,768]{2,1,0:T(8,128)(2,1)} %stack_pieces.3.refs_7_.refs_15_), channel_id=1, source_target_pairs={{0,8},{8,0},{16,24},{24,16},{1,9},{9,1},{17,25},{25,17},{2,10},{10... | collective-permute-start | bytes 1916936 | tf_op jit(solution)/shard_map/ppermute | solution.py:401
  119.0 24.8 %collective-permute-start.32 = (bf16[256,192]{1,0:T(8,128)(2,1)}, bf16[256,192]{1,0:T(8,128)(2,1)S(1)}, u32[]{:S(2)}, u32[]{:S(2)}) collective-permute-start(bf16[256,192]{1,0:T(8,128)(2,1)} %get-tuple-element.180), channel_id=1, source_target_pairs={{0,0},{1,1},{6,2},{7,3},{2,4},{3,5},{4,6},{5,7},{8,8},{9,9},{14,10... | collective-permute-start | bytes 294920 | tf_op jit(solution)/shard_map/ppermute | solution.py:417
  120.6 23.2 %collective-permute-start.33 = (bf16[256,192]{1,0:T(8,128)(2,1)}, bf16[256,192]{1,0:T(8,128)(2,1)S(1)}, u32[]{:S(2)}, u32[]{:S(2)}) collective-permute-start(bf16[256,192]{1,0:T(8,128)(2,1)} %get-tuple-element.181), channel_id=1, source_target_pairs={{1,0},{0,1},{7,2},{6,3},{3,4},{2,5},{5,6},{4,7},{9,8},{8,9},{15,10... | collective-permute-start | bytes 294920 | tf_op jit(solution)/shard_map/ppermute | solution.py:417
  122.7 21.1 %collective-permute-start.34 = (bf16[256,192]{1,0:T(8,128)(2,1)}, bf16[256,192]{1,0:T(8,128)(2,1)}, u32[]{:S(2)}, u32[]{:S(2)}) collective-permute-start(bf16[256,192]{1,0:T(8,128)(2,1)} %get-tuple-element.182), channel_id=1, source_target_pairs={{6,0},{7,1},{0,2},{1,3},{4,4},{5,5},{2,6},{3,7},{14,8},{15,9},{8,1... | collective-permute-start | bytes 294920 | tf_op jit(solution)/shard_map/ppermute | solution.py:417
  128.8 15.1 %collective-permute-start.35 = (bf16[256,192]{1,0:T(8,128)(2,1)}, bf16[256,192]{1,0:T(8,128)(2,1)}, u32[]{:S(2)}, u32[]{:S(2)}) collective-permute-start(bf16[256,192]{1,0:T(8,128)(2,1)} %get-tuple-element.183), channel_id=1, source_target_pairs={{7,0},{6,1},{1,2},{0,3},{5,4},{4,5},{3,6},{2,7},{15,8},{14,9},{9,1... | collective-permute-start | bytes 294920 | tf_op jit(solution)/shard_map/ppermute | solution.py:417
  132.0 33.3 %collective-permute-start.36 = (bf16[256,768]{1,0:T(8,128)(2,1)}, bf16[256,768]{1,0:T(8,128)(2,1)S(1)}, u32[]{:S(2)}, u32[]{:S(2)}) collective-permute-start(bf16[256,768]{1,0:T(8,128)(2,1)} %get-tuple-element.184), channel_id=1, source_target_pairs={{0,1},{1,0},{2,3},{3,2},{4,5},{5,4},{6,7},{7,6},{8,9},{9,8},{10,11... | collective-permute-start | bytes 1179656 | tf_op jit(solution)/shard_map/ppermute | solution.py:401
  143.9 21.4 %collective-permute-start.37 = (bf16[256,768]{1,0:T(8,128)(2,1)S(1)}, bf16[256,768]{1,0:T(8,128)(2,1)}, u32[]{:S(2)}, u32[]{:S(2)}) collective-permute-start(bf16[256,768]{1,0:T(8,128)(2,1)S(1)} %copy-done.19), channel_id=1, source_target_pairs={{0,2},{1,3},{2,0},{3,1},{4,6},{5,7},{6,4},{7,5},{8,10},{9,11},{10,... | collective-permute-start | bytes 1179656 | tf_op jit(solution)/shard_map/ppermute | solution.py:401
  143.9 56.5 %collective-permute-start.39 = (bf16[2,4,104,512]{3,2,1,0:T(8,128)(2,1)}, bf16[2,4,104,512]{3,2,1,0:T(8,128)(2,1)}, u32[]{:S(2)}, u32[]{:S(2)}) collective-permute-start(bf16[2,4,104,512]{3,2,1,0:T(8,128)(2,1)} %get-tuple-element.201), channel_id=1, source_target_pairs={{0,4},{4,0},{1,5},{5,1},{2,6},{6,2},{3,7},{7,3},{8,12},{12,8},{9,1... | collective-permute-start | bytes 2555912 | tf_op jit(solution)/shard_map/ppermute | solution.py:401
  147.4 54.3 %collective-permute-start.38 = (bf16[2,4,104,1280]{3,2,1,0:T(8,128)(2,1)}, bf16[2,4,104,1280]{3,2,1,0:T(8,128)(2,1)}, u32[]{:S(2)}, u32[]{:S(2)}) collective-permute-start(bf16[2,4,104,1280]{3,2,1,0:T(8,128)(2,1)} %get-tuple-element.199), channel_id=1, source_target_pairs={{0,16},{8,24},{16,0},{24,8},{1,17},{9,25},{17,1},{25,9},{2,18},{10... | collective-permute-start | bytes 6389768 | tf_op jit(solution)/shard_map/ppermute | solution.py:401
  166.9 37.3 %collective-permute-start.41 = (bf16[256,768]{1,0:T(8,128)(2,1)}, bf16[256,768]{1,0:T(8,128)(2,1)}, u32[]{:S(2)}, u32[]{:S(2)}) collective-permute-start(bf16[256,768]{1,0:T(8,128)(2,1)} %get-tuple-element.208), channel_id=1, source_target_pairs={{0,1},{1,0},{2,7},{3,6},{4,3},{5,2},{6,5},{7,4},{8,9},{9,8},{10,15... | collective-permute-start | bytes 1179656 | tf_op jit(solution)/shard_map/ppermute | solution.py:417
  167.5 36.7 %collective-permute-start.42 = (bf16[256,768]{1,0:T(8,128)(2,1)}, bf16[256,768]{1,0:T(8,128)(2,1)}, u32[]{:S(2)}, u32[]{:S(2)}) collective-permute-start(bf16[256,768]{1,0:T(8,128)(2,1)} %get-tuple-element.209), channel_id=1, source_target_pairs={{0,6},{1,7},{2,0},{3,1},{4,4},{5,5},{6,2},{7,3},{8,14},{9,15},{10,... | collective-permute-start | bytes 1179656 | tf_op jit(solution)/shard_map/ppermute | solution.py:417
  172.2 32.0 %collective-permute-start.43 = (bf16[256,768]{1,0:T(8,128)(2,1)}, bf16[256,768]{1,0:T(8,128)(2,1)S(1)}, u32[]{:S(2)}, u32[]{:S(2)}) collective-permute-start(bf16[256,768]{1,0:T(8,128)(2,1)} %get-tuple-element.210), channel_id=1, source_target_pairs={{0,7},{1,6},{2,1},{3,0},{4,5},{5,4},{6,3},{7,2},{8,15},{9,14},{10,... | collective-permute-start | bytes 1179656 | tf_op jit(solution)/shard_map/ppermute | solution.py:417
  204.3 27.8 %collective-permute-start.46 = (bf16[4,104,1280]{2,1,0:T(8,128)(2,1)}, bf16[4,104,1280]{2,1,0:T(8,128)(2,1)}, u32[]{:S(2)}, u32[]{:S(2)}) collective-permute-start(bf16[4,104,1280]{2,1,0:T(8,128)(2,1)} %fusion.3), channel_id=1, source_target_pairs={{0,4},{4,0},{1,5},{5,1},{2,6},{6,2},{3,7},{7,3},{8,12},{12,8},{9,1... | collective-permute-start | bytes 3194888 | tf_op jit(solution)/shard_map/ppermute | solution.py:401
  205.9 26.2 %collective-permute-start.47 = (bf16[4,104,512]{2,1,0:T(8,128)(2,1)S(1)}, bf16[4,104,512]{2,1,0:T(8,128)(2,1)}, u32[]{:S(2)}, u32[]{:S(2)}) collective-permute-start(bf16[4,104,512]{2,1,0:T(8,128)(2,1)S(1)} %fusion.9), channel_id=1, source_target_pairs={{0,16},{8,24},{16,0},{24,8},{1,17},{9,25},{17,1},{25,9},{2,18},{10... | collective-permute-start | bytes 1277960 | tf_op jit(solution)/shard_map/ppermute | solution.py:401
  211.0 19.4 %collective-permute-start.44 = (bf16[256,768]{1,0:T(8,128)(2,1)S(1)}, bf16[256,768]{1,0:T(8,128)(2,1)}, u32[]{:S(2)}, u32[]{:S(2)}) collective-permute-start(bf16[256,768]{1,0:T(8,128)(2,1)S(1)} %add_convert_fusion.2), channel_id=1, source_target_pairs={{0,2},{1,3},{2,0},{3,1},{4,6},{5,7},{6,4},{7,5},{8,10},{9,11},{10,... | collective-permute-start | bytes 1179656 | tf_op jit(solution)/shard_map/ppermute | solution.py:401
  213.9 18.2 %collective-permute-start.45 = (bf16[256,768]{1,0:T(8,128)(2,1)}, bf16[256,768]{1,0:T(8,128)(2,1)}, u32[]{:S(2)}, u32[]{:S(2)}) collective-permute-start(bf16[256,768]{1,0:T(8,128)(2,1)} %collective-permute-done.37), channel_id=1, source_target_pairs={{0,1},{1,0},{2,3},{3,2},{4,5},{5,4},{6,7},{7,6},{8,9},{9,8},{10,11... | collective-permute-start | bytes 1179656 | tf_op jit(solution)/shard_map/ppermute | solution.py:401
  235.5 19.6 %collective-permute-start.49 = (bf16[2,104,1792]{2,1,0:T(8,128)(2,1)S(1)}, bf16[2,104,1792]{2,1,0:T(8,128)(2,1)S(1)}, u32[]{:S(2)}, u32[]{:S(2)}) collective-permute-start(bf16[2,104,1792]{2,1,0:T(8,128)(2,1)S(1)} %fusion.1), channel_id=1, source_target_pairs={{0,1},{1,0},{2,3},{3,2},{4,5},{5,4},{6,7},{7,6},{8,9},{9,8},{10,11... | collective-permute-start | bytes 2236424 | tf_op jit(solution)/shard_map/ppermute | solution.py:401
  237.4 36.6 %collective-permute-start.48 = (bf16[256,768]{1,0:T(8,128)(2,1)S(1)}, bf16[256,768]{1,0:T(8,128)(2,1)S(1)}, u32[]{:S(2)}, u32[]{:S(2)}) collective-permute-start(bf16[256,768]{1,0:T(8,128)(2,1)S(1)} %add_convert_fusion.2), channel_id=1, source_target_pairs={{0,1},{1,0},{2,3},{3,2},{4,5},{5,4},{6,7},{7,6},{8,9},{9,8},{10,11... | collective-permute-start | bytes 1179656 | tf_op jit(solution)/shard_map/ppermute | solution.py:401
  241.3 13.9 %collective-permute-start.52 = (bf16[200,640]{1,0:T(8,128)(2,1)S(1)}, bf16[200,640]{1,0:T(8,128)(2,1)S(1)}, u32[]{:S(2)}, u32[]{:S(2)}) collective-permute-start(bf16[200,640]{1,0:T(8,128)(2,1)S(1)} %fusion.12), channel_id=1, source_target_pairs={{0,16},{8,24},{16,0},{24,8},{1,17},{9,25},{17,1},{25,9},{2,18},{10... | collective-permute-start | bytes 768008 | tf_op jit(solution)/shard_map/ppermute | solution.py:401
  256.4 15.3 %collective-permute-start.54 = (bf16[104,1792]{1,0:T(8,128)(2,1)S(1)}, bf16[104,1792]{1,0:T(8,128)(2,1)S(1)}, u32[]{:S(2)}, u32[]{:S(2)}) collective-permute-start(bf16[104,1792]{1,0:T(8,128)(2,1)S(1)} %fusion.10), channel_id=1, source_target_pairs={{0,2},{1,3},{2,0},{3,1},{4,6},{5,7},{6,4},{7,5},{8,10},{9,11},{10,... | collective-permute-start | bytes 1118216 | tf_op jit(solution)/shard_map/ppermute | solution.py:401
  260.5 16.8 %collective-permute-start.50 = (bf16[256,768]{1,0:T(8,128)(2,1)}, bf16[256,768]{1,0:T(8,128)(2,1)S(1)}, u32[]{:S(2)}, u32[]{:S(2)}) collective-permute-start(bf16[256,768]{1,0:T(8,128)(2,1)} %collective-permute-done.44), channel_id=1, source_target_pairs={{0,1},{1,0},{2,3},{3,2},{4,5},{5,4},{6,7},{7,6},{8,9},{9,8},{10,11... | collective-permute-start | bytes 1179656 | tf_op jit(solution)/shard_map/ppermute | solution.py:401
  (78 other events, 720.8 us)

commit v5 on v4

--- a/solution.py
+++ b/solution.py
@@ -693,8 +693,8 @@
     hidden = up_w.shape[2]
     taken = pieces[0].shape[1]
     copies = piece_copies(meta, pieces, taken, pl.ds(hidden, out_w.shape[2]), out_w, sems, 0)
-    copies += piece_copies(meta, pieces, taken, pl.ds(0, hidden), up_w, sems, 32)
-    for copy in copies:
+    up_copies = piece_copies(meta, pieces, taken, pl.ds(0, hidden), up_w, sems, 32)
+    for copy in copies + up_copies:
         copy.start()
     for step in range(4):
         both[step, :, hidden : hidden + width] = att[step][...]
@@ -708,6 +708,8 @@
     hat[...] = hat_one
     inverse[...] = inverse_one
     normed = low(hat_one * vectors[GAIN_ONE : GAIN_ONE + 1, :] + vectors[SHIFT_ONE : SHIFT_ONE + 1, :])
+    for copy in up_copies:
+        copy.wait()
     for place in range(4):
         inputs = dot32(normed, up_w[place], 1, 0) + wide(lines[meta[1] ^ place, 0:1, :])
         cumulative = 0.5 * (1.0 + lax.erf(inputs * (0.5**0.5)))
@@ -782,58 +784,65 @@
         mixed[4 + far, :, 3 * shard :] = jnp.zeros((rows + EXTRA, hidden - 3 * shard), jnp.bfloat16)
 
 
-def weights_kernel(meta, *refs, width):
-    keep, both, both_sib, mixed, mixed_sib = refs[:5]
-    near_up, far_up, mine_down, theirs_down, turned, whole = refs[5:]
+def slot_of(block, z):
+    apart = block ^ z
+    return 2 * (apart & 1) + (apart >> 1)
+
+
+def weights_kernel(meta, *refs):
+    keep, tail_sib, both, both_sib, att, att_sib, mixed, mixed_sib = refs[:8]
+    near_up, far_up, mine_down, theirs_down, turned, ordered = refs[8:]
     shard = keep.shape[3]
     rows = both.shape[1]
     half = shard // 2
-    hidden = mixed.shape[2]
-    padded = both.shape[2] - hidden
+    hidden, padded = mixed.shape[2], att.shape[2]
     starts = [pl.multiple_of(side * half, half) for side in (meta[0], 1 - meta[0])]
 
-    def slot(block):
-        apart = block ^ meta[1]
-        return 2 * (apart & 1) + (apart >> 1)
-
-    for kind in range(3):
+    @pl.when(pl.program_id(0) == 0)
+    def _():
+        for kind in range(3):
+            for far in range(2):
+                span = slice(far * shard, (far + 1) * shard)
+                turned[span, :rows] = keep[kind, far, :rows, :].T
+                turned[span, rows:] = tail_sib[far, :rows, kind * shard : (kind + 1) * shard].T
+                for side, start in enumerate(starts):
+                    first = (2 * far + side) * half
+                    ordered[kind, first : first + half, :] = turned[
+                        pl.ds(far * shard + start, half), :
+                    ]
+
+    operands = (
+        (both[0], both_sib[0]),
+        (mixed[0, :rows, :], mixed_sib[0, :rows, :]),
+        (att[0], att_sib[0]),
+    )
+    for kind, (left, right) in enumerate(operands):
+        value = dot32(ordered[kind, :, :rows], left, 1, 0)
+        value = value + dot32(ordered[kind, :, rows:], right, 1, 0)
         for far in range(2):
-            span = slice(far * shard, (far + 1) * shard)
-            turned[span, :rows] = keep[kind, far, :rows, :].T
-            turned[span, rows:] = mixed_sib[4 + far, :rows, kind * shard : (kind + 1) * shard].T
-        for place in range(4):
-            if kind == 1:
-                left, right = mixed[place, :rows, :], mixed_sib[place, :rows, :]
-            else:
-                columns = slice(0, hidden) if kind == 0 else slice(hidden, None)
-                left, right = both[place, :, columns], both_sib[place, :, columns]
-            value = dot32(turned[:, :rows], left, 1, 0) + dot32(turned[:, rows:], right, 1, 0)
-            target = slot(meta[4] ^ place if kind == 2 else place)
-            count = value.shape[1]
-            whole[:, :count] = value
-            for far in range(2):
-                for side, start in enumerate(starts):
-                    part = low(whole[pl.ds(far * shard + start, half), :count])
-                    if kind == 0:
-                        split = hidden - mine_down.shape[3]
-                        (mine_down, theirs_down)[side][far, target, :half, :] = part[:, split:]
-                        (near_up, far_up)[far][side, target, :half, hidden + padded :] = part[:, :split]
-                    elif kind == 1:
-                        (near_up, far_up)[far][side, target, :half, :hidden] = part
-                    else:
-                        (near_up, far_up)[far][side, target, :half, hidden : hidden + padded] = part
+            for side in range(2):
+                first = (2 * far + side) * half
+                part = low(value[first : first + half, :])
+                up = (near_up, far_up)[far]
+                if kind == 0:
+                    split = hidden - mine_down.shape[3]
+                    (mine_down, theirs_down)[side][far, 0, :half, :] = part[:, split:]
+                    up[side, 0, :half, hidden + padded :] = part[:, :split]
+                elif kind == 1:
+                    up[side, 0, :half, :hidden] = part
+                else:
+                    up[side, 0, :half, hidden : hidden + padded] = part
+    hidden_sums = low(wide(mixed[0, rows:, :]) + wide(mixed_sib[0, rows:, :]))
     for far in range(2):
-        vector_sums = low(wide(keep[0, far, rows:, :]) + wide(mixed_sib[4 + far, rows:, :shard]))
-        for place in range(4):
-            hidden_sums = low(wide(mixed[place, rows:, :]) + wide(mixed_sib[place, rows:, :]))
-            for side in range(2):
-                out = (mine_down, theirs_down)[side]
-                out[far, place, half:, :] = jnp.zeros((EXTRA, out.shape[3]), jnp.bfloat16)
-                out = (near_up, far_up)[far]
-                out[side, slot(place), half:, :hidden] = hidden_sums
-                out[side, place, half:, hidden : hidden + shard] = vector_sums
-                rest = slice(hidden + shard, None)
-                out[side, place, half:, rest] = jnp.zeros_like(out[side, place, half:, rest])
+        vector_sums = low(wide(keep[0, far, rows:, :]) + wide(tail_sib[far, rows:, :shard]))
+        for side in range(2):
+            out = (mine_down, theirs_down)[side]
+            out[far, 0, half:, :] = jnp.zeros((EXTRA, out.shape[3]), jnp.bfloat16)
+            out = (near_up, far_up)[far]
+            out[side, 0, half:, :hidden] = hidden_sums
+            out[side, 0, half:, hidden : hidden + shard] = vector_sums
+            rest = slice(hidden + shard, None)
+            out[side, 0, half:, rest] = jnp.zeros_like(out[side, 0, half:, rest])
 
 
 def projections_kernel(meta, own, other, grads, kept, sent, whole):
@@ -915,8 +924,9 @@
         ]
     )
     qkv_bias = wide(per_head((b_query, jnp.zeros_like(b_query), b_value)))[None, :]
-    qkv_y, far_a, meta = tied(swapped(qkv_shard, "fsdp", 2), far_a, meta)
-    line_a = stacked([half_a, near_half, far_a, swapped(far_a, "tp", 1)])
+    far_a, meta = tied(far_a, meta)
+    last_a, qkv_y = tied(swapped(far_a, "tp", 1), swapped(qkv_shard, "fsdp", 2))
+    line_a = stacked([half_a, near_half, far_a, last_a])
     qkv_pieces = (qkv_shard, swapped(qkv_shard, "fsdp", 1), qkv_y, swapped(qkv_y, "fsdp", 1))
 
     core = lambda array: swapped(array, "fsdp", 1)
@@ -1010,17 +1020,33 @@
     pack = struct((2, 4, half + EXTRA, first_x))
     pack_up = struct((2, 4, half + EXTRA, columns_a + hidden - first_x))
     mixed_sib = core(mixed)
+    per_block = lambda item, place=lambda block, meta: block, columns=None, lanes=0: pl.BlockSpec(
+        (1, item.shape[1], columns or item.shape[2]),
+        lambda block, meta: (place(block, meta), 0, lanes),
+    )
+    heads_of = lambda block, meta: block ^ meta[4]
+    sent_block = lambda item: pl.BlockSpec(
+        (2, 1) + item.shape[2:], lambda block, meta: (0, slot_of(block, meta[1]), 0, 0)
+    )
     near_up, far_up, mine_down, theirs_down = pl.pallas_call(
-        lambda *refs: weights_kernel(*refs, width=width),
-        grid_spec=grid(
-            specs([keep, both, both_sib, mixed, mixed_sib]),
-            specs([pack_up] * 2 + [pack] * 2),
-            [vm((2 * shard, 2 * rows)), vm((2 * shard, hidden), jnp.float32)],
+        weights_kernel,
+        grid_spec=pltpu.PrefetchScalarGridSpec(
+            num_scalar_prefetch=1,
+            grid=(4,),
+            in_specs=[
+                full(keep.shape),
+                pl.BlockSpec((2,) + mixed.shape[1:], lambda block, meta: (2, 0, 0)),
+                *[per_block(both, columns=hidden)] * 2,
+                *[per_block(both, heads_of, padded, hidden // padded)] * 2,
+                *[per_block(mixed)] * 2,
+            ],
+            out_specs=[sent_block(pack_up)] * 2 + [sent_block(pack)] * 2,
+            scratch_shapes=[vm((2 * shard, 2 * rows)), vm((3, 2 * shard, 2 * rows))],
         ),
         out_shape=[pack_up] * 2 + [pack] * 2,
         cost_estimate=cost(8 * rows * shard * (8 * hidden + 4 * width), 20e6),
         name="feed_weights",
-    )(meta, keep, both, both_sib, mixed, mixed_sib)
+    )(meta, keep, mixed_sib, both, both_sib, both, both_sib, mixed, mixed_sib)
 
     near_out = swapped(output, "tp", 1)
     far_up, theirs_down, output, *grad_att = tied(far_up, theirs_down, output, *grad_att)
@@ -1028,9 +1054,15 @@
     far_out = swapped(output, "tp", 2)
     grad_full, *grad_parts = attend_back_call(meta, qkv, grad_att, parts, stats, weight, heads)
 
-    near_out, far_out, *grad_parts = tied(near_out, far_out, *grad_parts)
+    got_down, near_out, far_out, *grad_parts = tied(got_down, near_out, far_out, *grad_parts)
     grad_rows = [to_owner(part, step) for step, part in enumerate(grad_parts)]
-    grad_full, grad_rows[0] = tied(grad_full, grad_rows[0])
+    far_out, up_sent, down_sent, grad_full, *grad_rows = tied(
+        far_out,
+        low(wide(near_up[1]) + wide(got_up[1])),
+        low(wide(mine_down[1]) + wide(got_down[1])),
+        grad_full,
+        *grad_rows,
+    )
     kept, sent = pl.pallas_call(
         projections_kernel,
         grid_spec=grid(
@@ -1045,14 +1077,6 @@
         cost_estimate=cost(12 * local_rows * model * width, 8e6),
         name="projection_weights",
     )(meta, tokens, other, grad_full)
-    far_out, up_sent, down_sent, kept, sent, *grad_rows = tied(
-        far_out,
-        low(wide(near_up[1]) + wide(got_up[1])),
-        low(wide(mine_down[1]) + wide(got_down[1])),
-        kept,
-        sent,
-        *grad_rows,
-    )
     second_up, second_down = swapped(up_sent, "ctx", 1), swapped(down_sent, "fsdp", 2)
     def spread_rows(pieces, dtype):
         blocks = [

time: 284 us -> 282 us (level)
  waiting for transfers between devices: 67.6 us -> 83.3 us
  starting transfers between devices: 102 us -> 88.6 us
    ppermute x12, starting transfers between devices: 53.9 us -> 35.7 us  [to_owner(): return lax.ppermute(value, ('ctx', 'tp'), pairs)]
    ppermute x44, waiting for transfers between devices: 63.1 us -> 76 us  [swapped(): lax.ppermute(value, axis, [(place, place ^ bit) for place in range(count)])]
    ppermute x44, starting transfers between devices: 48.3 us -> 52.9 us  [swapped(): lax.ppermute(value, axis, [(place, place ^ bit) for place in range(count)])]
    ppermute x12, waiting for transfers between devices: 4.46 us -> 7.34 us  [to_owner(): return lax.ppermute(value, ('ctx', 'tp'), pairs)]
  transfers between devices with their start and end apart: 56 -> 56, of which waited for: 18 -> 25; matrix products, arithmetic and copies ran while one was open for 8% -> 7% of each run, Pallas kernels for 22% -> 21%
where the time goes in v5:
time: 282 us; the launch traced here: 281 us
  starting transfers between devices  88.6 us (31%)
  waiting for transfers between devices  83.3 us (30%)
  Pallas kernels  75.2 us (27%)
  other arithmetic  22.1 us (8%)
  local copies, waits for them, and re-layouts  10.7 us (4%)
    ppermute x44, waiting for transfers between devices, swapped(): lax.ppermute(value, axis, [(place, place ^ bit) for place in range(count)])  76 us
    ppermute x44, starting transfers between devices, swapped(): lax.ppermute(value, axis, [(place, place ^ bit) for place in range(count)])  52.9 us
    ppermute x12, starting transfers between devices, to_owner(): return lax.ppermute(value, ('ctx', 'tp'), pairs)  35.7 us
    pallas_call x1, Pallas kernels, attend_back_call(): pl.pallas_call(lambda *refs: attend_back_kernel(*refs, block=block, heads...  17.2 us
    pallas_call x1, Pallas kernels, per_device_rows(): pl.pallas_call(lambda *refs: second_kernel(*refs, width=width), grid_spec...  14.8 us
    pallas_call x1, Pallas kernels, attend_call(): pl.pallas_call(lambda *refs: attend_kernel(*refs, block=block, heads=head...  14.8 us
    pallas_call x1, Pallas kernels, per_device_rows(): pl.pallas_call(weights_kernel, grid_spec=pltpu.PrefetchScalarGridSpec(num...  9.77 us
    pallas_call x1, Pallas kernels, per_device_rows(): pl.pallas_call(lambda *refs: first_kernel(*refs, width=width), grid_spec=...  9.24 us
  transfers between devices with their start and end apart: 56, of which 25 were waited for; matrix products, arithmetic and copies ran while one was open for 7% of the time, Pallas kernels for 21%

profile of v5, /device:TPU:0, one launch (start us, length us, event | category | flops | bytes accessed | tf_op | source)
XLA Modules:
  0.0 281.4 jit_solution(4540675448847273799)
XLA Ops:
  4.2 4.1 %collective-permute-start = (bf16[96,1024]{1,0:T(8,128)(2,1)S(1)}, bf16[96,1024]{1,0:T(8,128)(2,1)S(1)}, u32[]{:S(2)}, u32[]{:S(2)}) collective-permute-start(bf16[96,1024]{1,0:T(8,128)(2,1)S(1)} %pad.8.refs_0_), channel_id=1, source_target_pairs={{0,2},{1,3},{2,0},{3,1},{4,6},{5,7},{6,4},{7,5},{8,10},{9,11},{10,... | collective-permute-start | bytes 589832 | tf_op jit(solution)/shard_map/ppermute | solution.py:401
  19.3 4.2 %collective-permute-done.3.refs_3_ = bf16[96,1024]{1,0:T(8,128)(2,1)S(1)} collective-permute-done((bf16[96,1024]{1,0:T(8,128)(2,1)S(1)}, bf16[96,1024]{1,0:T(8,128)(2,1)S(1)}, u32[]{:S(2)}, u32[]{:S(2)}) %collective-permute-start.3) | collective-permute-done | bytes 196640 | tf_op jit(solution)/shard_map/ppermute | solution.py:401
  25.3 2.2 stack_pieces.2.refs_8_.refs_7_
  31.7 1.9 collective-permute-start.10
  35.3 14.8 %attend.1 = (bf16[1024,576]{1,0:T(8,128)(2,1)}, bf16[256,192]{1,0:T(8,128)(2,1)}, bf16[256,192]{1,0:T(8,128)(2,1)}, bf16[256,192]{1,0:T(8,128)(2,1)}, bf16[256,1...) custom-call(s32[9]{0:T(128)} %fusion.21.refs_0_.meta, ...), custom_call_target="tpu_custom_call" | custom-call | flops 10569646080 | bytes 8000000 | tf_op jit(solution)/shard_map/attend/pallas_call | solution.py:545
  53.9 7.6 %collective-permute-start.15 = (bf16[256,192]{1,0:T(8,128)(2,1)}, bf16[256,192]{1,0:T(8,128)(2,1)}, u32[]{:S(2)}, u32[]{:S(2)}) collective-permute-start(bf16[256,192]{1,0:T(8,128)(2,1)} %get-tuple-element.149.refs_8_), channel_id=1, source_target_pairs={{0,6},{1,7},{2,0},{3,1},{4,4},{5,5},{6,2},{7,3},{8,14},{9,15},{10,... | collective-permute-start | bytes 294920 | tf_op jit(solution)/shard_map/ppermute | solution.py:417
  62.3 2.0 stack_pieces.3.refs_7_.refs_15_
  64.4 2.7 collective-permute-done.15.refs_3_
  75.7 9.2 %feed_first.1 = (f32[256,768]{1,0:T(8,128)}, f32[256,1]{1,0:T(8,128)}, bf16[4,256,1024]{2,1,0:T(8,128)(2,1)}, bf16[4,256,768]{2,1,0:T(8,128)(2,1)}) custom-call(s32[9]{0:T(128)} %fusion.21.refs_0_.meta, bf16[256,192]{1,0:T(8,128)(2,1)} %copy-done.33, bf16[256,192]{1,0:T(8,128)(2,1)} %copy-done.34, bf16[256,192]{1,0:T(8,128)(2,1)} %collective-permute-done.15.refs_3_, ...), custom_call_target="tpu_custom_call" | custom-call | flops 1509949440 | bytes 12000000 | tf_op jit(solution)/shard_map/feed_first/pallas_call | solution.py:969
  90.8 8.8 %collective-permute-done.24.refs_18_ = bf16[2,104,768]{2,1,0:T(8,128)(2,1)S(1)} collective-permute-done((bf16[2,104,768]{2,1,0:T(8,128)(2,1)S(1)}, bf16[2,104,768]{2,1,0:T(8,128)(2,1)S(1)}, u32[]{:S(2)}, u32[]{:S(2)}) %collective-permute-start.24) | collective-permute-done | bytes 319520 | tf_op jit(solution)/shard_map/ppermute | solution.py:401
  102.9 14.8 %feed_second.1 = (bf16[256,768]{1,0:T(8,128)(2,1)}, f32[256,768]{1,0:T(8,128)}, bf16[256,192]{1,0:T(8,128)(2,1)}, bf16[256,192]{1,0:T(8,128)(2,1)}, bf16[256,192...) custom-call(s32[9]{0:T(128)} %fusion.21.refs_0_.meta, ...), custom_call_target="tpu_custom_call" | custom-call | flops 3925868544 | bytes 20000000 | tf_op jit(solution)/shard_map/feed_second/pallas_call | solution.py:996
  119.5 3.8 %collective-permute-start.33 = (bf16[256,192]{1,0:T(8,128)(2,1)}, bf16[256,192]{1,0:T(8,128)(2,1)S(1)}, u32[]{:S(2)}, u32[]{:S(2)}) collective-permute-start(bf16[256,192]{1,0:T(8,128)(2,1)} %get-tuple-element.181), channel_id=1, source_target_pairs={{1,0},{0,1},{7,2},{6,3},{3,4},{2,5},{5,6},{4,7},{9,8},{8,9},{15,10... | collective-permute-start | bytes 294920 | tf_op jit(solution)/shard_map/ppermute | solution.py:417
  123.3 5.6 %collective-permute-start.34 = (bf16[256,192]{1,0:T(8,128)(2,1)}, bf16[256,192]{1,0:T(8,128)(2,1)S(1)}, u32[]{:S(2)}, u32[]{:S(2)}) collective-permute-start(bf16[256,192]{1,0:T(8,128)(2,1)} %get-tuple-element.182), channel_id=1, source_target_pairs={{6,0},{7,1},{0,2},{1,3},{4,4},{5,5},{2,6},{3,7},{14,8},{15,9},{8,1... | collective-permute-start | bytes 294920 | tf_op jit(solution)/shard_map/ppermute | solution.py:417
  128.9 3.7 %collective-permute-start.35 = (bf16[256,192]{1,0:T(8,128)(2,1)}, bf16[256,192]{1,0:T(8,128)(2,1)S(1)}, u32[]{:S(2)}, u32[]{:S(2)}) collective-permute-start(bf16[256,192]{1,0:T(8,128)(2,1)} %get-tuple-element.183), channel_id=1, source_target_pairs={{7,0},{6,1},{1,2},{0,3},{5,4},{4,5},{3,6},{2,7},{15,8},{14,9},{9,1... | collective-permute-start | bytes 294920 | tf_op jit(solution)/shard_map/ppermute | solution.py:417
  134.0 9.8 %feed_weights.1 = (bf16[2,4,104,1280]{3,2,1,0:T(8,128)(2,1)}, bf16[2,4,104,1280]{3,2,1,0:T(8,128)(2,1)}, bf16[2,4,104,512]{3,2,1,0:T(8,128)(2,1)}, bf16[2,4,104,512]{3,2,1,0:T(8,128)(2,1)}) custom-call(s32[9]{0:T(128)} %fusion.21.refs_0_.meta, bf16[3,2,264,192]{3,2,1,0:T(8,128)(2,1)} %get-tuple-element.174.refs_0_, bf16[6,264,768]{2,1,0:T(8,128)(2,1)} %copy-done.2, ...), custom_call_target="tpu_custom_call" | custom-call | flops 2717908992 | bytes 20000000 | tf_op jit(solution)/shard_map/feed_weights/pallas_call | solution.py:1031
  143.9 3.5 %collective-permute-start.38 = (bf16[256,768]{1,0:T(8,128)(2,1)S(1)}, bf16[256,768]{1,0:T(8,128)(2,1)}, u32[]{:S(2)}, u32[]{:S(2)}) collective-permute-start(bf16[256,768]{1,0:T(8,128)(2,1)S(1)} %copy-done.20), channel_id=1, source_target_pairs={{0,2},{1,3},{2,0},{3,1},{4,6},{5,7},{6,4},{7,5},{8,10},{9,11},{10,... | collective-permute-start | bytes 1179656 | tf_op jit(solution)/shard_map/ppermute | solution.py:401
  148.7 17.2 %attend_back.1 = (bf16[1024,576]{1,0:T(8,128)(2,1)}, bf16[256,768]{1,0:T(8,128)(2,1)}, bf16[256,768]{1,0:T(8,128)(2,1)}, bf16[256,768]{1,0:T(8,128)(2,1)}, bf16[256,768]{1,0:T(8,128)(2,1)}) custom-call(s32[9]{0:T(128)} %fusion.21.refs_0_.meta, bf16[1024,576]{1,0:T(8,128)(2,1)} %get-tuple-element.186.refs_1_, bf16[256,192]{1,0:T(8,128)(2,1)} %copy-done.46, ...), custom_call_target="tpu_custom_call" | custom-call | flops 24159191040 | bytes 8000000 | tf_op jit(solution)/shard_map/attend_back/pallas_call | solution.py:648
  168.2 5.2 %collective-permute-start.42 = (bf16[256,768]{1,0:T(8,128)(2,1)}, bf16[256,768]{1,0:T(8,128)(2,1)S(1)}, u32[]{:S(2)}, u32[]{:S(2)}) collective-permute-start(bf16[256,768]{1,0:T(8,128)(2,1)} %get-tuple-element.206), channel_id=1, source_target_pairs={{0,6},{1,7},{2,0},{3,1},{4,4},{5,5},{6,2},{7,3},{8,14},{9,15},{10,... | collective-permute-start | bytes 1179656 | tf_op jit(solution)/shard_map/ppermute | solution.py:417
  173.4 2.1 collective-permute-start.43
  176.8 17.9 %collective-permute-done.39 = bf16[2,4,104,1280]{3,2,1,0:T(8,128)(2,1)} collective-permute-done((bf16[2,4,104,1280]{3,2,1,0:T(8,128)(2,1)}, bf16[2,4,104,1280]{3,2,1,0:T(8,128)(2,1)}, u32[]{:S(2)}, u32[]{:S(2)}) %collective-permute-start.39) | collective-permute-done | bytes 2129952 | tf_op jit(solution)/shard_map/ppermute | solution.py:401
  194.7 2.5 fusion.3
  197.2 2.8 %collective-permute-done.42 = bf16[256,768]{1,0:T(8,128)(2,1)S(1)} collective-permute-done((bf16[256,768]{1,0:T(8,128)(2,1)}, bf16[256,768]{1,0:T(8,128)(2,1)S(1)}, u32[]{:S(2)}, u32[]{:S(2)}) %collective-permute-start.42) | collective-permute-done | bytes 393248 | tf_op jit(solution)/shard_map/ppermute | solution.py:417
  201.7 10.6 %collective-permute-start.44 = (bf16[256,768]{1,0:T(8,128)(2,1)S(1)}, bf16[256,768]{1,0:T(8,128)(2,1)}, u32[]{:S(2)}, u32[]{:S(2)}) collective-permute-start(bf16[256,768]{1,0:T(8,128)(2,1)S(1)} %add_convert_fusion.2), channel_id=1, source_target_pairs={{0,2},{1,3},{2,0},{3,1},{4,6},{5,7},{6,4},{7,5},{8,10},{9,11},{10,... | collective-permute-start | bytes 1179656 | tf_op jit(solution)/shard_map/ppermute | solution.py:401
  212.2 5.1 %projection_weights.1 = (f32[2,200,640]{2,1,0:T(8,128)}, bf16[2,200,640]{2,1,0:T(8,128)(2,1)}) custom-call(s32[9]{0:T(128)} %fusion.21.refs_0_.meta, bf16[2,512,768]{2,1,0:T(8,128)(2,1)} %own.1, bf16[512,768]{1,0:T(8,128)(2,1)} %copy-done.16, bf16[1024,576]{1,0:T(8,128)(2,1)} %get-tuple-element.214.grads), custom_call_target="tpu_custom_call" | custom-call | flops 905969664 | bytes 8000000 | tf_op jit(solution)/shard_map/projection_weights/pallas_call | solution.py:1066
  217.3 10.0 %collective-permute-done.44 = bf16[256,768]{1,0:T(8,128)(2,1)} collective-permute-done((bf16[256,768]{1,0:T(8,128)(2,1)S(1)}, bf16[256,768]{1,0:T(8,128)(2,1)}, u32[]{:S(2)}, u32[]{:S(2)}) %collective-permute-start.44) | collective-permute-done | bytes 393248 | tf_op jit(solution)/shard_map/ppermute | solution.py:401
  227.4 2.4 collective-permute-done.45
  231.2 1.9 bitcast_add_fusion
  233.2 2.2 collective-permute-start.49
  240.8 12.1 %collective-permute-done.49 = bf16[2,104,1792]{2,1,0:T(8,128)(2,1)S(1)} collective-permute-done((bf16[2,104,1792]{2,1,0:T(8,128)(2,1)S(1)}, bf16[2,104,1792]{2,1,0:T(8,128)(2,1)S(1)}, u32[]{:S(2)}, u32[]{:S(2)}) %collective-permute-start.49) | collective-permute-done | bytes 745504 | tf_op jit(solution)/shard_map/ppermute | solution.py:401
  253.5 6.5 %collective-permute-start.54 = (bf16[104,1792]{1,0:T(8,128)(2,1)S(1)}, bf16[104,1792]{1,0:T(8,128)(2,1)S(1)}, u32[]{:S(2)}, u32[]{:S(2)}) collective-permute-start(bf16[104,1792]{1,0:T(8,128)(2,1)S(1)} %fusion.10), channel_id=1, source_target_pairs={{0,2},{1,3},{2,0},{3,1},{4,6},{5,7},{6,4},{7,5},{8,10},{9,11},{10,... | collective-permute-start | bytes 1118216 | tf_op jit(solution)/shard_map/ppermute | solution.py:401
  260.0 2.6 collective-permute-start.50
  266.6 5.1 %collective-permute-done.54 = bf16[104,1792]{1,0:T(8,128)(2,1)S(1)} collective-permute-done((bf16[104,1792]{1,0:T(8,128)(2,1)S(1)}, bf16[104,1792]{1,0:T(8,128)(2,1)S(1)}, u32[]{:S(2)}, u32[]{:S(2)}) %collective-permute-start.54) | collective-permute-done | bytes 372768 | tf_op jit(solution)/shard_map/ppermute | solution.py:401
  (246 shorter events, 74.7 us)
Async XLA Ops:
  8.3 16.2 %collective-permute-start.2 = (bf16[96,1024]{1,0:T(8,128)(2,1)S(1)}, bf16[96,1024]{1,0:T(8,128)(2,1)S(1)}, u32[]{:S(2)}, u32[]{:S(2)}) collective-permute-start(bf16[96,1024]{1,0:T(8,128)(2,1)S(1)} %pad.8.refs_0_), channel_id=1, source_target_pairs={{0,1},{1,0},{2,3},{3,2},{4,5},{5,4},{6,7},{7,6},{8,9},{9,8},{10,11... | collective-permute-start | bytes 589832 | tf_op jit(solution)/shard_map/ppermute | solution.py:401
  9.9 18.7 %collective-permute-start.1 = (bf16[512,768]{1,0:T(8,128)(2,1)S(1)}, bf16[512,768]{1,0:T(8,128)(2,1)S(1)}, u32[]{:S(2)}, u32[]{:S(2)}) collective-permute-start(bf16[512,768]{1,0:T(8,128)(2,1)S(1)} %dynamic-slice_bitcast_fusion), channel_id=1, source_target_pairs={{0,4},{4,0},{1,5},{5,1},{2,6},{6,2},{3,7},{7,3},{8,12},{12,8},{9,1... | collective-permute-start | bytes 2359304 | tf_op jit(solution)/shard_map/ppermute | solution.py:401
  28.7 21.6 %collective-permute-start.7 = (bf16[4,96,1024]{2,1,0:T(8,128)(2,1)}, bf16[4,96,1024]{2,1,0:T(8,128)(2,1)S(1)}, u32[]{:S(2)}, u32[]{:S(2)}) collective-permute-start(bf16[4,96,1024]{2,1,0:T(8,128)(2,1)} %stack_pieces.2.refs_8_.refs_7_), channel_id=1, source_target_pairs={{0,4},{4,0},{1,5},{5,1},{2,6},{6,2},{3,7},{7,3},{8,12},{12,8},{9,1... | collective-permute-start | bytes 2359304 | tf_op jit(solution)/shard_map/ppermute | solution.py:401
  30.1 20.1 %collective-permute-start.8 = (bf16[4,96,1024]{2,1,0:T(8,128)(2,1)}, bf16[4,96,1024]{2,1,0:T(8,128)(2,1)S(1)}, u32[]{:S(2)}, u32[]{:S(2)}) collective-permute-start(bf16[4,96,1024]{2,1,0:T(8,128)(2,1)} %stack_pieces.2.refs_8_.refs_7_), channel_id=1, source_target_pairs={{0,16},{8,24},{16,0},{24,8},{1,17},{9,25},{17,1},{25,9},{2,18},{10... | collective-permute-start | bytes 2359304 | tf_op jit(solution)/shard_map/ppermute | solution.py:401
  31.7 18.5 %collective-permute-start.10 = (bf16[104,768]{1,0:T(8,128)(2,1)S(1)}, bf16[104,768]{1,0:T(8,128)(2,1)}, u32[]{:S(2)}, u32[]{:S(2)}) collective-permute-start(bf16[104,768]{1,0:T(8,128)(2,1)S(1)} %maximum_maximum_fusion.refs_0_), channel_id=1, source_target_pairs={{0,2},{1,3},{2,0},{3,1},{4,6},{5,7},{6,4},{7,5},{8,10},{9,11},{10,... | collective-permute-start | bytes 479240 | tf_op jit(solution)/shard_map/ppermute | solution.py:401
  33.6 16.6 %collective-permute-start.11 = (bf16[104,768]{1,0:T(8,128)(2,1)S(1)}, bf16[104,768]{1,0:T(8,128)(2,1)}, u32[]{:S(2)}, u32[]{:S(2)}) collective-permute-start(bf16[104,768]{1,0:T(8,128)(2,1)S(1)} %maximum_maximum_fusion.refs_0_), channel_id=1, source_target_pairs={{0,3},{1,2},{2,1},{3,0},{4,7},{5,6},{6,5},{7,4},{8,11},{9,10},{10,... | collective-permute-start | bytes 479240 | tf_op jit(solution)/shard_map/ppermute | solution.py:401
  34.8 15.4 %collective-permute-start.9 = (bf16[104,768]{1,0:T(8,128)(2,1)S(1)}, bf16[104,768]{1,0:T(8,128)(2,1)}, u32[]{:S(2)}, u32[]{:S(2)}) collective-permute-start(bf16[104,768]{1,0:T(8,128)(2,1)S(1)} %maximum_maximum_fusion.refs_0_), channel_id=1, source_target_pairs={{0,1},{1,0},{2,3},{3,2},{4,5},{5,4},{6,7},{7,6},{8,9},{9,8},{10,11... | collective-permute-start | bytes 479240 | tf_op jit(solution)/shard_map/ppermute | solution.py:401
  50.3 18.9 %collective-permute-start.12 = (bf16[4,96,1024]{2,1,0:T(8,128)(2,1)S(1)}, bf16[4,96,1024]{2,1,0:T(8,128)(2,1)S(1)}, u32[]{:S(2)}, u32[]{:S(2)}) collective-permute-start(bf16[4,96,1024]{2,1,0:T(8,128)(2,1)S(1)} %collective-permute-done.7.refs_9_.refs_8_), channel_id=1, source_target_pairs={{0,16},{8,24},{16,0},{24,8},{1,17},{9,25},{17,1},{25,9},{2,18},{10... | collective-permute-start | bytes 2359304 | tf_op jit(solution)/shard_map/ppermute | solution.py:401
  70.2 16.7 %collective-permute-start.21 = (bf16[4,104,768]{2,1,0:T(8,128)(2,1)}, bf16[4,104,768]{2,1,0:T(8,128)(2,1)}, u32[]{:S(2)}, u32[]{:S(2)}) collective-permute-start(bf16[4,104,768]{2,1,0:T(8,128)(2,1)} %stack_pieces.3.refs_7_.refs_15_), channel_id=1, source_target_pairs={{0,4},{4,0},{1,5},{5,1},{2,6},{6,2},{3,7},{7,3},{8,12},{12,8},{9,1... | collective-permute-start | bytes 1916936 | tf_op jit(solution)/shard_map/ppermute | solution.py:401
  71.4 16.6 %collective-permute-start.22 = (bf16[4,104,768]{2,1,0:T(8,128)(2,1)}, bf16[4,104,768]{2,1,0:T(8,128)(2,1)S(1)}, u32[]{:S(2)}, u32[]{:S(2)}) collective-permute-start(bf16[4,104,768]{2,1,0:T(8,128)(2,1)} %stack_pieces.3.refs_7_.refs_15_), channel_id=1, source_target_pairs={{0,16},{8,24},{16,0},{24,8},{1,17},{9,25},{17,1},{25,9},{2,18},{10... | collective-permute-start | bytes 1916936 | tf_op jit(solution)/shard_map/ppermute | solution.py:401
  72.6 15.5 %collective-permute-start.23 = (bf16[4,104,768]{2,1,0:T(8,128)(2,1)}, bf16[4,104,768]{2,1,0:T(8,128)(2,1)}, u32[]{:S(2)}, u32[]{:S(2)}) collective-permute-start(bf16[4,104,768]{2,1,0:T(8,128)(2,1)} %stack_pieces.3.refs_7_.refs_15_), channel_id=1, source_target_pairs={{0,8},{8,0},{16,24},{24,16},{1,9},{9,1},{17,25},{25,17},{2,10},{10... | collective-permute-start | bytes 1916936 | tf_op jit(solution)/shard_map/ppermute | solution.py:401
  117.7 14.9 %collective-permute-start.31 = (bf16[6,264,768]{2,1,0:T(8,128)(2,1)}, bf16[6,264,768]{2,1,0:T(8,128)(2,1)S(1)}, u32[]{:S(2)}, u32[]{:S(2)}) collective-permute-start(bf16[6,264,768]{2,1,0:T(8,128)(2,1)} %get-tuple-element.175.refs_6_), channel_id=1, source_target_pairs={{0,8},{8,0},{16,24},{24,16},{1,9},{9,1},{17,25},{25,17},{2,10},{10... | collective-permute-start | bytes 7299080 | tf_op jit(solution)/shard_map/ppermute | solution.py:401
  117.9 25.9 %collective-permute-start.32 = (bf16[256,192]{1,0:T(8,128)(2,1)}, bf16[256,192]{1,0:T(8,128)(2,1)S(1)}, u32[]{:S(2)}, u32[]{:S(2)}) collective-permute-start(bf16[256,192]{1,0:T(8,128)(2,1)} %get-tuple-element.180), channel_id=1, source_target_pairs={{0,0},{1,1},{6,2},{7,3},{2,4},{3,5},{4,6},{5,7},{8,8},{9,9},{14,10... | collective-permute-start | bytes 294920 | tf_op jit(solution)/shard_map/ppermute | solution.py:417
  119.5 24.3 %collective-permute-start.33 = (bf16[256,192]{1,0:T(8,128)(2,1)}, bf16[256,192]{1,0:T(8,128)(2,1)S(1)}, u32[]{:S(2)}, u32[]{:S(2)}) collective-permute-start(bf16[256,192]{1,0:T(8,128)(2,1)} %get-tuple-element.181), channel_id=1, source_target_pairs={{1,0},{0,1},{7,2},{6,3},{3,4},{2,5},{5,6},{4,7},{9,8},{8,9},{15,10... | collective-permute-start | bytes 294920 | tf_op jit(solution)/shard_map/ppermute | solution.py:417
  123.3 20.5 %collective-permute-start.34 = (bf16[256,192]{1,0:T(8,128)(2,1)}, bf16[256,192]{1,0:T(8,128)(2,1)S(1)}, u32[]{:S(2)}, u32[]{:S(2)}) collective-permute-start(bf16[256,192]{1,0:T(8,128)(2,1)} %get-tuple-element.182), channel_id=1, source_target_pairs={{6,0},{7,1},{0,2},{1,3},{4,4},{5,5},{2,6},{3,7},{14,8},{15,9},{8,1... | collective-permute-start | bytes 294920 | tf_op jit(solution)/shard_map/ppermute | solution.py:417
  128.9 15.0 %collective-permute-start.35 = (bf16[256,192]{1,0:T(8,128)(2,1)}, bf16[256,192]{1,0:T(8,128)(2,1)S(1)}, u32[]{:S(2)}, u32[]{:S(2)}) collective-permute-start(bf16[256,192]{1,0:T(8,128)(2,1)} %get-tuple-element.183), channel_id=1, source_target_pairs={{7,0},{6,1},{1,2},{0,3},{5,4},{4,5},{3,6},{2,7},{15,8},{14,9},{9,1... | collective-permute-start | bytes 294920 | tf_op jit(solution)/shard_map/ppermute | solution.py:417
  132.6 33.3 %collective-permute-start.37 = (bf16[256,768]{1,0:T(8,128)(2,1)}, bf16[256,768]{1,0:T(8,128)(2,1)}, u32[]{:S(2)}, u32[]{:S(2)}) collective-permute-start(bf16[256,768]{1,0:T(8,128)(2,1)} %get-tuple-element.184), channel_id=1, source_target_pairs={{0,1},{1,0},{2,3},{3,2},{4,5},{5,4},{6,7},{7,6},{8,9},{9,8},{10,11... | collective-permute-start | bytes 1179656 | tf_op jit(solution)/shard_map/ppermute | solution.py:401
  143.9 22.1 %collective-permute-start.36 = (bf16[2,4,104,512]{3,2,1,0:T(8,128)(2,1)}, bf16[2,4,104,512]{3,2,1,0:T(8,128)(2,1)}, u32[]{:S(2)}, u32[]{:S(2)}) collective-permute-start(bf16[2,4,104,512]{3,2,1,0:T(8,128)(2,1)} %get-tuple-element.185), channel_id=1, source_target_pairs={{0,4},{4,0},{1,5},{5,1},{2,6},{6,2},{3,7},{7,3},{8,12},{12,8},{9,1... | collective-permute-start | bytes 2555912 | tf_op jit(solution)/shard_map/ppermute | solution.py:401
  143.9 22.0 %collective-permute-start.38 = (bf16[256,768]{1,0:T(8,128)(2,1)S(1)}, bf16[256,768]{1,0:T(8,128)(2,1)}, u32[]{:S(2)}, u32[]{:S(2)}) collective-permute-start(bf16[256,768]{1,0:T(8,128)(2,1)S(1)} %copy-done.20), channel_id=1, source_target_pairs={{0,2},{1,3},{2,0},{3,1},{4,6},{5,7},{6,4},{7,5},{8,10},{9,11},{10,... | collective-permute-start | bytes 1179656 | tf_op jit(solution)/shard_map/ppermute | solution.py:401
  147.4 47.2 %collective-permute-start.39 = (bf16[2,4,104,1280]{3,2,1,0:T(8,128)(2,1)}, bf16[2,4,104,1280]{3,2,1,0:T(8,128)(2,1)}, u32[]{:S(2)}, u32[]{:S(2)}) collective-permute-start(bf16[2,4,104,1280]{3,2,1,0:T(8,128)(2,1)} %get-tuple-element.200), channel_id=1, source_target_pairs={{0,16},{8,24},{16,0},{24,8},{1,17},{9,25},{17,1},{25,9},{2,18},{10... | collective-permute-start | bytes 6389768 | tf_op jit(solution)/shard_map/ppermute | solution.py:401
  166.0 31.2 %collective-permute-start.40 = (bf16[256,768]{1,0:T(8,128)(2,1)}, bf16[256,768]{1,0:T(8,128)(2,1)S(1)}, u32[]{:S(2)}, u32[]{:S(2)}) collective-permute-start(bf16[256,768]{1,0:T(8,128)(2,1)} %get-tuple-element.204), channel_id=1, source_target_pairs={{0,0},{1,1},{2,6},{3,7},{4,2},{5,3},{6,4},{7,5},{8,8},{9,9},{10,14... | collective-permute-start | bytes 1179656 | tf_op jit(solution)/shard_map/ppermute | solution.py:417
  167.6 29.6 %collective-permute-start.41 = (bf16[256,768]{1,0:T(8,128)(2,1)}, bf16[256,768]{1,0:T(8,128)(2,1)S(1)}, u32[]{:S(2)}, u32[]{:S(2)}) collective-permute-start(bf16[256,768]{1,0:T(8,128)(2,1)} %get-tuple-element.205), channel_id=1, source_target_pairs={{0,1},{1,0},{2,7},{3,6},{4,3},{5,2},{6,5},{7,4},{8,9},{9,8},{10,15... | collective-permute-start | bytes 1179656 | tf_op jit(solution)/shard_map/ppermute | solution.py:417
  168.2 31.8 %collective-permute-start.42 = (bf16[256,768]{1,0:T(8,128)(2,1)}, bf16[256,768]{1,0:T(8,128)(2,1)S(1)}, u32[]{:S(2)}, u32[]{:S(2)}) collective-permute-start(bf16[256,768]{1,0:T(8,128)(2,1)} %get-tuple-element.206), channel_id=1, source_target_pairs={{0,6},{1,7},{2,0},{3,1},{4,4},{5,5},{6,2},{7,3},{8,14},{9,15},{10,... | collective-permute-start | bytes 1179656 | tf_op jit(solution)/shard_map/ppermute | solution.py:417
  173.4 26.6 %collective-permute-start.43 = (bf16[256,768]{1,0:T(8,128)(2,1)}, bf16[256,768]{1,0:T(8,128)(2,1)S(1)}, u32[]{:S(2)}, u32[]{:S(2)}) collective-permute-start(bf16[256,768]{1,0:T(8,128)(2,1)} %get-tuple-element.207), channel_id=1, source_target_pairs={{0,7},{1,6},{2,1},{3,0},{4,5},{5,4},{6,3},{7,2},{8,15},{9,14},{10,... | collective-permute-start | bytes 1179656 | tf_op jit(solution)/shard_map/ppermute | solution.py:417
  200.1 29.7 %collective-permute-start.46 = (bf16[4,104,1280]{2,1,0:T(8,128)(2,1)}, bf16[4,104,1280]{2,1,0:T(8,128)(2,1)}, u32[]{:S(2)}, u32[]{:S(2)}) collective-permute-start(bf16[4,104,1280]{2,1,0:T(8,128)(2,1)} %fusion.3), channel_id=1, source_target_pairs={{0,4},{4,0},{1,5},{5,1},{2,6},{6,2},{3,7},{7,3},{8,12},{12,8},{9,1... | collective-permute-start | bytes 3194888 | tf_op jit(solution)/shard_map/ppermute | solution.py:401
  200.1 29.7 %collective-permute-start.47 = (bf16[4,104,512]{2,1,0:T(8,128)(2,1)S(1)}, bf16[4,104,512]{2,1,0:T(8,128)(2,1)}, u32[]{:S(2)}, u32[]{:S(2)}) collective-permute-start(bf16[4,104,512]{2,1,0:T(8,128)(2,1)S(1)} %fusion.9), channel_id=1, source_target_pairs={{0,16},{8,24},{16,0},{24,8},{1,17},{9,25},{17,1},{25,9},{2,18},{10... | collective-permute-start | bytes 1277960 | tf_op jit(solution)/shard_map/ppermute | solution.py:401
  201.7 25.7 %collective-permute-start.44 = (bf16[256,768]{1,0:T(8,128)(2,1)S(1)}, bf16[256,768]{1,0:T(8,128)(2,1)}, u32[]{:S(2)}, u32[]{:S(2)}) collective-permute-start(bf16[256,768]{1,0:T(8,128)(2,1)S(1)} %add_convert_fusion.2), channel_id=1, source_target_pairs={{0,2},{1,3},{2,0},{3,1},{4,6},{5,7},{6,4},{7,5},{8,10},{9,11},{10,... | collective-permute-start | bytes 1179656 | tf_op jit(solution)/shard_map/ppermute | solution.py:401
  212.2 17.5 %collective-permute-start.45 = (bf16[256,768]{1,0:T(8,128)(2,1)}, bf16[256,768]{1,0:T(8,128)(2,1)}, u32[]{:S(2)}, u32[]{:S(2)}) collective-permute-start(bf16[256,768]{1,0:T(8,128)(2,1)} %collective-permute-done.38), channel_id=1, source_target_pairs={{0,1},{1,0},{2,3},{3,2},{4,5},{5,4},{6,7},{7,6},{8,9},{9,8},{10,11... | collective-permute-start | bytes 1179656 | tf_op jit(solution)/shard_map/ppermute | solution.py:401
  233.2 19.7 %collective-permute-start.49 = (bf16[2,104,1792]{2,1,0:T(8,128)(2,1)S(1)}, bf16[2,104,1792]{2,1,0:T(8,128)(2,1)S(1)}, u32[]{:S(2)}, u32[]{:S(2)}) collective-permute-start(bf16[2,104,1792]{2,1,0:T(8,128)(2,1)S(1)} %fusion.1), channel_id=1, source_target_pairs={{0,1},{1,0},{2,3},{3,2},{4,5},{5,4},{6,7},{7,6},{8,9},{9,8},{10,11... | collective-permute-start | bytes 2236424 | tf_op jit(solution)/shard_map/ppermute | solution.py:401
  235.4 37.9 %collective-permute-start.48 = (bf16[256,768]{1,0:T(8,128)(2,1)S(1)}, bf16[256,768]{1,0:T(8,128)(2,1)S(1)}, u32[]{:S(2)}, u32[]{:S(2)}) collective-permute-start(bf16[256,768]{1,0:T(8,128)(2,1)S(1)} %add_convert_fusion.2), channel_id=1, source_target_pairs={{0,1},{1,0},{2,3},{3,2},{4,5},{5,4},{6,7},{7,6},{8,9},{9,8},{10,11... | collective-permute-start | bytes 1179656 | tf_op jit(solution)/shard_map/ppermute | solution.py:401
  253.5 18.2 %collective-permute-start.54 = (bf16[104,1792]{1,0:T(8,128)(2,1)S(1)}, bf16[104,1792]{1,0:T(8,128)(2,1)S(1)}, u32[]{:S(2)}, u32[]{:S(2)}) collective-permute-start(bf16[104,1792]{1,0:T(8,128)(2,1)S(1)} %fusion.10), channel_id=1, source_target_pairs={{0,2},{1,3},{2,0},{3,1},{4,6},{5,7},{6,4},{7,5},{8,10},{9,11},{10,... | collective-permute-start | bytes 1118216 | tf_op jit(solution)/shard_map/ppermute | solution.py:401
  260.0 14.9 %collective-permute-start.50 = (bf16[256,768]{1,0:T(8,128)(2,1)}, bf16[256,768]{1,0:T(8,128)(2,1)S(1)}, u32[]{:S(2)}, u32[]{:S(2)}) collective-permute-start(bf16[256,768]{1,0:T(8,128)(2,1)} %collective-permute-done.44), channel_id=1, source_target_pairs={{0,1},{1,0},{2,3},{3,2},{4,5},{5,4},{6,7},{7,6},{8,9},{9,8},{10,11... | collective-permute-start | bytes 1179656 | tf_op jit(solution)/shard_map/ppermute | solution.py:401
  (74 other events, 696.6 us)

commit v6 on v5

--- a/solution.py
+++ b/solution.py
@@ -1048,10 +1048,9 @@
         name="feed_weights",
     )(meta, keep, mixed_sib, both, both_sib, both, both_sib, mixed, mixed_sib)
 
-    near_out = swapped(output, "tp", 1)
     far_up, theirs_down, output, *grad_att = tied(far_up, theirs_down, output, *grad_att)
     got_up, got_down = swapped(far_up, "fsdp", 2), swapped(theirs_down, "ctx", 1)
-    far_out = swapped(output, "tp", 2)
+    far_out, near_out = swapped(output, "tp", 2), swapped(output, "tp", 1)
     grad_full, *grad_parts = attend_back_call(meta, qkv, grad_att, parts, stats, weight, heads)
 
     got_down, near_out, far_out, *grad_parts = tied(got_down, near_out, far_out, *grad_parts)

time: 282 us -> 282 us (level)
  starting transfers between devices: 88.6 us -> 84.7 us
  waiting for transfers between devices: 83.3 us -> 86.3 us
    ppermute x44, starting transfers between devices: 52.9 us -> 47.6 us  [swapped(): lax.ppermute(value, axis, [(place, place ^ bit) for place in range(count)])]
    unnamed x102 -> x106, local copies, waits for them, and re-layouts: 5.47 us -> 6.13 us
  transfers between devices with their start and end apart: 56 -> 56, of which waited for: 25 -> 26; matrix products, arithmetic and copies ran while one was open for 7% -> 7% of each run, Pallas kernels for 21% -> 21%
where the time goes in v6:
time: 282 us; the launch traced here: 281 us
  waiting for transfers between devices  86.3 us (31%)
  starting transfers between devices  84.7 us (30%)
  Pallas kernels  75.3 us (27%)
  other arithmetic  22 us (8%)
  local copies, waits for them, and re-layouts  11.4 us (4%)
    ppermute x44, waiting for transfers between devices, swapped(): lax.ppermute(value, axis, [(place, place ^ bit) for place in range(count)])  76.5 us
    ppermute x44, starting transfers between devices, swapped(): lax.ppermute(value, axis, [(place, place ^ bit) for place in range(count)])  47.6 us
    ppermute x12, starting transfers between devices, to_owner(): return lax.ppermute(value, ('ctx', 'tp'), pairs)  37.2 us
    pallas_call x1, Pallas kernels, attend_back_call(): pl.pallas_call(lambda *refs: attend_back_kernel(*refs, block=block, heads...  17.3 us
    pallas_call x1, Pallas kernels, per_device_rows(): pl.pallas_call(lambda *refs: second_kernel(*refs, width=width), grid_spec...  14.8 us
    pallas_call x1, Pallas kernels, attend_call(): pl.pallas_call(lambda *refs: attend_kernel(*refs, block=block, heads=head...  14.8 us
    pallas_call x1, Pallas kernels, per_device_rows(): pl.pallas_call(weights_kernel, grid_spec=pltpu.PrefetchScalarGridSpec(num...  9.81 us
    ppermute x12, waiting for transfers between devices, to_owner(): return lax.ppermute(value, ('ctx', 'tp'), pairs)  9.76 us
  transfers between devices with their start and end apart: 56, of which 26 were waited for; matrix products, arithmetic and copies ran while one was open for 7% of the time, Pallas kernels for 21%

profile of v6, /device:TPU:0, one launch (start us, length us, event | category | flops | bytes accessed | tf_op | source)
XLA Modules:
  0.0 281.1 jit_solution(13481208074612719063)
XLA Ops:
  4.2 4.1 %collective-permute-start = (bf16[96,1024]{1,0:T(8,128)(2,1)S(1)}, bf16[96,1024]{1,0:T(8,128)(2,1)S(1)}, u32[]{:S(2)}, u32[]{:S(2)}) collective-permute-start(bf16[96,1024]{1,0:T(8,128)(2,1)S(1)} %pad.8.refs_0_), channel_id=1, source_target_pairs={{0,2},{1,3},{2,0},{3,1},{4,6},{5,7},{6,4},{7,5},{8,10},{9,11},{10,... | collective-permute-start | bytes 589832 | tf_op jit(solution)/shard_map/ppermute | solution.py:401
  19.3 4.2 %collective-permute-done.3.refs_3_ = bf16[96,1024]{1,0:T(8,128)(2,1)S(1)} collective-permute-done((bf16[96,1024]{1,0:T(8,128)(2,1)S(1)}, bf16[96,1024]{1,0:T(8,128)(2,1)S(1)}, u32[]{:S(2)}, u32[]{:S(2)}) %collective-permute-start.3) | collective-permute-done | bytes 196640 | tf_op jit(solution)/shard_map/ppermute | solution.py:401
  25.3 2.2 stack_pieces.2.refs_8_.refs_7_
  31.7 1.9 collective-permute-start.10
  35.4 14.8 %attend.1 = (bf16[1024,576]{1,0:T(8,128)(2,1)}, bf16[256,192]{1,0:T(8,128)(2,1)}, bf16[256,192]{1,0:T(8,128)(2,1)}, bf16[256,192]{1,0:T(8,128)(2,1)}, bf16[256,1...) custom-call(s32[9]{0:T(128)} %fusion.21.refs_0_.meta, ...), custom_call_target="tpu_custom_call" | custom-call | flops 10569646080 | bytes 8000000 | tf_op jit(solution)/shard_map/attend/pallas_call | solution.py:545
  53.9 7.6 %collective-permute-start.15 = (bf16[256,192]{1,0:T(8,128)(2,1)}, bf16[256,192]{1,0:T(8,128)(2,1)}, u32[]{:S(2)}, u32[]{:S(2)}) collective-permute-start(bf16[256,192]{1,0:T(8,128)(2,1)} %get-tuple-element.149.refs_8_), channel_id=1, source_target_pairs={{0,6},{1,7},{2,0},{3,1},{4,4},{5,5},{6,2},{7,3},{8,14},{9,15},{10,... | collective-permute-start | bytes 294920 | tf_op jit(solution)/shard_map/ppermute | solution.py:417
  62.3 2.0 stack_pieces.3.refs_7_.refs_15_
  64.4 2.6 collective-permute-done.15.refs_3_
  75.8 9.2 %feed_first.1 = (f32[256,768]{1,0:T(8,128)}, f32[256,1]{1,0:T(8,128)}, bf16[4,256,1024]{2,1,0:T(8,128)(2,1)}, bf16[4,256,768]{2,1,0:T(8,128)(2,1)}) custom-call(s32[9]{0:T(128)} %fusion.21.refs_0_.meta, bf16[256,192]{1,0:T(8,128)(2,1)} %copy-done.35, bf16[256,192]{1,0:T(8,128)(2,1)} %copy-done.36, bf16[256,192]{1,0:T(8,128)(2,1)} %collective-permute-done.15.refs_3_, ...), custom_call_target="tpu_custom_call" | custom-call | flops 1509949440 | bytes 12000000 | tf_op jit(solution)/shard_map/feed_first/pallas_call | solution.py:969
  90.8 8.8 %collective-permute-done.24.refs_18_ = bf16[2,104,768]{2,1,0:T(8,128)(2,1)S(1)} collective-permute-done((bf16[2,104,768]{2,1,0:T(8,128)(2,1)S(1)}, bf16[2,104,768]{2,1,0:T(8,128)(2,1)S(1)}, u32[]{:S(2)}, u32[]{:S(2)}) %collective-permute-start.24) | collective-permute-done | bytes 319520 | tf_op jit(solution)/shard_map/ppermute | solution.py:401
  102.9 14.8 %feed_second.1 = (bf16[256,768]{1,0:T(8,128)(2,1)}, f32[256,768]{1,0:T(8,128)}, bf16[256,192]{1,0:T(8,128)(2,1)}, bf16[256,192]{1,0:T(8,128)(2,1)}, bf16[256,192...) custom-call(s32[9]{0:T(128)} %fusion.21.refs_0_.meta, ...), custom_call_target="tpu_custom_call" | custom-call | flops 3925868544 | bytes 20000000 | tf_op jit(solution)/shard_map/feed_second/pallas_call | solution.py:996
  119.5 3.8 %collective-permute-start.33 = (bf16[256,192]{1,0:T(8,128)(2,1)}, bf16[256,192]{1,0:T(8,128)(2,1)S(1)}, u32[]{:S(2)}, u32[]{:S(2)}) collective-permute-start(bf16[256,192]{1,0:T(8,128)(2,1)} %get-tuple-element.181), channel_id=1, source_target_pairs={{1,0},{0,1},{7,2},{6,3},{3,4},{2,5},{5,6},{4,7},{9,8},{8,9},{15,10... | collective-permute-start | bytes 294920 | tf_op jit(solution)/shard_map/ppermute | solution.py:417
  123.3 5.6 %collective-permute-start.34 = (bf16[256,192]{1,0:T(8,128)(2,1)}, bf16[256,192]{1,0:T(8,128)(2,1)S(1)}, u32[]{:S(2)}, u32[]{:S(2)}) collective-permute-start(bf16[256,192]{1,0:T(8,128)(2,1)} %get-tuple-element.182), channel_id=1, source_target_pairs={{6,0},{7,1},{0,2},{1,3},{4,4},{5,5},{2,6},{3,7},{14,8},{15,9},{8,1... | collective-permute-start | bytes 294920 | tf_op jit(solution)/shard_map/ppermute | solution.py:417
  128.9 3.7 %collective-permute-start.35 = (bf16[256,192]{1,0:T(8,128)(2,1)}, bf16[256,192]{1,0:T(8,128)(2,1)S(1)}, u32[]{:S(2)}, u32[]{:S(2)}) collective-permute-start(bf16[256,192]{1,0:T(8,128)(2,1)} %get-tuple-element.183), channel_id=1, source_target_pairs={{7,0},{6,1},{1,2},{0,3},{5,4},{4,5},{3,6},{2,7},{15,8},{14,9},{9,1... | collective-permute-start | bytes 294920 | tf_op jit(solution)/shard_map/ppermute | solution.py:417
  134.0 9.8 %feed_weights.1 = (bf16[2,4,104,1280]{3,2,1,0:T(8,128)(2,1)}, bf16[2,4,104,1280]{3,2,1,0:T(8,128)(2,1)}, bf16[2,4,104,512]{3,2,1,0:T(8,128)(2,1)}, bf16[2,4,104,512]{3,2,1,0:T(8,128)(2,1)}) custom-call(s32[9]{0:T(128)} %fusion.21.refs_0_.meta, bf16[3,2,264,192]{3,2,1,0:T(8,128)(2,1)} %get-tuple-element.174.refs_0_, bf16[6,264,768]{2,1,0:T(8,128)(2,1)} %copy-done.2, ...), custom_call_target="tpu_custom_call" | custom-call | flops 2717908992 | bytes 20000000 | tf_op jit(solution)/shard_map/feed_weights/pallas_call | solution.py:1031
  144.6 3.0 %collective-permute-start.36 = (bf16[2,4,104,512]{3,2,1,0:T(8,128)(2,1)}, bf16[2,4,104,512]{3,2,1,0:T(8,128)(2,1)}, u32[]{:S(2)}, u32[]{:S(2)}) collective-permute-start(bf16[2,4,104,512]{3,2,1,0:T(8,128)(2,1)} %get-tuple-element.185), channel_id=1, source_target_pairs={{0,4},{4,0},{1,5},{5,1},{2,6},{6,2},{3,7},{7,3},{8,12},{12,8},{9,1... | collective-permute-start | bytes 2555912 | tf_op jit(solution)/shard_map/ppermute | solution.py:401
  148.8 17.3 %attend_back.1 = (bf16[1024,576]{1,0:T(8,128)(2,1)}, bf16[256,768]{1,0:T(8,128)(2,1)}, bf16[256,768]{1,0:T(8,128)(2,1)}, bf16[256,768]{1,0:T(8,128)(2,1)}, bf16[256,768]{1,0:T(8,128)(2,1)}) custom-call(s32[9]{0:T(128)} %fusion.21.refs_0_.meta, bf16[1024,576]{1,0:T(8,128)(2,1)} %get-tuple-element.186.refs_1_, bf16[256,192]{1,0:T(8,128)(2,1)} %copy-done.48, ...), custom_call_target="tpu_custom_call" | custom-call | flops 24159191040 | bytes 8000000 | tf_op jit(solution)/shard_map/attend_back/pallas_call | solution.py:648
  167.7 1.9 collective-permute-start.41
  169.7 5.6 %collective-permute-start.42 = (bf16[256,768]{1,0:T(8,128)(2,1)}, bf16[256,768]{1,0:T(8,128)(2,1)S(1)}, u32[]{:S(2)}, u32[]{:S(2)}) collective-permute-start(bf16[256,768]{1,0:T(8,128)(2,1)} %get-tuple-element.206), channel_id=1, source_target_pairs={{0,6},{1,7},{2,0},{3,1},{4,4},{5,5},{6,2},{7,3},{8,14},{9,15},{10,... | collective-permute-start | bytes 1179656 | tf_op jit(solution)/shard_map/ppermute | solution.py:417
  178.4 16.4 %collective-permute-done.39 = bf16[2,4,104,1280]{3,2,1,0:T(8,128)(2,1)} collective-permute-done((bf16[2,4,104,1280]{3,2,1,0:T(8,128)(2,1)}, bf16[2,4,104,1280]{3,2,1,0:T(8,128)(2,1)}, u32[]{:S(2)}, u32[]{:S(2)}) %collective-permute-start.39) | collective-permute-done | bytes 2129952 | tf_op jit(solution)/shard_map/ppermute | solution.py:401
  194.8 2.5 fusion.3
  197.3 5.3 %collective-permute-done.42 = bf16[256,768]{1,0:T(8,128)(2,1)S(1)} collective-permute-done((bf16[256,768]{1,0:T(8,128)(2,1)}, bf16[256,768]{1,0:T(8,128)(2,1)S(1)}, u32[]{:S(2)}, u32[]{:S(2)}) %collective-permute-start.42) | collective-permute-done | bytes 393248 | tf_op jit(solution)/shard_map/ppermute | solution.py:417
  204.0 9.1 %collective-permute-start.44 = (bf16[256,768]{1,0:T(8,128)(2,1)S(1)}, bf16[256,768]{1,0:T(8,128)(2,1)}, u32[]{:S(2)}, u32[]{:S(2)}) collective-permute-start(bf16[256,768]{1,0:T(8,128)(2,1)S(1)} %add_convert_fusion.2), channel_id=1, source_target_pairs={{0,2},{1,3},{2,0},{3,1},{4,6},{5,7},{6,4},{7,5},{8,10},{9,11},{10,... | collective-permute-start | bytes 1179656 | tf_op jit(solution)/shard_map/ppermute | solution.py:401
  213.2 5.1 %projection_weights.1 = (f32[2,200,640]{2,1,0:T(8,128)}, bf16[2,200,640]{2,1,0:T(8,128)(2,1)}) custom-call(s32[9]{0:T(128)} %fusion.21.refs_0_.meta, bf16[2,512,768]{2,1,0:T(8,128)(2,1)} %own.1, bf16[512,768]{1,0:T(8,128)(2,1)} %copy-done.16, bf16[1024,576]{1,0:T(8,128)(2,1)} %get-tuple-element.214.grads), custom_call_target="tpu_custom_call" | custom-call | flops 905969664 | bytes 8000000 | tf_op jit(solution)/shard_map/projection_weights/pallas_call | solution.py:1065
  218.3 9.7 %collective-permute-done.44 = bf16[256,768]{1,0:T(8,128)(2,1)} collective-permute-done((bf16[256,768]{1,0:T(8,128)(2,1)S(1)}, bf16[256,768]{1,0:T(8,128)(2,1)}, u32[]{:S(2)}, u32[]{:S(2)}) %collective-permute-start.44) | collective-permute-done | bytes 393248 | tf_op jit(solution)/shard_map/ppermute | solution.py:401
  227.9 2.4 collective-permute-done.45
  231.8 1.9 bitcast_add_fusion
  233.8 2.0 collective-permute-start.49
  241.2 16.1 %collective-permute-done.49 = bf16[2,104,1792]{2,1,0:T(8,128)(2,1)S(1)} collective-permute-done((bf16[2,104,1792]{2,1,0:T(8,128)(2,1)S(1)}, bf16[2,104,1792]{2,1,0:T(8,128)(2,1)S(1)}, u32[]{:S(2)}, u32[]{:S(2)}) %collective-permute-start.49) | collective-permute-done | bytes 745504 | tf_op jit(solution)/shard_map/ppermute | solution.py:401
  257.9 2.0 collective-permute-start.54
  259.8 3.0 %collective-permute-start.50 = (bf16[256,768]{1,0:T(8,128)(2,1)}, bf16[256,768]{1,0:T(8,128)(2,1)S(1)}, u32[]{:S(2)}, u32[]{:S(2)}) collective-permute-start(bf16[256,768]{1,0:T(8,128)(2,1)} %collective-permute-done.44), channel_id=1, source_target_pairs={{0,1},{1,0},{2,3},{3,2},{4,5},{5,4},{6,7},{7,6},{8,9},{9,8},{10,11... | collective-permute-start | bytes 1179656 | tf_op jit(solution)/shard_map/ppermute | solution.py:401
  268.0 3.5 %collective-permute-done.54 = bf16[104,1792]{1,0:T(8,128)(2,1)S(1)} collective-permute-done((bf16[104,1792]{1,0:T(8,128)(2,1)S(1)}, bf16[104,1792]{1,0:T(8,128)(2,1)S(1)}, u32[]{:S(2)}, u32[]{:S(2)}) %collective-permute-start.54) | collective-permute-done | bytes 372768 | tf_op jit(solution)/shard_map/ppermute | solution.py:401
  (250 shorter events, 77.5 us)
Async XLA Ops:
  8.3 16.2 %collective-permute-start.2 = (bf16[96,1024]{1,0:T(8,128)(2,1)S(1)}, bf16[96,1024]{1,0:T(8,128)(2,1)S(1)}, u32[]{:S(2)}, u32[]{:S(2)}) collective-permute-start(bf16[96,1024]{1,0:T(8,128)(2,1)S(1)} %pad.8.refs_0_), channel_id=1, source_target_pairs={{0,1},{1,0},{2,3},{3,2},{4,5},{5,4},{6,7},{7,6},{8,9},{9,8},{10,11... | collective-permute-start | bytes 589832 | tf_op jit(solution)/shard_map/ppermute | solution.py:401
  9.9 18.7 %collective-permute-start.1 = (bf16[512,768]{1,0:T(8,128)(2,1)S(1)}, bf16[512,768]{1,0:T(8,128)(2,1)S(1)}, u32[]{:S(2)}, u32[]{:S(2)}) collective-permute-start(bf16[512,768]{1,0:T(8,128)(2,1)S(1)} %dynamic-slice_bitcast_fusion), channel_id=1, source_target_pairs={{0,4},{4,0},{1,5},{5,1},{2,6},{6,2},{3,7},{7,3},{8,12},{12,8},{9,1... | collective-permute-start | bytes 2359304 | tf_op jit(solution)/shard_map/ppermute | solution.py:401
  28.7 21.6 %collective-permute-start.7 = (bf16[4,96,1024]{2,1,0:T(8,128)(2,1)}, bf16[4,96,1024]{2,1,0:T(8,128)(2,1)S(1)}, u32[]{:S(2)}, u32[]{:S(2)}) collective-permute-start(bf16[4,96,1024]{2,1,0:T(8,128)(2,1)} %stack_pieces.2.refs_8_.refs_7_), channel_id=1, source_target_pairs={{0,4},{4,0},{1,5},{5,1},{2,6},{6,2},{3,7},{7,3},{8,12},{12,8},{9,1... | collective-permute-start | bytes 2359304 | tf_op jit(solution)/shard_map/ppermute | solution.py:401
  30.1 20.1 %collective-permute-start.8 = (bf16[4,96,1024]{2,1,0:T(8,128)(2,1)}, bf16[4,96,1024]{2,1,0:T(8,128)(2,1)S(1)}, u32[]{:S(2)}, u32[]{:S(2)}) collective-permute-start(bf16[4,96,1024]{2,1,0:T(8,128)(2,1)} %stack_pieces.2.refs_8_.refs_7_), channel_id=1, source_target_pairs={{0,16},{8,24},{16,0},{24,8},{1,17},{9,25},{17,1},{25,9},{2,18},{10... | collective-permute-start | bytes 2359304 | tf_op jit(solution)/shard_map/ppermute | solution.py:401
  31.7 18.5 %collective-permute-start.10 = (bf16[104,768]{1,0:T(8,128)(2,1)S(1)}, bf16[104,768]{1,0:T(8,128)(2,1)}, u32[]{:S(2)}, u32[]{:S(2)}) collective-permute-start(bf16[104,768]{1,0:T(8,128)(2,1)S(1)} %maximum_maximum_fusion.refs_0_), channel_id=1, source_target_pairs={{0,2},{1,3},{2,0},{3,1},{4,6},{5,7},{6,4},{7,5},{8,10},{9,11},{10,... | collective-permute-start | bytes 479240 | tf_op jit(solution)/shard_map/ppermute | solution.py:401
  33.6 16.6 %collective-permute-start.11 = (bf16[104,768]{1,0:T(8,128)(2,1)S(1)}, bf16[104,768]{1,0:T(8,128)(2,1)}, u32[]{:S(2)}, u32[]{:S(2)}) collective-permute-start(bf16[104,768]{1,0:T(8,128)(2,1)S(1)} %maximum_maximum_fusion.refs_0_), channel_id=1, source_target_pairs={{0,3},{1,2},{2,1},{3,0},{4,7},{5,6},{6,5},{7,4},{8,11},{9,10},{10,... | collective-permute-start | bytes 479240 | tf_op jit(solution)/shard_map/ppermute | solution.py:401
  34.8 15.4 %collective-permute-start.9 = (bf16[104,768]{1,0:T(8,128)(2,1)S(1)}, bf16[104,768]{1,0:T(8,128)(2,1)}, u32[]{:S(2)}, u32[]{:S(2)}) collective-permute-start(bf16[104,768]{1,0:T(8,128)(2,1)S(1)} %maximum_maximum_fusion.refs_0_), channel_id=1, source_target_pairs={{0,1},{1,0},{2,3},{3,2},{4,5},{5,4},{6,7},{7,6},{8,9},{9,8},{10,11... | collective-permute-start | bytes 479240 | tf_op jit(solution)/shard_map/ppermute | solution.py:401
  50.3 18.9 %collective-permute-start.12 = (bf16[4,96,1024]{2,1,0:T(8,128)(2,1)S(1)}, bf16[4,96,1024]{2,1,0:T(8,128)(2,1)S(1)}, u32[]{:S(2)}, u32[]{:S(2)}) collective-permute-start(bf16[4,96,1024]{2,1,0:T(8,128)(2,1)S(1)} %collective-permute-done.7.refs_9_.refs_8_), channel_id=1, source_target_pairs={{0,16},{8,24},{16,0},{24,8},{1,17},{9,25},{17,1},{25,9},{2,18},{10... | collective-permute-start | bytes 2359304 | tf_op jit(solution)/shard_map/ppermute | solution.py:401
  70.2 16.7 %collective-permute-start.21 = (bf16[4,104,768]{2,1,0:T(8,128)(2,1)}, bf16[4,104,768]{2,1,0:T(8,128)(2,1)}, u32[]{:S(2)}, u32[]{:S(2)}) collective-permute-start(bf16[4,104,768]{2,1,0:T(8,128)(2,1)} %stack_pieces.3.refs_7_.refs_15_), channel_id=1, source_target_pairs={{0,4},{4,0},{1,5},{5,1},{2,6},{6,2},{3,7},{7,3},{8,12},{12,8},{9,1... | collective-permute-start | bytes 1916936 | tf_op jit(solution)/shard_map/ppermute | solution.py:401
  71.5 16.6 %collective-permute-start.22 = (bf16[4,104,768]{2,1,0:T(8,128)(2,1)}, bf16[4,104,768]{2,1,0:T(8,128)(2,1)S(1)}, u32[]{:S(2)}, u32[]{:S(2)}) collective-permute-start(bf16[4,104,768]{2,1,0:T(8,128)(2,1)} %stack_pieces.3.refs_7_.refs_15_), channel_id=1, source_target_pairs={{0,16},{8,24},{16,0},{24,8},{1,17},{9,25},{17,1},{25,9},{2,18},{10... | collective-permute-start | bytes 1916936 | tf_op jit(solution)/shard_map/ppermute | solution.py:401
  72.6 15.5 %collective-permute-start.23 = (bf16[4,104,768]{2,1,0:T(8,128)(2,1)}, bf16[4,104,768]{2,1,0:T(8,128)(2,1)}, u32[]{:S(2)}, u32[]{:S(2)}) collective-permute-start(bf16[4,104,768]{2,1,0:T(8,128)(2,1)} %stack_pieces.3.refs_7_.refs_15_), channel_id=1, source_target_pairs={{0,8},{8,0},{16,24},{24,16},{1,9},{9,1},{17,25},{25,17},{2,10},{10... | collective-permute-start | bytes 1916936 | tf_op jit(solution)/shard_map/ppermute | solution.py:401
  117.7 14.9 %collective-permute-start.31 = (bf16[6,264,768]{2,1,0:T(8,128)(2,1)}, bf16[6,264,768]{2,1,0:T(8,128)(2,1)S(1)}, u32[]{:S(2)}, u32[]{:S(2)}) collective-permute-start(bf16[6,264,768]{2,1,0:T(8,128)(2,1)} %get-tuple-element.175.refs_6_), channel_id=1, source_target_pairs={{0,8},{8,0},{16,24},{24,16},{1,9},{9,1},{17,25},{25,17},{2,10},{10... | collective-permute-start | bytes 7299080 | tf_op jit(solution)/shard_map/ppermute | solution.py:401
  117.9 25.9 %collective-permute-start.32 = (bf16[256,192]{1,0:T(8,128)(2,1)}, bf16[256,192]{1,0:T(8,128)(2,1)S(1)}, u32[]{:S(2)}, u32[]{:S(2)}) collective-permute-start(bf16[256,192]{1,0:T(8,128)(2,1)} %get-tuple-element.180), channel_id=1, source_target_pairs={{0,0},{1,1},{6,2},{7,3},{2,4},{3,5},{4,6},{5,7},{8,8},{9,9},{14,10... | collective-permute-start | bytes 294920 | tf_op jit(solution)/shard_map/ppermute | solution.py:417
  119.5 24.4 %collective-permute-start.33 = (bf16[256,192]{1,0:T(8,128)(2,1)}, bf16[256,192]{1,0:T(8,128)(2,1)S(1)}, u32[]{:S(2)}, u32[]{:S(2)}) collective-permute-start(bf16[256,192]{1,0:T(8,128)(2,1)} %get-tuple-element.181), channel_id=1, source_target_pairs={{1,0},{0,1},{7,2},{6,3},{3,4},{2,5},{5,6},{4,7},{9,8},{8,9},{15,10... | collective-permute-start | bytes 294920 | tf_op jit(solution)/shard_map/ppermute | solution.py:417
  123.3 20.6 %collective-permute-start.34 = (bf16[256,192]{1,0:T(8,128)(2,1)}, bf16[256,192]{1,0:T(8,128)(2,1)S(1)}, u32[]{:S(2)}, u32[]{:S(2)}) collective-permute-start(bf16[256,192]{1,0:T(8,128)(2,1)} %get-tuple-element.182), channel_id=1, source_target_pairs={{6,0},{7,1},{0,2},{1,3},{4,4},{5,5},{2,6},{3,7},{14,8},{15,9},{8,1... | collective-permute-start | bytes 294920 | tf_op jit(solution)/shard_map/ppermute | solution.py:417
  128.9 15.0 %collective-permute-start.35 = (bf16[256,192]{1,0:T(8,128)(2,1)}, bf16[256,192]{1,0:T(8,128)(2,1)S(1)}, u32[]{:S(2)}, u32[]{:S(2)}) collective-permute-start(bf16[256,192]{1,0:T(8,128)(2,1)} %get-tuple-element.183), channel_id=1, source_target_pairs={{7,0},{6,1},{1,2},{0,3},{5,4},{4,5},{3,6},{2,7},{15,8},{14,9},{9,1... | collective-permute-start | bytes 294920 | tf_op jit(solution)/shard_map/ppermute | solution.py:417
  143.9 22.1 %collective-permute-start.37 = (bf16[256,768]{1,0:T(8,128)(2,1)S(1)}, bf16[256,768]{1,0:T(8,128)(2,1)S(1)}, u32[]{:S(2)}, u32[]{:S(2)}) collective-permute-start(bf16[256,768]{1,0:T(8,128)(2,1)S(1)} %copy-done.20), channel_id=1, source_target_pairs={{0,1},{1,0},{2,3},{3,2},{4,5},{5,4},{6,7},{7,6},{8,9},{9,8},{10,11... | collective-permute-start | bytes 1179656 | tf_op jit(solution)/shard_map/ppermute | solution.py:401
  144.5 21.6 %collective-permute-start.38 = (bf16[256,768]{1,0:T(8,128)(2,1)S(1)}, bf16[256,768]{1,0:T(8,128)(2,1)}, u32[]{:S(2)}, u32[]{:S(2)}) collective-permute-start(bf16[256,768]{1,0:T(8,128)(2,1)S(1)} %copy-done.20), channel_id=1, source_target_pairs={{0,2},{1,3},{2,0},{3,1},{4,6},{5,7},{6,4},{7,5},{8,10},{9,11},{10,... | collective-permute-start | bytes 1179656 | tf_op jit(solution)/shard_map/ppermute | solution.py:401
  144.6 21.5 %collective-permute-start.36 = (bf16[2,4,104,512]{3,2,1,0:T(8,128)(2,1)}, bf16[2,4,104,512]{3,2,1,0:T(8,128)(2,1)}, u32[]{:S(2)}, u32[]{:S(2)}) collective-permute-start(bf16[2,4,104,512]{3,2,1,0:T(8,128)(2,1)} %get-tuple-element.185), channel_id=1, source_target_pairs={{0,4},{4,0},{1,5},{5,1},{2,6},{6,2},{3,7},{7,3},{8,12},{12,8},{9,1... | collective-permute-start | bytes 2555912 | tf_op jit(solution)/shard_map/ppermute | solution.py:401
  147.5 47.2 %collective-permute-start.39 = (bf16[2,4,104,1280]{3,2,1,0:T(8,128)(2,1)}, bf16[2,4,104,1280]{3,2,1,0:T(8,128)(2,1)}, u32[]{:S(2)}, u32[]{:S(2)}) collective-permute-start(bf16[2,4,104,1280]{3,2,1,0:T(8,128)(2,1)} %get-tuple-element.200), channel_id=1, source_target_pairs={{0,16},{8,24},{16,0},{24,8},{1,17},{9,25},{17,1},{25,9},{2,18},{10... | collective-permute-start | bytes 6389768 | tf_op jit(solution)/shard_map/ppermute | solution.py:401
  166.1 31.2 %collective-permute-start.40 = (bf16[256,768]{1,0:T(8,128)(2,1)}, bf16[256,768]{1,0:T(8,128)(2,1)S(1)}, u32[]{:S(2)}, u32[]{:S(2)}) collective-permute-start(bf16[256,768]{1,0:T(8,128)(2,1)} %get-tuple-element.204), channel_id=1, source_target_pairs={{0,0},{1,1},{2,6},{3,7},{4,2},{5,3},{6,4},{7,5},{8,8},{9,9},{10,14... | collective-permute-start | bytes 1179656 | tf_op jit(solution)/shard_map/ppermute | solution.py:417
  167.7 29.6 %collective-permute-start.41 = (bf16[256,768]{1,0:T(8,128)(2,1)}, bf16[256,768]{1,0:T(8,128)(2,1)S(1)}, u32[]{:S(2)}, u32[]{:S(2)}) collective-permute-start(bf16[256,768]{1,0:T(8,128)(2,1)} %get-tuple-element.205), channel_id=1, source_target_pairs={{0,1},{1,0},{2,7},{3,6},{4,3},{5,2},{6,5},{7,4},{8,9},{9,8},{10,15... | collective-permute-start | bytes 1179656 | tf_op jit(solution)/shard_map/ppermute | solution.py:417
  169.7 32.9 %collective-permute-start.42 = (bf16[256,768]{1,0:T(8,128)(2,1)}, bf16[256,768]{1,0:T(8,128)(2,1)S(1)}, u32[]{:S(2)}, u32[]{:S(2)}) collective-permute-start(bf16[256,768]{1,0:T(8,128)(2,1)} %get-tuple-element.206), channel_id=1, source_target_pairs={{0,6},{1,7},{2,0},{3,1},{4,4},{5,5},{6,2},{7,3},{8,14},{9,15},{10,... | collective-permute-start | bytes 1179656 | tf_op jit(solution)/shard_map/ppermute | solution.py:417
  175.3 27.3 %collective-permute-start.43 = (bf16[256,768]{1,0:T(8,128)(2,1)}, bf16[256,768]{1,0:T(8,128)(2,1)S(1)}, u32[]{:S(2)}, u32[]{:S(2)}) collective-permute-start(bf16[256,768]{1,0:T(8,128)(2,1)} %get-tuple-element.207), channel_id=1, source_target_pairs={{0,7},{1,6},{2,1},{3,0},{4,5},{5,4},{6,3},{7,2},{8,15},{9,14},{10,... | collective-permute-start | bytes 1179656 | tf_op jit(solution)/shard_map/ppermute | solution.py:417
  202.6 27.8 %collective-permute-start.46 = (bf16[4,104,1280]{2,1,0:T(8,128)(2,1)}, bf16[4,104,1280]{2,1,0:T(8,128)(2,1)}, u32[]{:S(2)}, u32[]{:S(2)}) collective-permute-start(bf16[4,104,1280]{2,1,0:T(8,128)(2,1)} %fusion.3), channel_id=1, source_target_pairs={{0,4},{4,0},{1,5},{5,1},{2,6},{6,2},{3,7},{7,3},{8,12},{12,8},{9,1... | collective-permute-start | bytes 3194888 | tf_op jit(solution)/shard_map/ppermute | solution.py:401
  202.6 27.8 %collective-permute-start.47 = (bf16[4,104,512]{2,1,0:T(8,128)(2,1)S(1)}, bf16[4,104,512]{2,1,0:T(8,128)(2,1)}, u32[]{:S(2)}, u32[]{:S(2)}) collective-permute-start(bf16[4,104,512]{2,1,0:T(8,128)(2,1)S(1)} %fusion.9), channel_id=1, source_target_pairs={{0,16},{8,24},{16,0},{24,8},{1,17},{9,25},{17,1},{25,9},{2,18},{10... | collective-permute-start | bytes 1277960 | tf_op jit(solution)/shard_map/ppermute | solution.py:401
  204.0 23.9 %collective-permute-start.44 = (bf16[256,768]{1,0:T(8,128)(2,1)S(1)}, bf16[256,768]{1,0:T(8,128)(2,1)}, u32[]{:S(2)}, u32[]{:S(2)}) collective-permute-start(bf16[256,768]{1,0:T(8,128)(2,1)S(1)} %add_convert_fusion.2), channel_id=1, source_target_pairs={{0,2},{1,3},{2,0},{3,1},{4,6},{5,7},{6,4},{7,5},{8,10},{9,11},{10,... | collective-permute-start | bytes 1179656 | tf_op jit(solution)/shard_map/ppermute | solution.py:401
  213.2 17.1 %collective-permute-start.45 = (bf16[256,768]{1,0:T(8,128)(2,1)}, bf16[256,768]{1,0:T(8,128)(2,1)}, u32[]{:S(2)}, u32[]{:S(2)}) collective-permute-start(bf16[256,768]{1,0:T(8,128)(2,1)} %collective-permute-done.38), channel_id=1, source_target_pairs={{0,1},{1,0},{2,3},{3,2},{4,5},{5,4},{6,7},{7,6},{8,9},{9,8},{10,11... | collective-permute-start | bytes 1179656 | tf_op jit(solution)/shard_map/ppermute | solution.py:401
  233.8 23.6 %collective-permute-start.49 = (bf16[2,104,1792]{2,1,0:T(8,128)(2,1)S(1)}, bf16[2,104,1792]{2,1,0:T(8,128)(2,1)S(1)}, u32[]{:S(2)}, u32[]{:S(2)}) collective-permute-start(bf16[2,104,1792]{2,1,0:T(8,128)(2,1)S(1)} %fusion.1), channel_id=1, source_target_pairs={{0,1},{1,0},{2,3},{3,2},{4,5},{5,4},{6,7},{7,6},{8,9},{9,8},{10,11... | collective-permute-start | bytes 2236424 | tf_op jit(solution)/shard_map/ppermute | solution.py:401
  235.7 38.4 %collective-permute-start.48 = (bf16[256,768]{1,0:T(8,128)(2,1)S(1)}, bf16[256,768]{1,0:T(8,128)(2,1)S(1)}, u32[]{:S(2)}, u32[]{:S(2)}) collective-permute-start(bf16[256,768]{1,0:T(8,128)(2,1)S(1)} %add_convert_fusion.2), channel_id=1, source_target_pairs={{0,1},{1,0},{2,3},{3,2},{4,5},{5,4},{6,7},{7,6},{8,9},{9,8},{10,11... | collective-permute-start | bytes 1179656 | tf_op jit(solution)/shard_map/ppermute | solution.py:401
  239.7 17.8 %collective-permute-start.52 = (bf16[200,640]{1,0:T(8,128)(2,1)S(1)}, bf16[200,640]{1,0:T(8,128)(2,1)S(1)}, u32[]{:S(2)}, u32[]{:S(2)}) collective-permute-start(bf16[200,640]{1,0:T(8,128)(2,1)S(1)} %fusion.12), channel_id=1, source_target_pairs={{0,16},{8,24},{16,0},{24,8},{1,17},{9,25},{17,1},{25,9},{2,18},{10... | collective-permute-start | bytes 768008 | tf_op jit(solution)/shard_map/ppermute | solution.py:401
  259.8 15.0 %collective-permute-start.50 = (bf16[256,768]{1,0:T(8,128)(2,1)}, bf16[256,768]{1,0:T(8,128)(2,1)S(1)}, u32[]{:S(2)}, u32[]{:S(2)}) collective-permute-start(bf16[256,768]{1,0:T(8,128)(2,1)} %collective-permute-done.44), channel_id=1, source_target_pairs={{0,1},{1,0},{2,3},{3,2},{4,5},{5,4},{6,7},{7,6},{8,9},{9,8},{10,11... | collective-permute-start | bytes 1179656 | tf_op jit(solution)/shard_map/ppermute | solution.py:401
  (76 other events, 729.5 us)
